TPU v7x, 256 devices: a whole 4x4x8 slice. The times are simulated.
256 devices in a mesh: grp: 8 (over x, core), seq: 32 (over z, y).
Axes of the slice: x: 4, y: 4, z: 8, core: 2. Of those that a mesh axis runs over, the one named last changes fastest.
Arguments:
- queries: bfloat16 [8, 3, 32, 128, 512], P('grp', None, 'seq'), may hold values from -120 to 120
- key_input: bfloat16 [8, 3, 32, 128, 512], P('grp', None, 'seq'), may hold values from -8 to 8
- value_input: bfloat16 [8, 3, 32, 128, 512], P('grp', None, 'seq'), may hold values from -6 to 6
- grad_output: bfloat16 [8, 3, 32, 128, 512], P('grp', None, 'seq'), may hold values from -6 to 6
- block_lists: int32 [768, 16], replicated, may hold values from -1 to 767, as said below
- block_flags: int32 [768, 16], replicated, may hold values from 0 to 1, as said below
Outputs:
- attended: bfloat16 [8, 3, 32, 128, 512], P('grp', None, 'seq')
- grad_queries: bfloat16 [8, 3, 32, 128, 512], P('grp', None, 'seq')
- grad_keys: bfloat16 [8, 3, 32, 128, 512], P('grp', None, 'seq')
- grad_values: bfloat16 [8, 3, 32, 128, 512], P('grp', None, 'seq')
Inputs may be any that keep to these rules, and one draw needn't show every extreme that they name: `block_lists`: entry 0 of row t is t itself; the other used entries of a row are distinct tiles u < t, each either in the same block of 96 tiles as t, or in an earlier block with u % 32 == t % 32; used entries come first and -1 fills the rest. The 3 rows t = (a * 3 + b) * 32 + c that share a and c name together at most one tile of the form (a2 * 3 + b2) * 32 + c2 for each pair (a2, c2) other than (a, c). block_flags[t, 0] is 1 for every t; a flag whose list entry is -1 has no effect.
All inputs are finite; a program needn't handle non-finite values.
Results may differ from a plain program's by a relative error of at most 0.029.
Values may be sent and summed in bfloat16 or wider, within the bound.
No kernel may reach another device: no remote copies, remote signals or barrier semaphores. Data moves between devices by JAX's collectives and lax.ppermute only.
A program may use at most 256 MiB of HBM per device.

v0:
```python
import jax
import jax.numpy as jnp
from jax import lax
from jax.sharding import PartitionSpec as P

HEADS = 8
HEAD_DIM = 64


floor_score = -1e30


def locate(entry_ids, group_tiles, columns):
    safe_ids = jnp.maximum(entry_ids, 0)
    within = safe_ids % group_tiles
    return (safe_ids // group_tiles, within // columns, within % columns)


def per_device(queries, key_input, value_input, grad_output, block_lists, block_flags):
    tile_dev = queries.shape[1]
    tile_rows = queries.shape[3]
    width = queries.shape[4]
    entries = block_lists.shape[1]
    columns = lax.axis_size("seq")
    groups = lax.axis_size("grp")
    group_at = lax.axis_index("grp")
    column_at = lax.axis_index("seq")
    group_tiles = tile_dev * columns
    query_tiles = queries.reshape(tile_dev, tile_rows, width)
    key_tiles = key_input.reshape(tile_dev, tile_rows, width)
    value_tiles = value_input.reshape(tile_dev, tile_rows, width)
    grad_tiles = grad_output.reshape(tile_dev, tile_rows, width)
    ranks = jnp.arange(tile_dev, dtype=jnp.int32)
    column_ids = jnp.arange(columns, dtype=jnp.int32)
    group_ids = jnp.arange(groups, dtype=jnp.int32)
    my_tiles = (group_at * tile_dev + ranks) * columns + column_at
    my_lists = jnp.take(block_lists, my_tiles, axis=0)
    my_flags = jnp.take(block_flags, my_tiles, axis=0)
    present = my_lists >= 0
    owner_group, owner_rank, owner_column = locate(my_lists, group_tiles, columns)
    same_group = owner_group == group_at
    is_own = present & same_group & (owner_column == column_at)
    is_near = present & same_group & (owner_column != column_at)
    is_far = present & jnp.logical_not(same_group)
    group_rows = lax.dynamic_slice_in_dim(block_lists, group_at * group_tiles, group_tiles, 0)
    group_rows = group_rows.reshape(tile_dev, columns, entries)
    row_group, row_rank, row_column = locate(group_rows, group_tiles, columns)
    named_here = (group_rows >= 0) & (row_group == group_at) & (row_column == column_at)
    near_rank = jnp.max(jnp.where(named_here, row_rank, -1), axis=(0, 2))
    near_rank = jnp.where(column_ids == column_at, -1, near_rank)
    column_rows = jnp.take(
        block_lists.reshape(groups, tile_dev, columns, entries), column_at, axis=2
    )
    far_group, far_rank_all, far_column = locate(column_rows, group_tiles, columns)
    named_far = (column_rows >= 0) & (far_group == group_at) & (far_column == column_at)
    far_rank = jnp.max(jnp.where(named_far, far_rank_all, -1), axis=(1, 2))
    far_rank = jnp.where(group_ids == group_at, -1, far_rank)
    wanted = jnp.max(
        jnp.where(
            is_near[:, :, None] & (owner_column[:, :, None] == column_ids),
            owner_rank[:, :, None],
            -1,
        ),
        axis=(0, 1),
    )
    pieces = (
        lax.all_gather(key_tiles, "seq", axis=0, tiled=True),
        lax.all_gather(value_tiles, "seq", axis=0, tiled=True),
    )
    span_rows = pieces[0].shape[0]
    row_at = jnp.arange(span_rows, dtype=jnp.int32)
    select = (
        (row_at[None, :] // tile_dev == column_ids[:, None])
        & (row_at[None, :] % tile_dev == wanted[:, None])
    ).astype(jnp.bfloat16)
    new_keys = jnp.einsum("pn,ntw->ptw", select, pieces[0], preferred_element_type=jnp.float32)
    new_values = jnp.einsum("pn,ntw->ptw", select, pieces[1], preferred_element_type=jnp.float32)
    near_keys = new_keys.astype(jnp.bfloat16)
    near_values = new_values.astype(jnp.bfloat16)
    far_out = jnp.maximum(far_rank, 0)
    far_keys, far_values = (
        lax.all_to_all(
            jnp.take(key_tiles, far_out, axis=0), "grp", split_axis=0, concat_axis=0, tiled=True
        ),
        lax.all_to_all(
            jnp.take(value_tiles, far_out, axis=0), "grp", split_axis=0, concat_axis=0, tiled=True
        ),
    )
    own_slot = jnp.where(is_own, owner_rank, 0)
    near_slot = jnp.where(is_near, owner_column, 0)
    far_slot = jnp.where(is_far, owner_group, 0)
    own_pick = is_own[:, :, None, None]
    near_pick = is_near[:, :, None, None]
    far_pick = is_far[:, :, None, None]
    pair_width = 2 * HEAD_DIM
    score_scale = HEAD_DIM ** (-0.5)
    positions = jnp.arange(tile_rows)
    lower_mask = positions[None, :] <= positions[:, None]
    allowed = present[:, None, :, None] & (
        (my_flags == 0)[:, None, :, None] | lower_mask[None, :, None, :]
    )

    def spread(term, chosen_pick, slot, slots):
        total = jnp.zeros((slots, tile_rows, pair_width), jnp.float32)
        return total.at[slot].add(jnp.where(chosen_pick, term, 0.0)).astype(jnp.bfloat16)

    attended_parts = []
    query_parts = []
    own_key_parts = []
    near_key_parts = []
    far_key_parts = []
    own_value_parts = []
    near_value_parts = []
    far_value_parts = []
    for head_pair in range(HEADS // 2):
        start_col = head_pair * pair_width

        def columns_of(source):
            return source[..., start_col : start_col + pair_width]

        def fetch(own_source, near_source, far_source):
            from_own = jnp.take(columns_of(own_source), own_slot, axis=0)
            from_near = jnp.take(columns_of(near_source), near_slot, axis=0)
            from_far = jnp.take(columns_of(far_source), far_slot, axis=0)
            return jnp.where(own_pick, from_own, jnp.where(near_pick, from_near, from_far))

        key_block = fetch(key_tiles, near_keys, far_keys).reshape(
            tile_dev, entries, tile_rows, 2, HEAD_DIM
        )
        value_block = fetch(value_tiles, near_values, far_values).reshape(
            tile_dev, entries, tile_rows, 2, HEAD_DIM
        )
        query_block = columns_of(query_tiles).reshape(tile_dev, tile_rows, 2, HEAD_DIM)
        grad_block = columns_of(grad_tiles).reshape(tile_dev, tile_rows, 2, HEAD_DIM)
        scores = (
            jnp.einsum(
                "tihd,techd->thiec", query_block, key_block, preferred_element_type=jnp.float32
            )
            * score_scale
        )
        masked = jnp.where(allowed[:, None], scores, floor_score)
        row_top = jnp.max(masked, axis=(3, 4), keepdims=True)
        exponent = jnp.exp(masked - row_top)
        probs_exact = exponent / jnp.sum(exponent, axis=(3, 4), keepdims=True)
        probs = probs_exact.astype(jnp.bfloat16)
        attended_block = jnp.einsum(
            "thiec,techd->tihd", probs, value_block, preferred_element_type=jnp.float32
        ).astype(jnp.bfloat16)
        row_delta = jnp.sum(
            grad_block.astype(jnp.float32) * attended_block.astype(jnp.float32), axis=3
        )
        dprobs = jnp.einsum(
            "tihd,techd->thiec", grad_block, value_block, preferred_element_type=jnp.float32
        )
        dscores = (
            probs_exact * (dprobs - jnp.transpose(row_delta, (0, 2, 1))[..., None, None])
        ).astype(jnp.bfloat16)
        grad_query = (
            jnp.einsum("thiec,techd->tihd", dscores, key_block, preferred_element_type=jnp.float32)
            * score_scale
        )
        grad_key = (
            jnp.einsum(
                "thiec,tihd->techd", dscores, query_block, preferred_element_type=jnp.float32
            )
            * score_scale
        )
        grad_value = jnp.einsum(
            "thiec,tihd->techd", probs, grad_block, preferred_element_type=jnp.float32
        )
        grad_key = grad_key.reshape(tile_dev, entries, tile_rows, pair_width)
        grad_value = grad_value.reshape(tile_dev, entries, tile_rows, pair_width)
        attended_parts.append(attended_block.reshape(tile_dev, tile_rows, pair_width))
        query_parts.append(grad_query.astype(jnp.bfloat16).reshape(tile_dev, tile_rows, pair_width))
        own_key_parts.append(spread(grad_key, own_pick, own_slot, tile_dev))
        near_key_parts.append(spread(grad_key, near_pick, near_slot, columns))
        far_key_parts.append(spread(grad_key, far_pick, far_slot, groups))
        own_value_parts.append(spread(grad_value, own_pick, own_slot, tile_dev))
        near_value_parts.append(spread(grad_value, near_pick, near_slot, columns))
        far_value_parts.append(spread(grad_value, far_pick, far_slot, groups))

    def joined(parts):
        return jnp.concatenate(parts, axis=-1)

    near_back_keys, near_back_values = (
        lax.all_to_all(joined(near_key_parts), "seq", split_axis=0, concat_axis=0, tiled=True),
        lax.all_to_all(joined(near_value_parts), "seq", split_axis=0, concat_axis=0, tiled=True),
    )
    far_back_keys, far_back_values = (
        lax.all_to_all(joined(far_key_parts), "grp", split_axis=0, concat_axis=0, tiled=True),
        lax.all_to_all(joined(far_value_parts), "grp", split_axis=0, concat_axis=0, tiled=True),
    )
    near_onehot = (near_rank[None, :] == ranks[:, None]).astype(jnp.bfloat16)
    far_onehot = (far_rank[None, :] == ranks[:, None]).astype(jnp.bfloat16)

    def collect(own_part, near_back, far_back):
        total = own_part.astype(jnp.float32)
        total = total + jnp.einsum(
            "rp,ptw->rtw", near_onehot, near_back, preferred_element_type=jnp.float32
        )
        total = total + jnp.einsum(
            "rg,gtw->rtw", far_onehot, far_back, preferred_element_type=jnp.float32
        )
        return total.astype(jnp.bfloat16).reshape(1, tile_dev, 1, tile_rows, width)

    attended = joined(attended_parts).reshape(1, tile_dev, 1, tile_rows, width)
    grad_queries = joined(query_parts).reshape(1, tile_dev, 1, tile_rows, width)
    grad_keys = collect(joined(own_key_parts), near_back_keys, far_back_keys)
    grad_values = collect(joined(own_value_parts), near_back_values, far_back_values)
    return (attended, grad_queries, grad_keys, grad_values)


def solution(mesh):
    return jax.shard_map(
        per_device,
        mesh=mesh,
        in_specs=(
            P("grp", None, "seq", None, None),
            P("grp", None, "seq", None, None),
            P("grp", None, "seq", None, None),
            P("grp", None, "seq", None, None),
            P(),
            P(),
        ),
        out_specs=(
            P("grp", None, "seq", None, None),
            P("grp", None, "seq", None, None),
            P("grp", None, "seq", None, None),
            P("grp", None, "seq", None, None),
        ),
        check_vma=False,
    )
```

profile of v0, /device:TPU:10, one launch (start us, length us, event | category | flops | bytes accessed | tf_op | source)
XLA Modules:
  0.0 857.6 jit_solution(12798939972070502319)
XLA Ops:
  17.0 5.0 all-to-all-start
  27.1 9.4 %all-to-all-done = bf16[8,128,512]{2,1,0:T(8,128)(2,1)S(1)} async-done(((bf16[8,128,512]{2,1,0:T(8,128)(2,1)}), bf16[8,128,512]{2,1,0:T(8,128)(2,1)S(1)}, u32[]{:S(2)}, u32[]{:S(2)}) %all-to-all-start) | async-done | bytes 1048608 | tf_op jit(solution)/shard_map/all_to_all | solution.py:85
  36.5 5.6 all-to-all-start.1
  124.0 7.9 all-gather.5.cloned.1.call-done
  131.9 19.3 %fusion.26 = bf16[32,128,512]{2,0,1:T(8,128)(2,1)S(1)} fusion(bf16[1,96,1,128,512]{4,3,2,0,1:T(8,128)(2,1)} %all-gather.5.cloned.1.call-done, s32[96]{0:T(128)S(1)} %get-tuple-element.179, s32[96]{0:T(128)S(1)} %copy-done.72, s32[32]{0:T(128)S(1)} %select_reduce_fusion), kind=kOutput, calls=%fused_computation.121 | convolution fusion | flops 404759552 | bytes 16778112 | tf_op jit(solution)/shard_map/pn,ntw->ptw/dot_general | solution.py:77
  158.4 92.9 %all-gather.7.cloned.1.call-done = bf16[1,96,1,128,512]{4,3,2,0,1:T(8,128)(2,1)} async-done(((bf16[1,3,1,128,512]{4,3,2,0,1:T(8,128)(2,1)}), bf16[1,96,1,128,512]{4,3,2,0,1:T(8,128)(2,1)}) %all-gather.7.cloned.1.call-update) | async-done | bytes 12582928 | tf_op jit(solution)/shard_map/all_gather | solution.py:67
  251.3 19.1 %fusion.29 = bf16[32,128,512]{2,0,1:T(8,128)(2,1)S(1)} fusion(bf16[1,96,1,128,512]{4,3,2,0,1:T(8,128)(2,1)} %all-gather.7.cloned.1.call-done, s32[96]{0:T(128)S(1)} %get-tuple-element.179, s32[96]{0:T(128)S(1)} %copy-done.72, s32[32]{0:T(128)S(1)} %select_reduce_fusion), kind=kOutput, calls=%fused_computation.122 | convolution fusion | flops 404759552 | bytes 16778112 | tf_op jit(solution)/shard_map/pn,ntw->ptw/dot_general | solution.py:76
  314.9 8.7 %fusion.35 = (bf16[3,16,128,128]{2,3,1,0:T(8,128)(2,1)}, bf16[3,16,128,128]{2,3,1,0:T(8,128)(2,1)S(1)}, bf16[3,16,128,128]{2,3,1,0:T(8,128)(2,1)}, bf16[3,16,128,128]{2,3,1,0:T(8,128)(2,1)S(1)}) fusion(bf16[3,16,128,128]{2,3,1,0:T(8,128)(2,1)} %bitcast.460, bf16[3,16,128,128]{2,3,1,0:T(8,128)(2,1)} %copy.966, bf16[3,16,128,128]{2,3,1,0:T(8,128)(2,1)S(1)} %bitcast.452, ...), kind=kLoop, calls=%fused_computation.134 | loop fusion | flops 15728640 | bytes 25166064 | tf_op jit(solution)/shard_map/jit(_where)/select_n | solution.py:125
  329.2 4.9 fusion.39
  334.1 6.2 fusion.18
  340.3 6.1 fusion.11
  346.4 4.0 fusion.13
  353.4 3.5 convolution_bitcast_fusion
  356.9 3.2 fusion.6
  371.5 3.5 convolution_bitcast_fusion.2
  375.0 3.0 fusion.8
  378.1 3.0 multiply_reduce_fusion.3
  383.6 4.8 fusion.9
  408.1 32.1 %bitcast_select_fusion.18 = (f32[3,16,128,128]{2,3,1,0:T(8,128)}, f32[3,16,128,128]{2,3,1,0:T(8,128)}, f32[3,16,128,128]{2,3,1,0:T(8,128)}, f32[3,16,128,128]{2,...) fusion(f32[3,16,128,2,64]{2,4,3,1,0:T(8,128)S(1)} %copy.1022, ...), kind=kLoop, calls=%fused_computation.106 | loop fusion | flops 18874368 | bytes 100663440 | tf_op jit(solution)/shard_map/jit(_where)/select_n | solution.py:105
  440.2 3.5 copy.1033
  443.8 7.1 scatter_fusion.11
  451.0 3.6 copy.1032
  454.6 6.7 scatter_fusion.10
  462.1 3.6 copy.1031
  465.7 6.7 scatter_fusion.9
  473.2 3.6 copy.1030
  476.8 6.7 scatter_fusion.8
  485.9 4.8 all-to-all-start.3
  493.1 6.7 scatter_fusion.23
  499.8 3.5 copy.1056
  503.4 6.7 scatter_fusion.22
  510.9 3.7 copy.1055
  514.6 6.7 scatter_fusion.21
  522.1 3.6 copy.1054
  525.7 6.7 scatter_fusion.20
  534.8 5.0 all-to-all-start.5
  542.5 6.7 scatter_fusion.7
  549.4 3.6 copy.1026
  553.2 6.7 scatter_fusion.6
  561.0 3.6 copy.1025
  564.8 6.7 scatter_fusion.5
  572.7 3.6 copy.1024
  576.5 6.7 scatter_fusion.4
  587.0 7.5 all-to-all-start.2
  597.2 6.7 scatter_fusion.19
  604.1 3.6 copy.1050
  607.9 6.7 scatter_fusion.18
  615.8 3.5 copy.1049
  619.6 6.7 scatter_fusion.17
  627.5 3.5 copy.1048
  631.3 6.7 scatter_fusion.16
  641.8 50.1 %all-to-all-done.2 = bf16[32,128,512]{2,1,0:T(8,128)(2,1)} async-done(((bf16[32,128,512]{2,1,0:T(8,128)(2,1)}), bf16[32,128,512]{2,1,0:T(8,128)(2,1)}, u32[]{:S(2)}, u32[]{:S(2)}) %all-to-all-start.2) | async-done | bytes 4194336 | tf_op jit(solution)/shard_map/all_to_all | solution.py:186
  691.9 5.1 all-to-all-start.4
  707.9 3.3 fusion.123
  718.0 10.2 %scatter_fusion.3 = f32[3,128,128]{2,1,0:T(8,128)} fusion(f32[3,128,128]{2,1,0:T(8,128)} %broadcast.258.clone, s32[48]{0:T(128)S(1)} %copy-done.41, f32[48,128,128]{2,1,0:T(8,128)S(1)} %copy.1023), kind=kCustom, calls=%fused_computation.31 | custom fusion | flops 786432 | bytes 9437376 | tf_op jit(solution)/shard_map/scatter-add | solution.py:105
  732.2 10.2 %scatter_fusion.2 = f32[3,128,128]{2,1,0:T(8,128)} fusion(f32[3,128,128]{2,1,0:T(8,128)} %broadcast.258.clone.1, s32[48]{0:T(128)S(1)} %copy-done.41, f32[48,128,128]{2,1,0:T(8,128)S(1)} %copy.1020), kind=kCustom, calls=%fused_computation.30 | custom fusion | flops 786432 | bytes 9437376 | tf_op jit(solution)/shard_map/scatter-add | solution.py:105
  746.5 10.2 %scatter_fusion.1 = f32[3,128,128]{2,1,0:T(8,128)} fusion(f32[3,128,128]{2,1,0:T(8,128)} %broadcast.258.clone.2, s32[48]{0:T(128)S(1)} %copy-done.41, f32[48,128,128]{2,1,0:T(8,128)S(1)} %copy.1017), kind=kCustom, calls=%fused_computation.29 | custom fusion | flops 786432 | bytes 9437376 | tf_op jit(solution)/shard_map/scatter-add | solution.py:105
  760.7 10.2 %scatter_fusion = f32[3,128,128]{2,1,0:T(8,128)} fusion(f32[3,128,128]{2,1,0:T(8,128)} %broadcast.258.clone.3, s32[48]{0:T(128)S(1)} %copy-done.41, f32[48,128,128]{2,1,0:T(8,128)S(1)} %copy.1014), kind=kCustom, calls=%fused_computation.28 | custom fusion | flops 786432 | bytes 9437376 | tf_op jit(solution)/shard_map/scatter-add | solution.py:105
  775.6 10.2 %scatter_fusion.15 = f32[3,128,128]{2,1,0:T(8,128)} fusion(f32[3,128,128]{2,1,0:T(8,128)} %broadcast.258.clone.4, s32[48]{0:T(128)S(1)} %copy-done.41, f32[48,128,128]{2,1,0:T(8,128)S(1)} %copy.1047), kind=kCustom, calls=%fused_computation.43 | custom fusion | flops 786432 | bytes 9437376 | tf_op jit(solution)/shard_map/scatter-add | solution.py:105
  789.8 10.2 %scatter_fusion.14 = f32[3,128,128]{2,1,0:T(8,128)} fusion(f32[3,128,128]{2,1,0:T(8,128)} %broadcast.258.clone.5, s32[48]{0:T(128)S(1)} %copy-done.41, f32[48,128,128]{2,1,0:T(8,128)S(1)} %copy.1044), kind=kCustom, calls=%fused_computation.42 | custom fusion | flops 786432 | bytes 9437376 | tf_op jit(solution)/shard_map/scatter-add | solution.py:105
  804.7 10.2 %scatter_fusion.13 = f32[3,128,128]{2,1,0:T(8,128)} fusion(f32[3,128,128]{2,1,0:T(8,128)} %broadcast.258.clone.6, s32[48]{0:T(128)S(1)} %copy-done.41, f32[48,128,128]{2,1,0:T(8,128)S(1)} %copy.1041), kind=kCustom, calls=%fused_computation.41 | custom fusion | flops 786432 | bytes 9437376 | tf_op jit(solution)/shard_map/scatter-add | solution.py:105
  819.8 10.2 %scatter_fusion.12 = f32[3,128,128]{2,1,0:T(8,128)} fusion(f32[3,128,128]{2,1,0:T(8,128)} %broadcast.258.clone.7, s32[48]{0:T(128)S(1)} %copy-done.41, f32[48,128,128]{2,1,0:T(8,128)S(1)} %copy.1038), kind=kCustom, calls=%fused_computation.40 | custom fusion | flops 786432 | bytes 9437376 | tf_op jit(solution)/shard_map/scatter-add | solution.py:105
  838.6 4.6 fusion.24
  844.4 4.6 fusion.22
  (367 shorter events, 278.0 us)
Async XLA Ops:
  7.2 5.2 copy-start.12
  7.2 124.7 %all-gather.5.cloned.1.call-start = ((), (), s32[]{:S(2)}) async-start(), calls=%async_computation.6 | async-start | bytes 12976128 | tf_op jit(solution)/shard_map/all_gather | solution.py:68
  7.9 243.3 %all-gather.7.cloned.1.call-start = ((), (), s32[]{:S(2)}) async-start(), calls=%async_computation.7 | async-start | bytes 12976128 | tf_op jit(solution)/shard_map/all_gather | solution.py:67
  14.0 8.0 copy-start.56
  14.0 8.1 copy-start.65
  14.0 11.4 %copy-start.13 = (bf16[1,3,1,128,512]{4,3,2,1,0:T(8,128)(2,1)S(1)}, bf16[1,3,1,128,512]{4,3,2,1,0:T(8,128)(2,1)}, u32[]{:S(2)}) copy-start(bf16[1,3,1,128,512]{4,3,2,1,0:T(8,128)(2,1)} %param.17) | copy-start | bytes 1179652
  17.0 8.5 copy-start.51
  17.0 9.3 %copy-start.52 = (bf16[1,3,1,128,512]{4,3,2,1,0:T(8,128)(2,1)S(1)}, bf16[1,3,1,128,512]{4,3,2,1,0:T(8,128)(2,1)}, u32[]{:S(2)}) copy-start(bf16[1,3,1,128,512]{4,3,2,1,0:T(8,128)(2,1)} %param.16) | copy-start | bytes 1179652
  17.0 19.5 %all-to-all-start = ((bf16[8,128,512]{2,1,0:T(8,128)(2,1)}), bf16[8,128,512]{2,1,0:T(8,128)(2,1)S(1)}, u32[]{:S(2)}, u32[]{:S(2)}) async-start(bf16[8,128,512]{2,1,0:T(8,128)(2,1)} %get-tuple-element.167), calls=%async_computation | async-start | bytes 2097152 | tf_op jit(solution)/shard_map/all_to_all | solution.py:85
  24.1 302.4 %copy-start.68 = (pred[3,16]{1,0:T(4,128)(4,1)}, pred[3,16]{1,0:T(4,128)(4,1)S(1)}, u32[]{:S(2)}) copy-start(pred[3,16]{1,0:T(4,128)(4,1)S(1)} %get-tuple-element.61) | copy-start | bytes 148
  24.7 301.9 %copy-start.66 = (pred[3,16]{1,0:T(4,128)(4,1)}, pred[3,16]{1,0:T(4,128)(4,1)S(1)}, u32[]{:S(2)}) copy-start(pred[3,16]{1,0:T(4,128)(4,1)S(1)} %get-tuple-element.69) | copy-start | bytes 148
  36.5 11.7 %copy-start.24 = (bf16[8,128,512]{2,1,0:T(8,128)(2,1)}, bf16[8,128,512]{2,1,0:T(8,128)(2,1)S(1)}, u32[]{:S(2)}) copy-start(bf16[8,128,512]{2,1,0:T(8,128)(2,1)S(1)} %all-to-all-done) | copy-start | bytes 3145732
  36.5 54.1 %all-to-all-start.1 = ((bf16[8,128,512]{2,1,0:T(8,128)(2,1)}), bf16[8,128,512]{2,1,0:T(8,128)(2,1)}, u32[]{:S(2)}, u32[]{:S(2)}) async-start(bf16[8,128,512]{2,1,0:T(8,128)(2,1)} %get-tuple-element.166), calls=%async_computation.1 | async-start | bytes 2097152 | tf_op jit(solution)/shard_map/all_to_all | solution.py:82
  44.3 38.4 %copy-start.42 = (s32[48]{0:T(128)}, s32[48]{0:T(128)S(1)}, u32[]{:S(2)}) copy-start(s32[48]{0:T(128)S(1)} %reshape.872) | copy-start | bytes 580
  57.4 4.6 copy-start.55
  62.2 261.5 %copy-start.36 = (bf16[3,128,128]{1,2,0:T(8,128)(2,1)}, bf16[3,128,128]{1,2,0:T(8,128)(2,1)S(1)}, u32[]{:S(2)}) copy-start(bf16[3,128,128]{1,2,0:T(8,128)(2,1)S(1)} %copy.972) | copy-start | bytes 294916
  73.8 8.1 copy-start.53
  73.8 9.0 %copy-start.73 = (pred[3,16]{1,0:T(4,128)(4,1)S(1)}, pred[3,16]{1,0:T(4,128)(4,1)}, u32[]{:S(2)}) copy-start(pred[3,16]{1,0:T(4,128)(4,1)} %get-tuple-element.165) | copy-start | bytes 148
  74.6 6.5 copy-start.54
  119.3 12.6 %copy-start.72 = (s32[96]{0:T(128)S(1)}, s32[96]{0:T(128)}, u32[]{:S(2)}) copy-start(s32[96]{0:T(128)} %get-tuple-element.180) | copy-start | bytes 1156
  325.3 2.9 copy-start.20
  325.3 3.4 copy-start.21
  325.3 3.8 copy-start.22
  329.2 4.9 copy-start.46
  334.0 6.3 copy-start.14
  334.0 6.3 copy-start.15
  334.1 6.3 copy-start.29
  334.1 6.3 copy-start.47
  346.4 4.0 copy-start.35
  346.4 4.0 copy-start.61
  356.9 3.3 copy-start.33
  356.9 3.3 copy-start.64
  360.2 28.3 %copy-start.4 = (bf16[3,2,128,16,128]{2,4,3,1,0:T(8,128)(2,1)}, bf16[3,2,128,16,128]{2,4,3,1,0:T(8,128)(2,1)S(1)}, u32[]{:S(2)}) copy-start(bf16[3,2,128,16,128]{2,4,3,1,0:T(8,128)(2,1)S(1)} %fusion.6) | copy-start | bytes 9437188
  365.6 2.9 copy-start.34
  365.6 2.9 copy-start.63
  368.5 36.5 %copy-start.5 = (bf16[3,2,128,16,128]{2,4,3,1,0:T(8,128)(2,1)}, bf16[3,2,128,16,128]{2,4,3,1,0:T(8,128)(2,1)S(1)}, u32[]{:S(2)}) copy-start(bf16[3,2,128,16,128]{2,4,3,1,0:T(8,128)(2,1)S(1)} %fusion.7) | copy-start | bytes 9437188
  371.5 6.5 slice-start
  375.0 3.0 copy-start.32
  375.0 3.0 copy-start.62
  375.0 3.0 slice-start.1
  378.0 23.9 %copy-start.6 = (bf16[3,2,128,16,128]{2,4,3,1,0:T(8,128)(2,1)}, bf16[3,2,128,16,128]{2,4,3,1,0:T(8,128)(2,1)S(1)}, u32[]{:S(2)}) copy-start(bf16[3,2,128,16,128]{2,4,3,1,0:T(8,128)(2,1)S(1)} %fusion.8) | copy-start | bytes 9437188
  383.6 4.8 copy-start.39
  388.4 10.4 %copy-start.7 = (bf16[3,2,128,16,128]{2,4,3,1,0:T(8,128)(2,1)}, bf16[3,2,128,16,128]{2,4,3,1,0:T(8,128)(2,1)S(1)}, u32[]{:S(2)}) copy-start(bf16[3,2,128,16,128]{2,4,3,1,0:T(8,128)(2,1)S(1)} %fusion.9) | copy-start | bytes 9437188
  393.9 3.0 copy-start.30
  440.2 3.6 copy-start.45
  483.6 7.1 copy-start.11
  485.9 48.9 %all-to-all-start.3 = ((bf16[8,128,512]{2,1,0:T(8,128)(2,1)}), bf16[8,128,512]{2,1,0:T(8,128)(2,1)}, u32[]{:S(2)}, u32[]{:S(2)}) async-start(bf16[8,128,512]{2,1,0:T(8,128)(2,1)} %pad_maximum_fusion.2), calls=%async_computation.3 | async-start | bytes 2097152 | tf_op jit(solution)/shard_map/all_to_all | solution.py:190
  532.5 7.4 copy-start.10
  534.8 52.2 %all-to-all-start.5 = ((bf16[8,128,512]{2,1,0:T(8,128)(2,1)}), bf16[8,128,512]{2,1,0:T(8,128)(2,1)}, u32[]{:S(2)}, u32[]{:S(2)}) async-start(bf16[8,128,512]{2,1,0:T(8,128)(2,1)} %pad_maximum_fusion.3), calls=%async_computation.5 | async-start | bytes 2097152 | tf_op jit(solution)/shard_map/all_to_all | solution.py:191
  587.0 7.5 copy-start.9
  587.0 104.9 %all-to-all-start.2 = ((bf16[32,128,512]{2,1,0:T(8,128)(2,1)}), bf16[32,128,512]{2,1,0:T(8,128)(2,1)}, u32[]{:S(2)}, u32[]{:S(2)}) async-start(bf16[32,128,512]{2,1,0:T(8,128)(2,1)} %pad_maximum_fusion), calls=%async_computation.2 | async-start | bytes 8388608 | tf_op jit(solution)/shard_map/all_to_all | solution.py:186
  641.8 56.4 %copy-start.57 = (bf16[3,2,64,128]{3,2,1,0:T(8,128)(2,1)S(1)}, bf16[3,2,64,128]{3,2,1,0:T(8,128)(2,1)}, u32[]{:S(2)}) copy-start(bf16[3,2,64,128]{3,2,1,0:T(8,128)(2,1)} %get-tuple-element.172) | copy-start | bytes 294916
  641.8 57.1 %copy-start.58 = (bf16[3,2,64,128]{3,2,1,0:T(8,128)(2,1)S(1)}, bf16[3,2,64,128]{3,2,1,0:T(8,128)(2,1)}, u32[]{:S(2)}) copy-start(bf16[3,2,64,128]{3,2,1,0:T(8,128)(2,1)} %get-tuple-element.174) | copy-start | bytes 294916
  641.8 57.9 %copy-start.59 = (bf16[3,2,64,128]{3,2,1,0:T(8,128)(2,1)S(1)}, bf16[3,2,64,128]{3,2,1,0:T(8,128)(2,1)}, u32[]{:S(2)}) copy-start(bf16[3,2,64,128]{3,2,1,0:T(8,128)(2,1)} %get-tuple-element.176) | copy-start | bytes 294916
  641.8 58.7 %copy-start.60 = (bf16[3,2,64,128]{3,2,1,0:T(8,128)(2,1)S(1)}, bf16[3,2,64,128]{3,2,1,0:T(8,128)(2,1)}, u32[]{:S(2)}) copy-start(bf16[3,2,64,128]{3,2,1,0:T(8,128)(2,1)} %get-tuple-element.178) | copy-start | bytes 294916
  641.8 59.4 %copy-start.3 = (bf16[3,16,128,128]{2,3,1,0:T(8,128)(2,1)S(1)}, bf16[3,16,128,128]{2,3,1,0:T(8,128)(2,1)}, u32[]{:S(2)}) copy-start(bf16[3,16,128,128]{2,3,1,0:T(8,128)(2,1)} %copy-done.2) | copy-start | bytes 4718596
  691.9 152.5 %all-to-all-start.4 = ((bf16[32,128,512]{2,1,0:T(8,128)(2,1)}), bf16[32,128,512]{2,1,0:T(8,128)(2,1)}, u32[]{:S(2)}, u32[]{:S(2)}) async-start(bf16[32,128,512]{2,1,0:T(8,128)(2,1)} %pad_maximum_fusion.1), calls=%async_computation.4 | async-start | bytes 8388608 | tf_op jit(solution)/shard_map/all_to_all | solution.py:187
  697.1 7.5 copy-start.1
  707.2 4.8 copy-start.8
  714.9 3.1 copy-start.41
  819.8 14.8 %copy-start.71 = (s32[8]{0:T(128)S(1)}, s32[8]{0:T(128)}, u32[]{:S(2)}) copy-start(s32[8]{0:T(128)} %copy-done.70) | copy-start | bytes 100
  838.6 4.6 copy-start.48
  844.4 4.7 copy-start.49
  844.4 4.7 copy-start.50
  (21 other events, 35.3 us)
Sparse Core Ops, SparseCore 0:
  10.6 121.2 all-gather.4
  134.4 116.7 all-gather.6
where the time goes:
time: 874 us; the launch traced here: 858 us
  other arithmetic  280 us (32%)
  local copies, waits for them, and re-layouts  247 us (28%)
  waiting for transfers between devices  162 us (19%)
  matrix products  120 us (14%)
  starting transfers between devices  33.1 us (4%)
  between operations  15.9 us (2%)
    scatter-add x24, other arithmetic, spread(): total.at[slot].add(jnp.where(chosen_pick, term, 0.0)).astype(jnp.bfloat16)  190 us
    all_gather x1, waiting for transfers between devices, per_device(): lax.all_gather(key_tiles, 'seq', axis=0, tiled=True)  92.9 us
    select_n x24, local copies, waits for them, and re-layouts, spread(): jnp.where(chosen_pick, term, 0.0)  72.8 us
    all_to_all x1, waiting for transfers between devices, per_device(): lax.all_to_all(joined(near_key_parts), 'seq', split_axis=0, concat_axis=0...  50.1 us
    gather x16, local copies, waits for them, and re-layouts, fetch(): from_near = jnp.take(columns_of(near_source), near_slot, axis=0)  36.9 us
    gather x16, local copies, waits for them, and re-layouts, fetch(): from_far = jnp.take(columns_of(far_source), far_slot, axis=0)  36.7 us
    select_n x1, other arithmetic, spread(): jnp.where(chosen_pick, term, 0.0)  32.1 us
    gather x16, local copies, waits for them, and re-layouts, fetch(): from_own = jnp.take(columns_of(own_source), own_slot, axis=0)  31.8 us
  transfers between devices with their start and end apart: 8, of which 4 were waited for; matrix products, arithmetic and copies ran while one was open for 47% of the time, Pallas kernels for 0%

commit v1 on v0

v1 whole, which is shorter than its diff:
```python
import functools

import jax
import jax.numpy as jnp
from jax import lax
from jax.experimental import pallas as pl
from jax.experimental.pallas import tpu as pltpu
from jax.sharding import PartitionSpec as P

HEADS = 8
HEAD_DIM = 64
Y_SIZE = 4
LOG2E = 1.4426950408889634
HIDDEN = -1e30


def pack_kernel(q_ref, k_ref, v_ref, g_ref, kv_ref, qg_ref):
    for head in range(HEADS):
        at = head * HEAD_DIM
        cols = slice(at, at + HEAD_DIM)
        kv_ref[head] = jnp.concatenate([k_ref[:, :, cols], v_ref[:, :, cols]], axis=-1)
        qg_ref[head] = jnp.concatenate([q_ref[:, :, cols], g_ref[:, :, cols]], axis=-1)


def unpack_kernel(in_ref, first_ref, second_ref):
    for pair in range(HEADS // 2):
        even = in_ref[2 * pair]
        odd = in_ref[2 * pair + 1]
        cols = slice(pair * 128, pair * 128 + 128)
        first_ref[:, :, cols] = jnp.concatenate([even[..., :HEAD_DIM], odd[..., :HEAD_DIM]], axis=-1)
        second_ref[:, :, cols] = jnp.concatenate([even[..., HEAD_DIM:], odd[..., HEAD_DIM:]], axis=-1)


def far_kernel(rank_ref, kv_ref, out_ref, *, groups, zs):
    def step(at, carry):
        z = at % zs
        rank = jnp.maximum(rank_ref[at], 0)
        out_ref[at] = kv_ref[z, rank]
        return carry

    lax.fori_loop(0, groups * zs, step, 0)


def attend_kernel(
    code_ref, count_ref, near_ref, far_ref, qg_ref,
    odq_ref, dnear_ref, dfar_ref,
    table, totals, scores, dprobs, masks, weights, sems,
    *, tiles, entries, near, far,
):
    copies = [
        pltpu.make_async_copy(near_ref, table.at[pl.ds(0, near)], sems.at[0]),
        pltpu.make_async_copy(far_ref, table.at[pl.ds(near, far)], sems.at[1]),
    ]
    for copy in copies:
        copy.start()
    rows = 128
    key_at = lax.broadcasted_iota(jnp.int32, (rows, rows), 0)
    query_at = lax.broadcasted_iota(jnp.int32, (rows, rows), 1)
    masks[0] = jnp.zeros((rows, rows), jnp.float32)
    masks[1] = jnp.where(key_at <= query_at, 0.0, HIDDEN).astype(jnp.float32)
    masks[2] = jnp.full((rows, rows), HIDDEN, jnp.float32)
    table[near + far] = jnp.zeros((rows, rows), table.dtype)

    def clear(at, carry):
        totals[at] = jnp.zeros((rows, rows), jnp.float32)
        return carry

    lax.fori_loop(0, near + far + 1, clear, 0)
    for copy in copies:
        copy.wait()
    left = lax.broadcasted_iota(jnp.int32, (rows, rows), 1) < HEAD_DIM
    scale = HEAD_DIM ** -0.5

    def tile_step(tile, carry):
        qg = qg_ref[tile]
        weights[pl.ds(0, rows), :] = jnp.where(left, qg, jnp.zeros_like(qg))
        weights[pl.ds(rows, rows), :] = jnp.where(left, jnp.zeros_like(qg), qg)
        pairs = (count_ref[tile] + 1) // 2

        def score_step(pair, top):
            for half in range(2):
                entry = pair * 2 + half
                code = code_ref[tile * entries + entry]
                kv = table[code // 4]
                both = lax.dot_general(
                    kv, weights[...], (((1,), (1,)), ((), ())), preferred_element_type=jnp.float32
                )
                masked = both[:, :rows] + masks[code % 4]
                scores[entry] = masked
                dprobs[entry] = both[:, rows:]
                top = jnp.maximum(top, jnp.max(masked.reshape(rows // 8, 8, rows), axis=0))
            return top

        top = lax.fori_loop(0, pairs, score_step, jnp.full((8, rows), HIDDEN, jnp.float32))
        row_top = jnp.max(top, axis=0, keepdims=True)

        def exp_step(pair, carry):
            total, mixed = carry
            for half in range(2):
                entry = pair * 2 + half
                prob = jnp.exp2((scores[entry] - row_top) * (scale * LOG2E))
                scores[entry] = prob
                total = total + jnp.sum(prob.reshape(rows // 8, 8, rows), axis=0)
                mixed = mixed + jnp.sum((prob * dprobs[entry]).reshape(rows // 8, 8, rows), axis=0)
            return total, mixed

        zero = jnp.zeros((8, rows), jnp.float32)
        total, mixed = lax.fori_loop(0, pairs, exp_step, (zero, zero))
        inverse = 1.0 / jnp.sum(total, axis=0, keepdims=True)
        delta = jnp.sum(mixed, axis=0, keepdims=True) * inverse

        def grad_step(pair, carry):
            attended, grad_query = carry
            for half in range(2):
                entry = pair * 2 + half
                slot = code_ref[tile * entries + entry] // 4
                prob = scores[entry] * inverse
                dscore = prob * (dprobs[entry] - delta)
                both = jnp.concatenate([dscore, prob], axis=1).astype(jnp.bfloat16)
                totals[slot] = totals[slot] + jnp.dot(
                    both, weights[...], preferred_element_type=jnp.float32
                )
                mixed = lax.dot_general(
                    table[slot], both, (((0,), (0,)), ((), ())), preferred_element_type=jnp.float32
                )
                grad_query = grad_query + mixed[:HEAD_DIM, :rows]
                attended = attended + mixed[HEAD_DIM:, rows:]
            return attended, grad_query

        zero = jnp.zeros((HEAD_DIM, rows), jnp.float32)
        attended, grad_query = lax.fori_loop(0, pairs, grad_step, (zero, zero))
        joined = jnp.concatenate([attended, grad_query * scale], axis=0)
        odq_ref[tile] = joined.T.astype(odq_ref.dtype)
        return carry

    lax.fori_loop(0, tiles, tile_step, 0)
    scales = jnp.where(left, scale, 1.0).astype(jnp.float32)

    def near_out(at, carry):
        dnear_ref[at] = (totals[at] * scales).astype(dnear_ref.dtype)
        return carry

    def far_out(at, carry):
        dfar_ref[at] = (totals[near + at] * scales).astype(dfar_ref.dtype)
        return carry

    lax.fori_loop(0, near, near_out, 0)
    lax.fori_loop(0, far, far_out, 0)


def combine_kernel(rank_ref, near_ref, far_ref, out_ref, sums, *, ys, groups, zs, tile_dev):
    def add_near(at, carry):
        total = near_ref[0, at].astype(jnp.float32)
        for y in range(1, ys):
            total = total + near_ref[y, at].astype(jnp.float32)
        sums[at] = total
        return carry

    lax.fori_loop(0, zs * tile_dev, add_near, 0)

    def add_far(at, carry):
        rank = rank_ref[at]

        @pl.when(rank >= 0)
        def _():
            slot = (at % zs) * tile_dev + rank
            sums[slot] = sums[slot] + far_ref[at].astype(jnp.float32)

        return carry

    lax.fori_loop(0, groups * zs, add_far, 0)

    def write(at, carry):
        out_ref[at] = sums[at].astype(out_ref.dtype)
        return carry

    lax.fori_loop(0, zs * tile_dev, write, 0)


def limits(size):
    return pltpu.CompilerParams(vmem_limit_bytes=size << 20)


def vmem(count):
    return [pl.BlockSpec(memory_space=pltpu.VMEM) for _ in range(count)]


def smem(count):
    return [pl.BlockSpec(memory_space=pltpu.SMEM) for _ in range(count)]


def per_device(queries, key_input, value_input, grad_output, block_lists, block_flags):
    tile_dev = queries.shape[1]
    rows = queries.shape[3]
    width = queries.shape[4]
    entries = block_lists.shape[1]
    columns = lax.axis_size("seq")
    groups = lax.axis_size("grp")
    ys = Y_SIZE
    zs = columns // ys
    group_at = lax.axis_index("grp")
    y_at = lax.axis_index("seq") % ys
    group_tiles = tile_dev * columns
    z_groups = [[z * ys + y for z in range(zs)] for y in range(ys)]
    y_groups = [[z * ys + y for y in range(ys)] for z in range(zs)]
    bf16 = jnp.bfloat16
    near = group_tiles
    far = groups * zs
    tiles = zs * tile_dev

    lists = block_lists.reshape(groups, tile_dev, zs, ys, entries)
    flags = block_flags.reshape(groups, tile_dev, zs, ys, entries)
    lists = lax.dynamic_index_in_dim(lists, y_at, 3, keepdims=False)
    flags = lax.dynamic_index_in_dim(flags, y_at, 3, keepdims=False)
    present = lists >= 0
    safe = jnp.maximum(lists, 0)
    to_group = safe // group_tiles
    within = safe % group_tiles
    to_rank = within // columns
    to_column = within % columns
    z_ids = jnp.arange(zs, dtype=jnp.int32)[None, None, :, None]
    group_ids = jnp.arange(groups, dtype=jnp.int32)
    named = present & (to_group == group_at) & (to_column == z_ids * ys + y_at)
    far_rank = jnp.max(jnp.where(named, to_rank, -1), axis=(1, 3))
    far_rank = jnp.where(group_ids[:, None] == group_at, -1, far_rank).reshape(far)
    near_slot = (to_column % ys) * tiles + (to_column // ys) * tile_dev + to_rank
    far_slot = near + to_group * zs + z_ids
    slot = jnp.where(to_group == group_at, near_slot, far_slot)
    slot = jnp.where(present, slot, near + far)
    mask_at = jnp.where(present, jnp.where(flags != 0, 1, 0), 2)
    code = lax.dynamic_index_in_dim(slot * 4 + mask_at, group_at, 0, keepdims=False)
    code = jnp.transpose(code, (1, 0, 2)).reshape(tiles * entries)
    count = lax.dynamic_index_in_dim(present, group_at, 0, keepdims=False).astype(jnp.int32)
    count = jnp.transpose(jnp.sum(count, axis=2), (1, 0)).reshape(tiles)

    def rearrange(kernel, outs, size, *args):
        return pl.pallas_call(
            kernel, out_shape=outs, in_specs=vmem(len(args)), out_specs=vmem(len(outs)),
            compiler_params=limits(size),
        )(*args)

    head_shape = jax.ShapeDtypeStruct((HEADS, tile_dev, rows, 128), bf16)
    tile_shape = jax.ShapeDtypeStruct((tile_dev, rows, width), bf16)

    def flat(source):
        return source.reshape(tile_dev, rows, width)

    send_kv, send_qg = rearrange(
        pack_kernel, (head_shape, head_shape), 16,
        flat(queries), flat(key_input), flat(value_input), flat(grad_output),
    )

    def over_z(source):
        return lax.all_to_all(
            source, "seq", split_axis=0, concat_axis=0, tiled=True, axis_index_groups=z_groups
        )

    kv = over_z(send_kv)
    qg = over_z(send_qg)
    near_kv = lax.all_gather(
        kv.reshape(tiles, rows, 128), "seq", axis=0, tiled=True, axis_index_groups=y_groups
    )
    far_send = pl.pallas_call(
        functools.partial(far_kernel, groups=groups, zs=zs),
        out_shape=jax.ShapeDtypeStruct((far, rows, 128), bf16),
        in_specs=smem(1) + vmem(1), out_specs=vmem(1)[0], compiler_params=limits(16),
    )(far_rank, kv)
    far_kv = lax.all_to_all(far_send, "grp", split_axis=0, concat_axis=0, tiled=True)

    slots = near + far + 1
    odq, dnear, dfar = pl.pallas_call(
        functools.partial(attend_kernel, tiles=tiles, entries=entries, near=near, far=far),
        out_shape=(
            jax.ShapeDtypeStruct((tiles, rows, 128), bf16),
            jax.ShapeDtypeStruct((near, rows, 128), bf16),
            jax.ShapeDtypeStruct((far, rows, 128), bf16),
        ),
        in_specs=smem(2) + [pl.BlockSpec(memory_space=pl.ANY)] * 2 + vmem(1),
        out_specs=vmem(3),
        scratch_shapes=[
            pltpu.VMEM((slots, rows, 128), bf16),
            pltpu.VMEM((slots, rows, 128), jnp.float32),
            pltpu.VMEM((entries, rows, rows), jnp.float32),
            pltpu.VMEM((entries, rows, rows), jnp.float32),
            pltpu.VMEM((3, rows, rows), jnp.float32),
            pltpu.VMEM((2 * rows, 128), bf16),
            pltpu.SemaphoreType.DMA((2,)),
        ],
        compiler_params=limits(48),
    )(code, count, near_kv, far_kv, qg.reshape(tiles, rows, 128))

    far_back = lax.all_to_all(dfar, "grp", split_axis=0, concat_axis=0, tiled=True)
    near_back = lax.all_to_all(
        dnear, "seq", split_axis=0, concat_axis=0, tiled=True, axis_index_groups=y_groups
    )
    odq_back = over_z(odq.reshape(zs, tile_dev, rows, 128))
    dkv = pl.pallas_call(
        functools.partial(combine_kernel, ys=ys, groups=groups, zs=zs, tile_dev=tile_dev),
        out_shape=jax.ShapeDtypeStruct((tiles, rows, 128), bf16),
        in_specs=smem(1) + vmem(2), out_specs=vmem(1)[0],
        scratch_shapes=[pltpu.VMEM((tiles, rows, 128), jnp.float32)],
        compiler_params=limits(24),
    )(far_rank, near_back.reshape(ys, tiles, rows, 128), far_back)
    dkv_back = over_z(dkv.reshape(zs, tile_dev, rows, 128))
    attended, grad_queries = rearrange(unpack_kernel, (tile_shape, tile_shape), 16, odq_back)
    grad_keys, grad_values = rearrange(unpack_kernel, (tile_shape, tile_shape), 16, dkv_back)
    return tuple(
        out.reshape(1, tile_dev, 1, rows, width)
        for out in (attended, grad_queries, grad_keys, grad_values)
    )


def solution(mesh):
    spec = P("grp", None, "seq", None, None)
    return jax.shard_map(
        per_device,
        mesh=mesh,
        in_specs=(spec, spec, spec, spec, P(), P()),
        out_specs=(spec, spec, spec, spec),
        check_vma=False,
    )
```

time: 874 us -> 319 us (0.36); the launches traced: 858 us -> 318 us
  other arithmetic: 280 us -> 0.72 us
  local copies, waits for them, and re-layouts: 247 us -> 10.7 us
  matrix products: 120 us -> 0 us
  blocking collectives: 0 us -> 120 us
  waiting for transfers between devices: 162 us -> 78.5 us
  Pallas kernels: 0 us -> 77.9 us
  starting transfers between devices: 33.1 us -> 16.3 us
    scatter-add x24 -> x0, other arithmetic: 190 us -> none  [spread(): total.at[slot].add(jnp.where(chosen_pick, term, 0.0)).astype(jnp.bfloat16)]
    all_to_all x0 -> x3, blocking collectives: none -> 120 us  [the longest x1 44.3 us: per_device(): lax.all_to_all(dfar, 'grp', split_axis=0, concat_axis=0, tiled=True)]
    dot_general x30 -> x0, matrix products: 120 us -> none  [the longest x1 19.3 us: per_device(): jnp.einsum('pn,ntw->ptw', select, pieces[1], preferred_element_type=jnp.f...]
    gather x52 -> x0, local copies, waits for them, and re-layouts: 110 us -> none  [the longest x16 36.9 us: fetch(): from_near = jnp.take(columns_of(near_source), near_slot, axis=0)]
    all_gather x2 -> x1, waiting for transfers between devices: 101 us -> 0.01 us  [per_device(): lax.all_gather(kv.reshape(tiles, rows, 128), 'seq', axis=0, tiled=True, a...]
    pallas_call x0 -> x6, Pallas kernels: none -> 77.9 us  [the longest x1 69.5 us: per_device(): pl.pallas_call(functools.partial(attend_kernel, tiles=tiles, entries=entr...]
    select_n x24 -> x1, local copies, waits for them, and re-layouts: 72.8 us -> 0.08 us  [per_device(): jnp.where(group_ids[:, None] == group_at, -1, far_rank).reshape(far)]
    select_n x6 -> x2, other arithmetic: 49.3 us -> 0.09 us  [the longest x1 0.07 us: per_device(): jnp.where(group_ids[:, None] == group_at, -1, far_rank).reshape(far)]
  transfers between devices with their start and end apart: 8 -> 5, of which waited for: 4 -> 4; matrix products, arithmetic and copies ran while one was open for 47% -> 0% of each run, Pallas kernels for 0% -> 2%
where the time goes in v1:
time: 319 us; the launch traced here: 318 us
  blocking collectives  120 us (38%)
  waiting for transfers between devices  78.5 us (25%)
  Pallas kernels  77.9 us (24%)
  starting transfers between devices  16.3 us (5%)
  between operations  14.2 us (4%)
  local copies, waits for them, and re-layouts  10.7 us (3%)
    pallas_call x1, Pallas kernels, per_device(): pl.pallas_call(functools.partial(attend_kernel, tiles=tiles, entries=entr...  69.5 us
    all_to_all x3, waiting for transfers between devices, over_z(): lax.all_to_all(source, 'seq', split_axis=0, concat_axis=0, tiled=True, ax...  53.2 us
    all_to_all x1, blocking collectives, per_device(): lax.all_to_all(dfar, 'grp', split_axis=0, concat_axis=0, tiled=True)  44.3 us
    all_to_all x1, blocking collectives, per_device(): lax.all_to_all(dnear, 'seq', split_axis=0, concat_axis=0, tiled=True, axi...  44.1 us
    all_to_all x1, blocking collectives, over_z(): lax.all_to_all(source, 'seq', split_axis=0, concat_axis=0, tiled=True, ax...  31.6 us
    all_to_all x1, waiting for transfers between devices, per_device(): lax.all_to_all(far_send, 'grp', split_axis=0, concat_axis=0, tiled=True)  25.3 us
    all_to_all x3, starting transfers between devices, over_z(): lax.all_to_all(source, 'seq', split_axis=0, concat_axis=0, tiled=True, ax...  11.4 us
    unnamed x30, local copies, waits for them, and re-layouts  10.2 us
  transfers between devices with their start and end apart: 5, of which 4 were waited for; matrix products, arithmetic and copies ran while one was open for 0% of the time, Pallas kernels for 2%

profile of v1, /device:TPU:10, one launch (start us, length us, event | category | flops | bytes accessed | tf_op | source)
XLA Modules:
  0.0 318.4 jit_solution(17614019017811385314)
XLA Ops:
  7.2 0.0 all-gather.2.cloned.1.call-start
  7.2 0.0 copy-start.7
  7.2 1.0 copy-done.7
  8.2 0.0 copy-start.8
  8.2 1.0 copy-done.8
  9.2 0.0 copy-start.9
  9.2 1.0 copy-done.9
  10.2 0.0 copy-start.10
  10.2 1.0 copy-done.10
  11.2 1.4 shard_map.93
  12.6 0.0 copy-start.12
  12.6 0.0 copy-start.13
  12.6 31.6 %all_to_all.35.kv_ref = bf16[8,3,128,128]{3,2,1,0:T(8,128)(2,1)} all-to-all(bf16[8,3,128,128]{3,2,1,0:T(8,128)(2,1)S(1)} %get-tuple-element.13), channel_id=1, replica_groups={{0,4,8,12,16,20,24,28},{1,5,9,13,17,21,25,29},{2,6,10,14,18,22,26,30},{..., dimensions={0} | all-to-all | bytes 1572864 | tf_op jit(solution)/shard_map/all_to_all | solution.py:254
  44.2 0.0 copy-start.2
  44.2 0.0 all-gather.2.cloned.1.call-update
  44.2 3.7 %all-to-all-start.2 = ((bf16[8,3,128,128]{3,2,1,0:T(8,128)(2,1)}), bf16[8,3,128,128]{3,2,1,0:T(8,128)(2,1)S(1)}, u32[]{:S(2)}, u32[]{:S(2)}) async-start(bf16[8,3,128,128]{3,2,1,0:T(8,128)(2,1)} %get-tuple-element.14), calls=%async_computation.2 | async-start | bytes 1572864 | tf_op jit(solution)/shard_map/all_to_all | solution.py:254
  47.9 0.0 copy-done.12
  47.9 0.2 copy.57
  48.1 0.0 copy-done.13
  48.1 0.2 copy.64
  48.3 0.2 constant_dynamic-slice_fusion
  48.5 0.4 fusion
  49.0 0.1 broadcast_select_fusion
  49.0 0.1 select_n.88.rank_ref
  49.1 0.0 copy-done.2
  49.1 1.2 shard_map.94
  50.3 0.0 copy-start.1
  50.3 1.4 copy-done.1
  51.7 17.8 %all-to-all-done.2 = bf16[8,3,128,128]{3,2,1,0:T(8,128)(2,1)S(1)} async-done(((bf16[8,3,128,128]{3,2,1,0:T(8,128)(2,1)}), bf16[8,3,128,128]{3,2,1,0:T(8,128)(2,1)S(1)}, u32[]{:S(2)}, u32[]{:S(2)}) %all-to-all-start.2) | async-done | bytes 786464 | tf_op jit(solution)/shard_map/all_to_all | solution.py:254
  69.4 0.0 copy-start.4
  69.5 0.9 copy-done.4
  70.3 4.8 %all-to-all-start.1 = ((bf16[64,128,128]{2,1,0:T(8,128)(2,1)}), bf16[64,128,128]{2,1,0:T(8,128)(2,1)S(1)}, u32[]{:S(2)}, u32[]{:S(2)}) async-start(bf16[64,128,128]{2,1,0:T(8,128)(2,1)} %copy-done.1), calls=%async_computation.1 | async-start | bytes 4194304 | tf_op jit(solution)/shard_map/all_to_all | solution.py:268
  75.2 0.1 convert_reduce_fusion
  75.3 0.1 copy.67
  75.4 0.1 reshape.98.count_ref
  75.6 0.1 reshape.97.code_ref
  75.6 25.3 %all-to-all-done.1.far_ref = bf16[64,128,128]{2,1,0:T(8,128)(2,1)S(1)} async-done(((bf16[64,128,128]{2,1,0:T(8,128)(2,1)}), bf16[64,128,128]{2,1,0:T(8,128)(2,1)S(1)}, u32[]{:S(2)}, u32[]{:S(2)}) %all-to-all-start.1) | async-done | bytes 2097184 | tf_op jit(solution)/shard_map/all_to_all | solution.py:268
  100.9 0.0 all-gather.2.cloned.1.call-done.near_ref
  100.9 0.0 copy-start.5
  100.9 1.1 copy-done.5
  102.1 69.5 %shard_map.95 = (bf16[24,128,128]{2,1,0:T(8,128)(2,1)S(1)}, bf16[96,128,128]{2,1,0:T(8,128)(2,1)}, bf16[64,128,128]{2,1,0:T(8,128)(2,1)S(1)}) custom-call(s32[384]{0:T(512)S(1)} %reshape.97.code_ref, s32[24]{0:T(128)S(1)} %reshape.98.count_ref, bf16[96,128,128]{2,1,0:T(8,128)(2,1)} %all-gather.2.cloned.1.call-done.near_ref, ...), custom_call_target="tpu_custom_call" | custom-call | tf_op jit(solution)/shard_map/pallas_call | solution.py:271
  171.5 0.0 copy-start.6
  171.5 0.0 copy-start.11
  171.6 44.3 %all_to_all.36.far_ref = bf16[64,128,128]{2,1,0:T(8,128)(2,1)} all-to-all(bf16[64,128,128]{2,1,0:T(8,128)(2,1)S(1)} %get-tuple-element.19), channel_id=1, replica_groups=mesh['grp'=8,'seq'=32] {'grp'}, dimensions={0} | all-to-all | bytes 4194304 | tf_op jit(solution)/shard_map/all_to_all | solution.py:292
  215.8 0.0 copy-done.11
  215.8 44.1 %all_to_all.37 = bf16[96,128,128]{2,1,0:T(8,128)(2,1)S(1)} all-to-all(bf16[96,128,128]{2,1,0:T(8,128)(2,1)S(1)} %copy-done.11), channel_id=1, replica_groups={{0,1,2,3},{4,5,6,7},{8,9,10,11},{12,13,14,15},{16,17,18,19},{20,21,22,2..., dimensions={0} | all-to-all | bytes 6291456 | tf_op jit(solution)/shard_map/all_to_all | solution.py:293
  259.9 0.0 copy-done.6
  259.9 4.2 %all-to-all-start.3 = ((bf16[8,3,128,128]{3,2,1,0:T(8,128)(2,1)}), bf16[8,3,128,128]{3,2,1,0:T(8,128)(2,1)}, u32[]{:S(2)}, u32[]{:S(2)}) async-start(bf16[8,3,128,128]{3,2,1,0:T(8,128)(2,1)} %bitcast.160), calls=%async_computation.3 | async-start | bytes 1572864 | tf_op jit(solution)/shard_map/all_to_all | solution.py:254
  264.1 0.0 copy-start
  264.1 1.6 copy-done
  265.7 2.5 shard_map.97
  268.2 0.0 copy-start.3
  268.2 0.9 copy-done.3
  269.1 16.6 %all-to-all-done.3.in_ref = bf16[8,3,128,128]{3,2,1,0:T(8,128)(2,1)} async-done(((bf16[8,3,128,128]{3,2,1,0:T(8,128)(2,1)}), bf16[8,3,128,128]{3,2,1,0:T(8,128)(2,1)}, u32[]{:S(2)}, u32[]{:S(2)}) %all-to-all-start.3) | async-done | bytes 786464 | tf_op jit(solution)/shard_map/all_to_all | solution.py:254
  285.7 3.5 %all-to-all-start.6 = ((bf16[8,3,128,128]{3,2,1,0:T(8,128)(2,1)}), bf16[8,3,128,128]{3,2,1,0:T(8,128)(2,1)S(1)}, u32[]{:S(2)}, u32[]{:S(2)}) async-start(bf16[8,3,128,128]{3,2,1,0:T(8,128)(2,1)} %bitcast.158), calls=%async_computation.6 | async-start | bytes 1572864 | tf_op jit(solution)/shard_map/all_to_all | solution.py:254
  289.3 2.3 shard_map.96
  291.5 18.9 %all-to-all-done.6.in_ref = bf16[8,3,128,128]{3,2,1,0:T(8,128)(2,1)S(1)} async-done(((bf16[8,3,128,128]{3,2,1,0:T(8,128)(2,1)}), bf16[8,3,128,128]{3,2,1,0:T(8,128)(2,1)S(1)}, u32[]{:S(2)}, u32[]{:S(2)}) %all-to-all-start.6) | async-done | bytes 786464 | tf_op jit(solution)/shard_map/all_to_all | solution.py:254
  310.4 1.1 shard_map.98
  (5 shorter events, 0.1 us)
Async XLA Ops:
  7.2 93.8 %all-gather.2.cloned.1.call-start = ((), (), s32[]{:S(2)}) async-start(), calls=%async_computation.7 | async-start | bytes 3932160 | tf_op jit(solution)/shard_map/all_gather | solution.py:260
  7.2 1.0 copy-start.7
  8.2 1.0 copy-start.8
  9.2 1.0 copy-start.9
  10.2 1.0 copy-start.10
  12.6 35.3 %copy-start.12 = (s32[768,16]{0,1:T(8,128)S(1)}, s32[768,16]{0,1:T(8,128)}, u32[]{:S(2)}) copy-start(s32[768,16]{0,1:T(8,128)} %param.10) | copy-start | bytes 147460
  12.6 35.5 %copy-start.13 = (s32[768,16]{0,1:T(8,128)S(1)}, s32[768,16]{0,1:T(8,128)}, u32[]{:S(2)}) copy-start(s32[768,16]{0,1:T(8,128)} %param.11) | copy-start | bytes 147460
  44.2 5.0 %copy-start.2 = (bf16[8,3,128,128]{3,2,1,0:T(8,128)(2,1)S(1)}, bf16[8,3,128,128]{3,2,1,0:T(8,128)(2,1)}, u32[]{:S(2)}) copy-start(bf16[8,3,128,128]{3,2,1,0:T(8,128)(2,1)} %all_to_all.35.kv_ref) | copy-start | bytes 2359300
  44.2 25.3 %all-to-all-start.2 = ((bf16[8,3,128,128]{3,2,1,0:T(8,128)(2,1)}), bf16[8,3,128,128]{3,2,1,0:T(8,128)(2,1)S(1)}, u32[]{:S(2)}, u32[]{:S(2)}) async-start(bf16[8,3,128,128]{3,2,1,0:T(8,128)(2,1)} %get-tuple-element.14), calls=%async_computation.2 | async-start | bytes 1572864 | tf_op jit(solution)/shard_map/all_to_all | solution.py:254
  50.3 1.4 copy-start.1
  69.4 0.9 copy-start.4
  70.3 30.6 %all-to-all-start.1 = ((bf16[64,128,128]{2,1,0:T(8,128)(2,1)}), bf16[64,128,128]{2,1,0:T(8,128)(2,1)S(1)}, u32[]{:S(2)}, u32[]{:S(2)}) async-start(bf16[64,128,128]{2,1,0:T(8,128)(2,1)} %copy-done.1), calls=%async_computation.1 | async-start | bytes 4194304 | tf_op jit(solution)/shard_map/all_to_all | solution.py:268
  100.9 1.1 copy-start.5
  171.5 88.4 %copy-start.6 = (bf16[24,128,128]{2,1,0:T(8,128)(2,1)}, bf16[24,128,128]{2,1,0:T(8,128)(2,1)S(1)}, u32[]{:S(2)}) copy-start(bf16[24,128,128]{2,1,0:T(8,128)(2,1)S(1)} %get-tuple-element.15) | copy-start | bytes 2359300
  171.5 44.3 %copy-start.11 = (bf16[96,128,128]{2,1,0:T(8,128)(2,1)S(1)}, bf16[96,128,128]{2,1,0:T(8,128)(2,1)}, u32[]{:S(2)}) copy-start(bf16[96,128,128]{2,1,0:T(8,128)(2,1)} %get-tuple-element.18) | copy-start | bytes 9437188
  259.9 25.8 %all-to-all-start.3 = ((bf16[8,3,128,128]{3,2,1,0:T(8,128)(2,1)}), bf16[8,3,128,128]{3,2,1,0:T(8,128)(2,1)}, u32[]{:S(2)}, u32[]{:S(2)}) async-start(bf16[8,3,128,128]{3,2,1,0:T(8,128)(2,1)} %bitcast.160), calls=%async_computation.3 | async-start | bytes 1572864 | tf_op jit(solution)/shard_map/all_to_all | solution.py:254
  264.1 1.6 copy-start
  268.2 0.9 copy-start.3
  285.7 24.7 %all-to-all-start.6 = ((bf16[8,3,128,128]{3,2,1,0:T(8,128)(2,1)}), bf16[8,3,128,128]{3,2,1,0:T(8,128)(2,1)S(1)}, u32[]{:S(2)}, u32[]{:S(2)}) async-start(bf16[8,3,128,128]{3,2,1,0:T(8,128)(2,1)} %bitcast.158), calls=%async_computation.6 | async-start | bytes 1572864 | tf_op jit(solution)/shard_map/all_to_all | solution.py:254
Sparse Core Ops, SparseCore 0:
  44.3 37.5 all-gather.1

commit v2 on v1

v2 whole, which is shorter than its diff:
```python
import functools

import jax
import jax.numpy as jnp
from jax import lax
from jax.experimental import pallas as pl
from jax.experimental.pallas import tpu as pltpu
from jax.sharding import PartitionSpec as P

HEADS = 8
HEAD_DIM = 64
Y_SIZE = 4
LOG2E = 1.4426950408889634
HIDDEN = -1e30


def pack_kernel(first_ref, second_ref, out_ref, first, second, packed, sems):
    copies = [
        pltpu.make_async_copy(first_ref, first, sems.at[0]),
        pltpu.make_async_copy(second_ref, second, sems.at[1]),
    ]
    for copy in copies:
        copy.start()
    for copy in copies:
        copy.wait()
    for head in range(HEADS):
        cols = slice(head * HEAD_DIM, (head + 1) * HEAD_DIM)
        packed[head] = jnp.concatenate([first[:, :, cols], second[:, :, cols]], axis=-1)
    copy = pltpu.make_async_copy(packed, out_ref, sems.at[2])
    copy.start()
    copy.wait()


def unpack_kernel(in_ref, first_ref, second_ref, packed, first, second, sems):
    copy = pltpu.make_async_copy(in_ref, packed, sems.at[2])
    copy.start()
    copy.wait()
    for pair in range(HEADS // 2):
        even = packed[2 * pair]
        odd = packed[2 * pair + 1]
        cols = slice(pair * 128, pair * 128 + 128)
        first[:, :, cols] = jnp.concatenate([even[..., :HEAD_DIM], odd[..., :HEAD_DIM]], axis=-1)
        second[:, :, cols] = jnp.concatenate([even[..., HEAD_DIM:], odd[..., HEAD_DIM:]], axis=-1)
    copies = [
        pltpu.make_async_copy(first, first_ref, sems.at[0]),
        pltpu.make_async_copy(second, second_ref, sems.at[1]),
    ]
    for copy in copies:
        copy.start()
    for copy in copies:
        copy.wait()


def far_kernel(rank_ref, kv_ref, out_ref, sem, *, far, zs, tile_dev):
    def step(at, carry):
        slot = (at % zs) * tile_dev + jnp.maximum(rank_ref[at], 0)
        pltpu.make_async_copy(kv_ref.at[slot], out_ref.at[at], sem).start()
        return carry

    lax.fori_loop(0, far, step, 0, unroll=4)
    pltpu.make_async_copy(out_ref, out_ref, sem).wait()


def attend_kernel(*refs, tiles, entries, ys, far):
    code_ref, count_ref = refs[:2]
    kv_refs = refs[2 : 3 + ys]
    qg_ref = refs[3 + ys]
    odq_ref = refs[4 + ys]
    dkv_refs = refs[5 + ys : 6 + 2 * ys]
    table, totals, scores, dprobs, masks, qg_tiles, sems = refs[6 + 2 * ys :]
    spans = [(at * tiles, tiles) for at in range(ys)] + [(ys * tiles, far)]
    slots_all = ys * tiles + far
    copies = [
        pltpu.make_async_copy(ref, table.at[pl.ds(*span)], sems.at[at])
        for at, (ref, span) in enumerate(zip(kv_refs, spans))
    ]
    copies.append(pltpu.make_async_copy(qg_ref, qg_tiles, sems.at[ys + 1]))
    for copy in copies:
        copy.start()
    rows = 128
    key_at = lax.broadcasted_iota(jnp.int32, (rows, rows), 0)
    query_at = lax.broadcasted_iota(jnp.int32, (rows, rows), 1)
    masks[0] = jnp.zeros((rows, rows), jnp.float32)
    masks[1] = jnp.where(key_at <= query_at, 0.0, HIDDEN).astype(jnp.float32)
    masks[2] = jnp.full((rows, rows), HIDDEN, jnp.float32)
    table[slots_all] = jnp.zeros((rows, rows), table.dtype)

    def clear(at, carry):
        totals[at] = jnp.zeros((rows, rows), jnp.float32)
        return carry

    lax.fori_loop(0, slots_all + 1, clear, 0, unroll=7)
    for copy in copies:
        copy.wait()
    left = query_at < HEAD_DIM
    scale = HEAD_DIM ** -0.5
    group = 4

    def fold(block, op):
        return op(block.reshape(rows // 8, 8, rows), axis=0)

    def one_tile(tile, size):
        qg = qg_tiles[tile]
        none = jnp.zeros_like(qg)
        weights = jnp.concatenate([jnp.where(left, qg, none), jnp.where(left, none, qg)], axis=0)
        codes = [code_ref[tile * entries + entry] for entry in range(size)]
        slots = [code // 4 for code in codes]
        top = jnp.full((8, rows), HIDDEN, jnp.float32)
        for start in range(0, size, group):
            kv = jnp.concatenate([table[slot] for slot in slots[start : start + group]], axis=0)
            both = lax.dot_general(
                kv, weights, (((1,), (1,)), ((), ())), preferred_element_type=jnp.float32
            )
            for at in range(group):
                entry = start + at
                part = both[at * rows : (at + 1) * rows]
                masked = part[:, :rows] + masks[codes[entry] % 4]
                scores[entry] = masked
                dprobs[entry] = part[:, rows:]
                top = jnp.maximum(top, fold(masked, jnp.max))
        row_top = jnp.max(top, axis=0, keepdims=True)
        total = jnp.zeros((8, rows), jnp.float32)
        mixed = total
        for entry in range(size):
            prob = jnp.exp2((scores[entry] - row_top) * (scale * LOG2E))
            scores[entry] = prob
            total = total + fold(prob, jnp.sum)
            mixed = mixed + fold(prob * dprobs[entry], jnp.sum)
        inverse = 1.0 / jnp.sum(total, axis=0, keepdims=True)
        delta = jnp.sum(mixed, axis=0, keepdims=True) * inverse
        attended = jnp.zeros((HEAD_DIM, rows), jnp.float32)
        grad_query = attended
        for start in range(0, size, group):
            parts = []
            for entry in range(start, start + group):
                prob = scores[entry] * inverse
                dscore = prob * (dprobs[entry] - delta)
                parts.append(jnp.concatenate([dscore, prob], axis=1).astype(jnp.bfloat16))
            both = jnp.concatenate(parts, axis=0)
            chosen = slots[start : start + group]
            added = jnp.dot(both, weights, preferred_element_type=jnp.float32)
            before = [totals[slot] for slot in chosen]
            for at in range(group):
                totals[chosen[at]] = before[at] + added[at * rows : (at + 1) * rows]
            kv = jnp.concatenate([table[slot] for slot in chosen], axis=0)
            back = lax.dot_general(
                kv, both, (((0,), (0,)), ((), ())), preferred_element_type=jnp.float32
            )
            attended = attended + back[HEAD_DIM:, rows:]
            grad_query = grad_query + back[:HEAD_DIM, :rows]
        joined = jnp.concatenate([attended, grad_query * scale], axis=0)
        qg_tiles[tile] = joined.T.astype(qg_tiles.dtype)

    def tile_step(tile, carry):
        count = count_ref[tile]
        for size in range(group, entries + 1, group):

            @pl.when((count > size - group) & (count <= size))
            def _():
                one_tile(tile, size)

        return carry

    lax.fori_loop(0, tiles, tile_step, 0)
    copies = [pltpu.make_async_copy(qg_tiles, odq_ref, sems.at[ys + 1])]
    copies[0].start()
    scales = jnp.where(left, scale, 1.0).astype(jnp.float32)

    def write(at, carry):
        table[at] = (totals[at] * scales).astype(table.dtype)
        return carry

    for at in (ys, *range(ys)):
        first, size = spans[at]
        lax.fori_loop(first, first + size, write, 0, unroll=4)
        copies.append(pltpu.make_async_copy(table.at[pl.ds(first, size)], dkv_refs[at], sems.at[at]))
        copies[-1].start()
    for copy in copies:
        copy.wait()


def combine_kernel(*refs, ys, far, zs, tile_dev):
    rank_ref = refs[0]
    near_refs = refs[1 : 1 + ys]
    far_ref, out_ref, near, far_tiles, sums, sems = refs[1 + ys :]
    tiles = zs * tile_dev
    copies = [
        pltpu.make_async_copy(ref, near.at[at], sems.at[at]) for at, ref in enumerate(near_refs)
    ]
    copies.append(pltpu.make_async_copy(far_ref, far_tiles, sems.at[ys]))
    for copy in copies:
        copy.start()
    for copy in copies:
        copy.wait()

    def add_near(at, carry):
        total = near[0, at].astype(jnp.float32)
        for y in range(1, ys):
            total = total + near[y, at].astype(jnp.float32)
        sums[at] = total
        return carry

    lax.fori_loop(0, tiles, add_near, 0, unroll=2)

    def add_far(at, carry):
        rank = rank_ref[at]

        @pl.when(rank >= 0)
        def _():
            slot = (at % zs) * tile_dev + rank
            sums[slot] = sums[slot] + far_tiles[at].astype(jnp.float32)

        return carry

    lax.fori_loop(0, far, add_far, 0)

    def write(at, carry):
        near[0, at] = sums[at].astype(near.dtype)
        return carry

    lax.fori_loop(0, tiles, write, 0, unroll=4)
    copy = pltpu.make_async_copy(near.at[0], out_ref, sems.at[0])
    copy.start()
    copy.wait()


def pin(source):
    return pltpu.with_memory_space_constraint(source, pltpu.HBM)


def limits(size):
    return pltpu.CompilerParams(vmem_limit_bytes=size << 20)


def hbm(count):
    return [pl.BlockSpec(memory_space=pl.ANY) for _ in range(count)]


def smem(count):
    return [pl.BlockSpec(memory_space=pltpu.SMEM) for _ in range(count)]


def per_device(queries, key_input, value_input, grad_output, block_lists, block_flags):
    tile_dev = queries.shape[1]
    rows = queries.shape[3]
    width = queries.shape[4]
    entries = block_lists.shape[1]
    columns = lax.axis_size("seq")
    groups = lax.axis_size("grp")
    ys = Y_SIZE
    zs = columns // ys
    group_at = lax.axis_index("grp")
    y_at = lax.axis_index("seq") % ys
    group_tiles = tile_dev * columns
    z_groups = [[z * ys + y for z in range(zs)] for y in range(ys)]
    bf16 = jnp.bfloat16
    near = group_tiles
    far = groups * zs
    tiles = zs * tile_dev

    lists = block_lists.reshape(groups, tile_dev, zs, ys, entries)
    flags = block_flags.reshape(groups, tile_dev, zs, ys, entries)
    lists = lax.dynamic_index_in_dim(lists, y_at, 3, keepdims=False)
    flags = lax.dynamic_index_in_dim(flags, y_at, 3, keepdims=False)
    present = lists >= 0
    safe = jnp.maximum(lists, 0)
    to_group = safe // group_tiles
    within = safe % group_tiles
    to_rank = within // columns
    to_column = within % columns
    z_ids = jnp.arange(zs, dtype=jnp.int32)[None, None, :, None]
    group_ids = jnp.arange(groups, dtype=jnp.int32)
    named = present & (to_group == group_at) & (to_column == z_ids * ys + y_at)
    far_rank = jnp.max(jnp.where(named, to_rank, -1), axis=(1, 3))
    far_rank = jnp.where(group_ids[:, None] == group_at, -1, far_rank).reshape(far)
    near_slot = ((to_column - y_at) % ys) * tiles + (to_column // ys) * tile_dev + to_rank
    far_slot = near + to_group * zs + z_ids
    slot = jnp.where(to_group == group_at, near_slot, far_slot)
    slot = jnp.where(present, slot, near + far)
    mask_at = jnp.where(present, jnp.where(flags != 0, 1, 0), 2)
    code = lax.dynamic_index_in_dim(slot * 4 + mask_at, group_at, 0, keepdims=False)
    code = jnp.transpose(code, (1, 0, 2)).reshape(tiles * entries)
    count = lax.dynamic_index_in_dim(present, group_at, 0, keepdims=False).astype(jnp.int32)
    count = jnp.transpose(jnp.sum(count, axis=2), (1, 0)).reshape(tiles)

    def shape_of(*shape):
        return pltpu.HBM(shape, bf16)

    head_shape = shape_of(HEADS, tile_dev, rows, 128)
    tile_shape = shape_of(tile_dev, rows, width)
    block_shape = shape_of(tiles, rows, 128)
    far_shape = shape_of(far, rows, 128)

    def scratch(shape, dtype=bf16):
        return pltpu.VMEM(shape.shape, dtype)

    def pack(first, second):
        return pl.pallas_call(
            pack_kernel,
            out_shape=head_shape,
            in_specs=hbm(2),
            out_specs=hbm(1)[0],
            scratch_shapes=[scratch(tile_shape), scratch(tile_shape), scratch(head_shape), pltpu.SemaphoreType.DMA((3,))],
            compiler_params=limits(16),
        )(pin(first.reshape(tile_shape.shape)), pin(second.reshape(tile_shape.shape)))

    def unpack(joined):
        first, second = pl.pallas_call(
            unpack_kernel,
            out_shape=(tile_shape, tile_shape),
            in_specs=hbm(1),
            out_specs=hbm(2),
            scratch_shapes=[scratch(head_shape), scratch(tile_shape), scratch(tile_shape), pltpu.SemaphoreType.DMA((3,))],
            compiler_params=limits(16),
        )(joined.reshape(head_shape.shape))
        return (
            first.reshape(1, tile_dev, 1, rows, width),
            second.reshape(1, tile_dev, 1, rows, width),
        )

    def over_z(source):
        return lax.all_to_all(
            source.reshape(head_shape.shape),
            "seq",
            split_axis=0,
            concat_axis=0,
            tiled=True,
            axis_index_groups=z_groups,
        ).reshape(block_shape.shape)

    def over_groups(source):
        return lax.all_to_all(source, "grp", split_axis=0, concat_axis=0, tiled=True)

    def over_y(source, shift):
        pairs = [(z * ys + y, z * ys + (y + shift) % ys) for z in range(zs) for y in range(ys)]
        return lax.ppermute(source, "seq", pairs)

    def after(source, *others):
        return lax.optimization_barrier((source, *others))

    kv = over_z(pack(key_input, value_input))
    send_qg = pack(queries, grad_output)
    near_kv = [kv] + [over_y(kv, -shift) for shift in range(1, ys)]
    far_send = pl.pallas_call(
        functools.partial(far_kernel, far=far, zs=zs, tile_dev=tile_dev),
        out_shape=far_shape,
        in_specs=smem(1) + hbm(1),
        out_specs=hbm(1)[0],
        scratch_shapes=[pltpu.SemaphoreType.DMA],
        compiler_params=limits(8),
    )(far_rank, kv)
    far_kv = over_groups(far_send)
    send_qg, far_kv, near_kv[1], near_kv[-1] = after(send_qg, far_kv, near_kv[1], near_kv[-1])
    qg = over_z(send_qg)

    slots = near + far + 1
    odq, *dkv_parts = pl.pallas_call(
        functools.partial(attend_kernel, tiles=tiles, entries=entries, ys=ys, far=far),
        out_shape=(block_shape,) * (ys + 1) + (far_shape,),
        in_specs=smem(2) + hbm(ys + 2),
        out_specs=hbm(ys + 2),
        scratch_shapes=[
            pltpu.VMEM((slots, rows, 128), bf16),
            pltpu.VMEM((slots, rows, 128), jnp.float32),
            pltpu.VMEM((entries, rows, rows), jnp.float32),
            pltpu.VMEM((entries, rows, rows), jnp.float32),
            pltpu.VMEM((3, rows, rows), jnp.float32),
            scratch(block_shape),
            pltpu.SemaphoreType.DMA((ys + 2,)),
        ],
        compiler_params=limits(40),
    )(code, count, kv, *map(pin, near_kv[1:]), pin(far_kv), qg)

    near_back = [dkv_parts[0]] + [over_y(dkv_parts[shift], shift) for shift in range(1, ys)]
    far_back = over_groups(dkv_parts[ys])
    odq, far_back, near_back[1], near_back[-1] = after(odq, far_back, near_back[1], near_back[-1])
    odq_back = over_z(odq)
    dkv = pl.pallas_call(
        functools.partial(combine_kernel, ys=ys, far=far, zs=zs, tile_dev=tile_dev),
        out_shape=block_shape,
        in_specs=smem(1) + hbm(ys + 1),
        out_specs=hbm(1)[0],
        scratch_shapes=[
            pltpu.VMEM((ys, tiles, rows, 128), bf16),
            scratch(far_shape),
            scratch(block_shape, jnp.float32),
            pltpu.SemaphoreType.DMA((ys + 1,)),
        ],
        compiler_params=limits(24),
    )(far_rank, *map(pin, near_back), pin(far_back))
    attended, grad_queries = unpack(odq_back)
    grad_keys, grad_values = unpack(over_z(dkv))
    return attended, grad_queries, grad_keys, grad_values


def solution(mesh):
    spec = P("grp", None, "seq", None, None)
    return jax.shard_map(
        per_device,
        mesh=mesh,
        in_specs=(spec, spec, spec, spec, P(), P()),
        out_specs=(spec, spec, spec, spec),
        check_vma=False,
    )
```

time: 319 us -> 224 us (0.70)
  blocking collectives: 120 us -> 0 us
  waiting for transfers between devices: 78.5 us -> 124 us
  Pallas kernels: 77.9 us -> 50.2 us
  starting transfers between devices: 16.3 us -> 43.4 us
  between operations: 14.2 us -> 0.82 us
  local copies, waits for them, and re-layouts: 10.7 us -> 1.78 us
    all_to_all x3 -> x0, blocking collectives: 120 us -> none  [the longest x1 44.3 us: per_device(): lax.all_to_all(dfar, 'grp', split_axis=0, concat_axis=0, tiled=True)]
    ppermute x0 -> x6, waiting for transfers between devices: none -> 69.5 us  [over_y(): return lax.ppermute(source, 'seq', pairs)]
    pallas_call x1, Pallas kernels: 69.5 us -> 35.5 us  [per_device(): pl.pallas_call(functools.partial(attend_kernel, tiles=tiles, entries=entr...]
    all_to_all x4 -> x6, waiting for transfers between devices: 78.5 us -> 54.3 us  [the longest x4 43.9 us: over_z(): lax.all_to_all(source.reshape(head_shape.shape), 'seq', split_axis=0, con...]
    all_to_all x4 -> x6, starting transfers between devices: 16.3 us -> 34.6 us  [the longest x4 23.3 us: over_z(): lax.all_to_all(source.reshape(head_shape.shape), 'seq', split_axis=0, con...]
    unnamed x30 -> x20, local copies, waits for them, and re-layouts: 10.2 us -> 1.24 us
    ppermute x0 -> x6, starting transfers between devices: none -> 8.79 us  [over_y(): return lax.ppermute(source, 'seq', pairs)]
    pallas_call x5 -> x6, Pallas kernels: 8.42 us -> 14.7 us  [the longest x1 5.86 us: per_device(): pl.pallas_call(functools.partial(combine_kernel, ys=ys, far=far, zs=zs, t...]
  transfers between devices with their start and end apart: 5 -> 12, of which waited for: 4 -> 11; matrix products, arithmetic and copies ran while one was open for 0% -> 2% of each run, Pallas kernels for 2% -> 4%
where the time goes in v2:
time: 224 us; the launch traced here: 223 us
  waiting for transfers between devices  124 us (55%)
  Pallas kernels  50.2 us (22%)
  starting transfers between devices  43.4 us (19%)
  other arithmetic  2.66 us (1%)
    ppermute x6, waiting for transfers between devices, over_y(): return lax.ppermute(source, 'seq', pairs)  69.5 us
    all_to_all x4, waiting for transfers between devices, over_z(): lax.all_to_all(source.reshape(head_shape.shape), 'seq', split_axis=0, con...  43.9 us
    pallas_call x1, Pallas kernels, per_device(): pl.pallas_call(functools.partial(attend_kernel, tiles=tiles, entries=entr...  35.5 us
    all_to_all x4, starting transfers between devices, over_z(): lax.all_to_all(source.reshape(head_shape.shape), 'seq', split_axis=0, con...  23.3 us
    all_to_all x2, starting transfers between devices, over_groups(): lax.all_to_all(source, 'grp', split_axis=0, concat_axis=0, tiled=True)  11.3 us
    all_to_all x2, waiting for transfers between devices, over_groups(): lax.all_to_all(source, 'grp', split_axis=0, concat_axis=0, tiled=True)  10.4 us
    ppermute x6, starting transfers between devices, over_y(): return lax.ppermute(source, 'seq', pairs)  8.79 us
    pallas_call x1, Pallas kernels, per_device(): pl.pallas_call(functools.partial(combine_kernel, ys=ys, far=far, zs=zs, t...  5.86 us
  transfers between devices with their start and end apart: 12, of which 11 were waited for; matrix products, arithmetic and copies ran while one was open for 2% of the time, Pallas kernels for 4%

profile of v2, /device:TPU:10, one launch (start us, length us, event | category | flops | bytes accessed | tf_op | source)
XLA Modules:
  0.0 222.6 jit_solution(11334477569208203903)
XLA Ops:
  0.6 0.0 copy-start.5
  0.6 0.0 copy-start.6
  0.7 2.3 %shard_map.93 = bf16[8,3,128,128]{3,2,1,0:T(8,128)(2,1)} custom-call(bf16[3,128,512]{2,1,0:T(8,128)(2,1)} %bitcast.167, bf16[3,128,512]{2,1,0:T(8,128)(2,1)} %bitcast.168), custom_call_target="tpu_custom_call" | custom-call | tf_op jit(solution)/shard_map/pallas_call | solution.py:298
  3.0 8.5 %all-to-all-start = ((bf16[8,3,128,128]{3,2,1,0:T(8,128)(2,1)}), bf16[8,3,128,128]{3,2,1,0:T(8,128)(2,1)S(1)}, u32[]{:S(2)}, u32[]{:S(2)}) async-start(bf16[8,3,128,128]{3,2,1,0:T(8,128)(2,1)} %shard_map.93), calls=%async_computation | async-start | bytes 1572864 | tf_op jit(solution)/shard_map/all_to_all | solution.py:322
  11.5 0.0 copy-done.5
  11.5 0.2 copy.57
  11.6 0.0 copy-done.6
  11.6 0.2 copy.64
  11.8 0.2 constant_dynamic-slice_fusion
  12.1 1.0 fusion.1
  13.1 0.1 broadcast_select_fusion
  13.1 0.1 select_n.88.rank_ref.refs_0_
  13.2 21.4 %all-to-all-done = bf16[8,3,128,128]{3,2,1,0:T(8,128)(2,1)S(1)} async-done(((bf16[8,3,128,128]{3,2,1,0:T(8,128)(2,1)}), bf16[8,3,128,128]{3,2,1,0:T(8,128)(2,1)S(1)}, u32[]{:S(2)}, u32[]{:S(2)}) %all-to-all-start) | async-done | bytes 786464 | tf_op jit(solution)/shard_map/all_to_all | solution.py:322
  34.6 1.9 shard_map.95
  36.4 4.8 %all-to-all-start.1 = ((bf16[64,128,128]{2,1,0:T(8,128)(2,1)}), bf16[64,128,128]{2,1,0:T(8,128)(2,1)}, u32[]{:S(2)}, u32[]{:S(2)}) async-start(bf16[64,128,128]{2,1,0:T(8,128)(2,1)} %shard_map.95), calls=%async_computation.1 | async-start | bytes 4194304 | tf_op jit(solution)/shard_map/all_to_all | solution.py:332
  41.3 1.6 collective-permute-start.1
  42.9 0.4 collective-permute-start
  43.3 2.3 %shard_map.94 = bf16[8,3,128,128]{3,2,1,0:T(8,128)(2,1)} custom-call(bf16[3,128,512]{2,1,0:T(8,128)(2,1)} %bitcast.169, bf16[3,128,512]{2,1,0:T(8,128)(2,1)} %bitcast.170), custom_call_target="tpu_custom_call" | custom-call | tf_op jit(solution)/shard_map/pallas_call | solution.py:298
  45.6 15.3 %collective-permute-done.1.refs_5_ = bf16[24,128,128]{2,1,0:T(8,128)(2,1)S(1)} collective-permute-done((bf16[24,128,128]{2,1,0:T(8,128)(2,1)S(1)}, bf16[24,128,128]{2,1,0:T(8,128)(2,1)S(1)}, u32[]{:S(2)}, u32[]{:S(2)}) %collective-permute-start.1) | collective-permute-done | bytes 786464 | tf_op jit(solution)/shard_map/ppermute | solution.py:336
  60.9 0.0 copy-start.3
  60.9 1.3 collective-permute-done.refs_3_
  62.2 0.0 copy-start.4
  62.2 5.0 %all-to-all-done.1.refs_6_ = bf16[64,128,128]{2,1,0:T(8,128)(2,1)} async-done(((bf16[64,128,128]{2,1,0:T(8,128)(2,1)}), bf16[64,128,128]{2,1,0:T(8,128)(2,1)}, u32[]{:S(2)}, u32[]{:S(2)}) %all-to-all-start.1) | async-done | bytes 2097184 | tf_op jit(solution)/shard_map/all_to_all | solution.py:332
  67.1 3.5 %all-to-all-start.2 = ((bf16[8,3,128,128]{3,2,1,0:T(8,128)(2,1)}), bf16[8,3,128,128]{3,2,1,0:T(8,128)(2,1)S(1)}, u32[]{:S(2)}, u32[]{:S(2)}) async-start(bf16[8,3,128,128]{3,2,1,0:T(8,128)(2,1)} %shard_map.94), calls=%async_computation.2 | async-start | bytes 1572864 | tf_op jit(solution)/shard_map/all_to_all | solution.py:322
  70.7 2.4 %collective-permute-start.2 = (bf16[24,128,128]{2,1,0:T(8,128)(2,1)S(1)}, bf16[24,128,128]{2,1,0:T(8,128)(2,1)}, u32[]{:S(2)}, u32[]{:S(2)}) collective-permute-start(bf16[24,128,128]{2,1,0:T(8,128)(2,1)S(1)} %bitcast.158), channel_id=1, source_target_pairs={{0,2},{1,3},{2,0},{3,1},{4,6},{5,7},{6,4},{7,5},{8,10},{9,11},{10,... | collective-permute-start | bytes 2359304 | tf_op jit(solution)/shard_map/ppermute | solution.py:336
  73.1 0.8 convert_reduce_fusion
  73.9 0.1 copy.67
  74.0 0.1 reshape.95.refs_1_
  74.1 0.7 fusion.12
  74.8 0.1 reshape.94.refs_0_
  74.9 16.5 %collective-permute-done.2.refs_4_ = bf16[24,128,128]{2,1,0:T(8,128)(2,1)} collective-permute-done((bf16[24,128,128]{2,1,0:T(8,128)(2,1)S(1)}, bf16[24,128,128]{2,1,0:T(8,128)(2,1)}, u32[]{:S(2)}, u32[]{:S(2)}) %collective-permute-start.2) | collective-permute-done | bytes 786464 | tf_op jit(solution)/shard_map/ppermute | solution.py:336
  91.5 2.3 %all-to-all-done.2 = bf16[8,3,128,128]{3,2,1,0:T(8,128)(2,1)S(1)} async-done(((bf16[8,3,128,128]{3,2,1,0:T(8,128)(2,1)}), bf16[8,3,128,128]{3,2,1,0:T(8,128)(2,1)S(1)}, u32[]{:S(2)}, u32[]{:S(2)}) %all-to-all-start.2) | async-done | bytes 786464 | tf_op jit(solution)/shard_map/all_to_all | solution.py:322
  93.8 0.0 copy-done.3
  93.8 0.0 copy-done.4
  93.8 35.5 %shard_map.96 = (bf16[24,128,128]{2,1,0:T(8,128)(2,1)}, bf16[24,128,128]{2,1,0:T(8,128)(2,1)}, bf16[24,128,128]{2,1,0:T(8,128)(2,1)}, bf16[24,128,128]{2,1,0:T(8...) custom-call(s32[384]{0:T(512)S(1)} %reshape.94.refs_0_, s32[24]{0:T(128)S(1)} %reshape.95.refs_1_, ...), custom_call_target="tpu_custom_call" | custom-call | tf_op jit(solution)/shard_map/pallas_call | solution.py:357
  129.3 0.0 copy-start.8
  129.3 0.0 copy-start.7
  129.3 6.4 %all-to-all-start.3 = ((bf16[64,128,128]{2,1,0:T(8,128)(2,1)}), bf16[64,128,128]{2,1,0:T(8,128)(2,1)}, u32[]{:S(2)}, u32[]{:S(2)}) async-start(bf16[64,128,128]{2,1,0:T(8,128)(2,1)} %get-tuple-element.27), calls=%async_computation.3 | async-start | bytes 4194304 | tf_op jit(solution)/shard_map/all_to_all | solution.py:332
  135.7 1.0 collective-permute-start.3
  136.7 0.0 copy-done.8
  136.7 1.1 collective-permute-start.4
  137.8 17.8 %collective-permute-done.3.refs_2_ = bf16[24,128,128]{2,1,0:T(8,128)(2,1)S(1)} collective-permute-done((bf16[24,128,128]{2,1,0:T(8,128)(2,1)}, bf16[24,128,128]{2,1,0:T(8,128)(2,1)S(1)}, u32[]{:S(2)}, u32[]{:S(2)}) %collective-permute-start.3) | collective-permute-done | bytes 786464 | tf_op jit(solution)/shard_map/ppermute | solution.py:336
  155.5 0.0 copy-start
  155.5 0.6 collective-permute-done.4.refs_4_
  156.2 0.0 copy-start.1
  156.2 5.4 %all-to-all-done.3.refs_5_ = bf16[64,128,128]{2,1,0:T(8,128)(2,1)} async-done(((bf16[64,128,128]{2,1,0:T(8,128)(2,1)}), bf16[64,128,128]{2,1,0:T(8,128)(2,1)}, u32[]{:S(2)}, u32[]{:S(2)}) %all-to-all-start.3) | async-done | bytes 2097184 | tf_op jit(solution)/shard_map/all_to_all | solution.py:332
  161.6 4.4 %all-to-all-start.4 = ((bf16[8,3,128,128]{3,2,1,0:T(8,128)(2,1)}), bf16[8,3,128,128]{3,2,1,0:T(8,128)(2,1)S(1)}, u32[]{:S(2)}, u32[]{:S(2)}) async-start(bf16[8,3,128,128]{3,2,1,0:T(8,128)(2,1)} %bitcast.20), calls=%async_computation.4 | async-start | bytes 1572864 | tf_op jit(solution)/shard_map/all_to_all | solution.py:322
  166.0 0.0 copy-done.7
  166.0 2.4 %collective-permute-start.5 = (bf16[24,128,128]{2,1,0:T(8,128)(2,1)S(1)}, bf16[24,128,128]{2,1,0:T(8,128)(2,1)S(1)}, u32[]{:S(2)}, u32[]{:S(2)}) collective-permute-start(bf16[24,128,128]{2,1,0:T(8,128)(2,1)S(1)} %copy-done.7), channel_id=1, source_target_pairs={{0,2},{1,3},{2,0},{3,1},{4,6},{5,7},{6,4},{7,5},{8,10},{9,11},{10,... | collective-permute-start | bytes 2359304 | tf_op jit(solution)/shard_map/ppermute | solution.py:336
  168.4 18.0 %collective-permute-done.5.refs_3_ = bf16[24,128,128]{2,1,0:T(8,128)(2,1)S(1)} collective-permute-done((bf16[24,128,128]{2,1,0:T(8,128)(2,1)S(1)}, bf16[24,128,128]{2,1,0:T(8,128)(2,1)S(1)}, u32[]{:S(2)}, u32[]{:S(2)}) %collective-permute-start.5) | collective-permute-done | bytes 786464 | tf_op jit(solution)/shard_map/ppermute | solution.py:336
  186.4 0.0 copy-start.2
  186.4 0.0 copy-done
  186.4 0.0 copy-done.1
  186.4 0.9 copy-done.2
  187.3 5.9 %shard_map.98 = bf16[24,128,128]{2,1,0:T(8,128)(2,1)} custom-call(s32[64]{0:T(128)S(1)} %select_n.88.rank_ref.refs_0_, bf16[24,128,128]{2,1,0:T(8,128)(2,1)} %get-tuple-element.33.refs_1_, bf16[24,128,128]{2,1,0:T(8,128)(2,1)} %copy-done, bf16[24,128,128]{2,1,0:T(8,128)(2,1)} %copy-done.2, bf16[24,128,128]{2,1,0:T(8,128)(2,1)} %copy-done.1, ...), custom_call_target="tpu_custom_call" | custom-call | tf_op jit(solution)/shard_map/pallas_call | solution.py:378
  193.2 0.0 all-to-all-done.4.in_ref
  193.2 6.8 %all-to-all-start.5 = ((bf16[8,3,128,128]{3,2,1,0:T(8,128)(2,1)}), bf16[8,3,128,128]{3,2,1,0:T(8,128)(2,1)S(1)}, u32[]{:S(2)}, u32[]{:S(2)}) async-start(bf16[8,3,128,128]{3,2,1,0:T(8,128)(2,1)} %bitcast.161), calls=%async_computation.5 | async-start | bytes 1572864 | tf_op jit(solution)/shard_map/all_to_all | solution.py:322
  200.1 1.2 shard_map.97
  201.3 20.2 %all-to-all-done.5.in_ref = bf16[8,3,128,128]{3,2,1,0:T(8,128)(2,1)S(1)} async-done(((bf16[8,3,128,128]{3,2,1,0:T(8,128)(2,1)}), bf16[8,3,128,128]{3,2,1,0:T(8,128)(2,1)S(1)}, u32[]{:S(2)}, u32[]{:S(2)}) %all-to-all-start.5) | async-done | bytes 786464 | tf_op jit(solution)/shard_map/all_to_all | solution.py:322
  221.4 1.2 shard_map.99
  (4 shorter events, 0.0 us)
Async XLA Ops:
  0.6 10.8 %copy-start.5 = (s32[768,16]{0,1:T(8,128)S(1)}, s32[768,16]{0,1:T(8,128)}, u32[]{:S(2)}) copy-start(s32[768,16]{0,1:T(8,128)} %param.10) | copy-start | bytes 147460
  0.6 11.0 %copy-start.6 = (s32[768,16]{0,1:T(8,128)S(1)}, s32[768,16]{0,1:T(8,128)}, u32[]{:S(2)}) copy-start(s32[768,16]{0,1:T(8,128)} %param.11) | copy-start | bytes 147460
  3.0 31.6 %all-to-all-start = ((bf16[8,3,128,128]{3,2,1,0:T(8,128)(2,1)}), bf16[8,3,128,128]{3,2,1,0:T(8,128)(2,1)S(1)}, u32[]{:S(2)}, u32[]{:S(2)}) async-start(bf16[8,3,128,128]{3,2,1,0:T(8,128)(2,1)} %shard_map.93), calls=%async_computation | async-start | bytes 1572864 | tf_op jit(solution)/shard_map/all_to_all | solution.py:322
  36.4 30.7 %all-to-all-start.1 = ((bf16[64,128,128]{2,1,0:T(8,128)(2,1)}), bf16[64,128,128]{2,1,0:T(8,128)(2,1)}, u32[]{:S(2)}, u32[]{:S(2)}) async-start(bf16[64,128,128]{2,1,0:T(8,128)(2,1)} %shard_map.95), calls=%async_computation.1 | async-start | bytes 4194304 | tf_op jit(solution)/shard_map/all_to_all | solution.py:332
  41.3 19.6 %collective-permute-start.1 = (bf16[24,128,128]{2,1,0:T(8,128)(2,1)S(1)}, bf16[24,128,128]{2,1,0:T(8,128)(2,1)S(1)}, u32[]{:S(2)}, u32[]{:S(2)}) collective-permute-start(bf16[24,128,128]{2,1,0:T(8,128)(2,1)S(1)} %bitcast.156), channel_id=1, source_target_pairs={{0,1},{1,2},{2,3},{3,0},{4,5},{5,6},{6,7},{7,4},{8,9},{9,10},{10,1... | collective-permute-start | bytes 2359304 | tf_op jit(solution)/shard_map/ppermute | solution.py:336
  42.9 19.3 %collective-permute-start = (bf16[24,128,128]{2,1,0:T(8,128)(2,1)S(1)}, bf16[24,128,128]{2,1,0:T(8,128)(2,1)S(1)}, u32[]{:S(2)}, u32[]{:S(2)}) collective-permute-start(bf16[24,128,128]{2,1,0:T(8,128)(2,1)S(1)} %bitcast.157), channel_id=1, source_target_pairs={{0,3},{1,0},{2,1},{3,2},{4,7},{5,4},{6,5},{7,6},{8,11},{9,8},{10,9... | collective-permute-start | bytes 2359304 | tf_op jit(solution)/shard_map/ppermute | solution.py:336
  60.9 32.9 %copy-start.3 = (bf16[24,128,128]{2,1,0:T(8,128)(2,1)}, bf16[24,128,128]{2,1,0:T(8,128)(2,1)S(1)}, u32[]{:S(2)}) copy-start(bf16[24,128,128]{2,1,0:T(8,128)(2,1)S(1)} %collective-permute-done.1.refs_5_) | copy-start | bytes 2359300
  62.2 31.6 %copy-start.4 = (bf16[24,128,128]{2,1,0:T(8,128)(2,1)}, bf16[24,128,128]{2,1,0:T(8,128)(2,1)S(1)}, u32[]{:S(2)}) copy-start(bf16[24,128,128]{2,1,0:T(8,128)(2,1)S(1)} %collective-permute-done.refs_3_) | copy-start | bytes 2359300
  67.1 26.7 %all-to-all-start.2 = ((bf16[8,3,128,128]{3,2,1,0:T(8,128)(2,1)}), bf16[8,3,128,128]{3,2,1,0:T(8,128)(2,1)S(1)}, u32[]{:S(2)}, u32[]{:S(2)}) async-start(bf16[8,3,128,128]{3,2,1,0:T(8,128)(2,1)} %shard_map.94), calls=%async_computation.2 | async-start | bytes 1572864 | tf_op jit(solution)/shard_map/all_to_all | solution.py:322
  70.7 20.8 %collective-permute-start.2 = (bf16[24,128,128]{2,1,0:T(8,128)(2,1)S(1)}, bf16[24,128,128]{2,1,0:T(8,128)(2,1)}, u32[]{:S(2)}, u32[]{:S(2)}) collective-permute-start(bf16[24,128,128]{2,1,0:T(8,128)(2,1)S(1)} %bitcast.158), channel_id=1, source_target_pairs={{0,2},{1,3},{2,0},{3,1},{4,6},{5,7},{6,4},{7,5},{8,10},{9,11},{10,... | collective-permute-start | bytes 2359304 | tf_op jit(solution)/shard_map/ppermute | solution.py:336
  129.3 7.4 %copy-start.8 = (bf16[24,128,128]{2,1,0:T(8,128)(2,1)S(1)}, bf16[24,128,128]{2,1,0:T(8,128)(2,1)}, u32[]{:S(2)}) copy-start(bf16[24,128,128]{2,1,0:T(8,128)(2,1)} %get-tuple-element.29) | copy-start | bytes 2359300
  129.3 36.7 %copy-start.7 = (bf16[24,128,128]{2,1,0:T(8,128)(2,1)S(1)}, bf16[24,128,128]{2,1,0:T(8,128)(2,1)}, u32[]{:S(2)}) copy-start(bf16[24,128,128]{2,1,0:T(8,128)(2,1)} %get-tuple-element.35) | copy-start | bytes 2359300
  129.3 32.3 %all-to-all-start.3 = ((bf16[64,128,128]{2,1,0:T(8,128)(2,1)}), bf16[64,128,128]{2,1,0:T(8,128)(2,1)}, u32[]{:S(2)}, u32[]{:S(2)}) async-start(bf16[64,128,128]{2,1,0:T(8,128)(2,1)} %get-tuple-element.27), calls=%async_computation.3 | async-start | bytes 4194304 | tf_op jit(solution)/shard_map/all_to_all | solution.py:332
  135.7 19.8 %collective-permute-start.3 = (bf16[24,128,128]{2,1,0:T(8,128)(2,1)}, bf16[24,128,128]{2,1,0:T(8,128)(2,1)S(1)}, u32[]{:S(2)}, u32[]{:S(2)}) collective-permute-start(bf16[24,128,128]{2,1,0:T(8,128)(2,1)} %get-tuple-element.28), channel_id=1, source_target_pairs={{0,1},{1,2},{2,3},{3,0},{4,5},{5,6},{6,7},{7,4},{8,9},{9,10},{10,1... | collective-permute-start | bytes 2359304 | tf_op jit(solution)/shard_map/ppermute | solution.py:336
  136.7 19.4 %collective-permute-start.4 = (bf16[24,128,128]{2,1,0:T(8,128)(2,1)S(1)}, bf16[24,128,128]{2,1,0:T(8,128)(2,1)S(1)}, u32[]{:S(2)}, u32[]{:S(2)}) collective-permute-start(bf16[24,128,128]{2,1,0:T(8,128)(2,1)S(1)} %copy-done.8), channel_id=1, source_target_pairs={{0,3},{1,0},{2,1},{3,2},{4,7},{5,4},{6,5},{7,6},{8,11},{9,8},{10,9... | collective-permute-start | bytes 2359304 | tf_op jit(solution)/shard_map/ppermute | solution.py:336
  155.5 30.9 %copy-start = (bf16[24,128,128]{2,1,0:T(8,128)(2,1)}, bf16[24,128,128]{2,1,0:T(8,128)(2,1)S(1)}, u32[]{:S(2)}) copy-start(bf16[24,128,128]{2,1,0:T(8,128)(2,1)S(1)} %collective-permute-done.3.refs_2_) | copy-start | bytes 2359300
  156.2 30.3 %copy-start.1 = (bf16[24,128,128]{2,1,0:T(8,128)(2,1)}, bf16[24,128,128]{2,1,0:T(8,128)(2,1)S(1)}, u32[]{:S(2)}) copy-start(bf16[24,128,128]{2,1,0:T(8,128)(2,1)S(1)} %collective-permute-done.4.refs_4_) | copy-start | bytes 2359300
  161.6 31.6 %all-to-all-start.4 = ((bf16[8,3,128,128]{3,2,1,0:T(8,128)(2,1)}), bf16[8,3,128,128]{3,2,1,0:T(8,128)(2,1)S(1)}, u32[]{:S(2)}, u32[]{:S(2)}) async-start(bf16[8,3,128,128]{3,2,1,0:T(8,128)(2,1)} %bitcast.20), calls=%async_computation.4 | async-start | bytes 1572864 | tf_op jit(solution)/shard_map/all_to_all | solution.py:322
  166.0 20.4 %collective-permute-start.5 = (bf16[24,128,128]{2,1,0:T(8,128)(2,1)S(1)}, bf16[24,128,128]{2,1,0:T(8,128)(2,1)S(1)}, u32[]{:S(2)}, u32[]{:S(2)}) collective-permute-start(bf16[24,128,128]{2,1,0:T(8,128)(2,1)S(1)} %copy-done.7), channel_id=1, source_target_pairs={{0,2},{1,3},{2,0},{3,1},{4,6},{5,7},{6,4},{7,5},{8,10},{9,11},{10,... | collective-permute-start | bytes 2359304 | tf_op jit(solution)/shard_map/ppermute | solution.py:336
  186.4 0.9 copy-start.2
  193.2 28.2 %all-to-all-start.5 = ((bf16[8,3,128,128]{3,2,1,0:T(8,128)(2,1)}), bf16[8,3,128,128]{3,2,1,0:T(8,128)(2,1)S(1)}, u32[]{:S(2)}, u32[]{:S(2)}) async-start(bf16[8,3,128,128]{3,2,1,0:T(8,128)(2,1)} %bitcast.161), calls=%async_computation.5 | async-start | bytes 1572864 | tf_op jit(solution)/shard_map/all_to_all | solution.py:322

commit v3 on v2

--- a/solution.py
+++ b/solution.py
@@ -31,10 +31,50 @@
     copy.wait()
 
 
+def pack_apart_kernel(z_ref, first_ref, second_ref, *refs):
+    outs, (first, second, packed, sems) = refs[:HEADS], refs[HEADS:]
+    copies = [
+        pltpu.make_async_copy(first_ref, first, sems.at[0]),
+        pltpu.make_async_copy(second_ref, second, sems.at[1]),
+    ]
+    for copy in copies:
+        copy.start()
+    for copy in copies:
+        copy.wait()
+    for head in range(HEADS):
+        cols = slice(head * HEAD_DIM, (head + 1) * HEAD_DIM)
+        packed[head] = jnp.concatenate([first[:, :, cols], second[:, :, cols]], axis=-1)
+    copies = [
+        pltpu.make_async_copy(packed.at[(z_ref[0] + shift) % HEADS], out, sems.at[shift])
+        for shift, out in enumerate(outs)
+    ]
+    for copy in copies:
+        copy.start()
+    for copy in copies:
+        copy.wait()
+
+
 def unpack_kernel(in_ref, first_ref, second_ref, packed, first, second, sems):
     copy = pltpu.make_async_copy(in_ref, packed, sems.at[2])
     copy.start()
     copy.wait()
+    unpack_heads(first_ref, second_ref, packed, first, second, sems)
+
+
+def unpack_apart_kernel(z_ref, *refs):
+    ins, (first_ref, second_ref, packed, first, second, sems) = refs[:HEADS], refs[HEADS:]
+    copies = [
+        pltpu.make_async_copy(source, packed.at[(z_ref[0] + HEADS - shift) % HEADS], sems.at[shift])
+        for shift, source in enumerate(ins)
+    ]
+    for copy in copies:
+        copy.start()
+    for copy in copies:
+        copy.wait()
+    unpack_heads(first_ref, second_ref, packed, first, second, sems)
+
+
+def unpack_heads(first_ref, second_ref, packed, first, second, sems):
     for pair in range(HEADS // 2):
         even = packed[2 * pair]
         odd = packed[2 * pair + 1]
@@ -61,20 +101,29 @@
     pltpu.make_async_copy(out_ref, out_ref, sem).wait()
 
 
-def attend_kernel(*refs, tiles, entries, ys, far):
-    code_ref, count_ref = refs[:2]
-    kv_refs = refs[2 : 3 + ys]
-    qg_ref = refs[3 + ys]
-    odq_ref = refs[4 + ys]
-    dkv_refs = refs[5 + ys : 6 + 2 * ys]
-    table, totals, scores, dprobs, masks, qg_tiles, sems = refs[6 + 2 * ys :]
+def attend_kernel(*refs, tiles, entries, ys, zs, far):
+    code_ref, count_ref, z_ref = refs[:3]
+    refs = refs[3:]
+    kv_refs, refs = refs[: ys + 1], refs[ys + 1 :]
+    qg_refs, refs = refs[:zs], refs[zs:]
+    odq_refs, refs = refs[:zs], refs[zs:]
+    dkv_refs, refs = refs[: ys + 1], refs[ys + 1 :]
+    table, totals, scores, dprobs, masks, qg_tiles, sems = refs
+    tile_dev = tiles // zs
+
+    def z_part(distance):
+        return qg_tiles.at[pl.ds(((z_ref[0] + zs + distance) % zs) * tile_dev, tile_dev)]
+
     spans = [(at * tiles, tiles) for at in range(ys)] + [(ys * tiles, far)]
     slots_all = ys * tiles + far
     copies = [
         pltpu.make_async_copy(ref, table.at[pl.ds(*span)], sems.at[at])
         for at, (ref, span) in enumerate(zip(kv_refs, spans))
     ]
-    copies.append(pltpu.make_async_copy(qg_ref, qg_tiles, sems.at[ys + 1]))
+    copies += [
+        pltpu.make_async_copy(ref, z_part(-at), sems.at[ys + 1 + at])
+        for at, ref in enumerate(qg_refs)
+    ]
     for copy in copies:
         copy.start()
     rows = 128
@@ -162,8 +211,12 @@
         return carry
 
     lax.fori_loop(0, tiles, tile_step, 0)
-    copies = [pltpu.make_async_copy(qg_tiles, odq_ref, sems.at[ys + 1])]
-    copies[0].start()
+    copies = [
+        pltpu.make_async_copy(z_part(at), ref, sems.at[ys + 1 + at])
+        for at, ref in enumerate(odq_refs)
+    ]
+    for copy in copies:
+        copy.start()
     scales = jnp.where(left, scale, 1.0).astype(jnp.float32)
 
     def write(at, carry):
@@ -304,6 +357,37 @@
             compiler_params=limits(16),
         )(pin(first.reshape(tile_shape.shape)), pin(second.reshape(tile_shape.shape)))
 
+    z_at = jnp.reshape(lax.axis_index("seq") // ys, (1,)).astype(jnp.int32)
+    part_shape = shape_of(tile_dev, rows, 128)
+
+    def pack_apart(first, second):
+        return pl.pallas_call(
+            pack_apart_kernel,
+            out_shape=(part_shape,) * zs,
+            in_specs=smem(1) + hbm(2),
+            out_specs=hbm(zs),
+            scratch_shapes=[scratch(tile_shape), scratch(tile_shape), scratch(head_shape), pltpu.SemaphoreType.DMA((zs,))],
+            compiler_params=limits(16),
+        )(z_at, pin(first.reshape(tile_shape.shape)), pin(second.reshape(tile_shape.shape)))
+
+    def unpack_apart(parts):
+        first, second = pl.pallas_call(
+            unpack_apart_kernel,
+            out_shape=(tile_shape, tile_shape),
+            in_specs=smem(1) + hbm(zs),
+            out_specs=hbm(2),
+            scratch_shapes=[scratch(head_shape), scratch(tile_shape), scratch(tile_shape), pltpu.SemaphoreType.DMA((zs,))],
+            compiler_params=limits(16),
+        )(z_at, *map(pin, parts))
+        return (
+            first.reshape(1, tile_dev, 1, rows, width),
+            second.reshape(1, tile_dev, 1, rows, width),
+        )
+
+    def shift_z(source, shift):
+        pairs = [(z * ys + y, ((z + shift) % zs) * ys + y) for z in range(zs) for y in range(ys)]
+        return lax.ppermute(source, "seq", pairs)
+
     def unpack(joined):
         first, second = pl.pallas_call(
             unpack_kernel,
@@ -335,11 +419,8 @@
         pairs = [(z * ys + y, z * ys + (y + shift) % ys) for z in range(zs) for y in range(ys)]
         return lax.ppermute(source, "seq", pairs)
 
-    def after(source, *others):
-        return lax.optimization_barrier((source, *others))
-
     kv = over_z(pack(key_input, value_input))
-    send_qg = pack(queries, grad_output)
+    qg = list(pack_apart(queries, grad_output))
     near_kv = [kv] + [over_y(kv, -shift) for shift in range(1, ys)]
     far_send = pl.pallas_call(
         functools.partial(far_kernel, far=far, zs=zs, tile_dev=tile_dev),
@@ -350,15 +431,14 @@
         compiler_params=limits(8),
     )(far_rank, kv)
     far_kv = over_groups(far_send)
-    send_qg, far_kv, near_kv[1], near_kv[-1] = after(send_qg, far_kv, near_kv[1], near_kv[-1])
-    qg = over_z(send_qg)
+    qg[1:] = [shift_z(qg[shift], shift) for shift in range(1, zs)]
 
     slots = near + far + 1
-    odq, *dkv_parts = pl.pallas_call(
-        functools.partial(attend_kernel, tiles=tiles, entries=entries, ys=ys, far=far),
-        out_shape=(block_shape,) * (ys + 1) + (far_shape,),
-        in_specs=smem(2) + hbm(ys + 2),
-        out_specs=hbm(ys + 2),
+    parts = pl.pallas_call(
+        functools.partial(attend_kernel, tiles=tiles, entries=entries, ys=ys, zs=zs, far=far),
+        out_shape=(part_shape,) * zs + (block_shape,) * ys + (far_shape,),
+        in_specs=smem(3) + hbm(ys + 1 + zs),
+        out_specs=hbm(ys + 1 + zs),
         scratch_shapes=[
             pltpu.VMEM((slots, rows, 128), bf16),
             pltpu.VMEM((slots, rows, 128), jnp.float32),
@@ -366,15 +446,16 @@
             pltpu.VMEM((entries, rows, rows), jnp.float32),
             pltpu.VMEM((3, rows, rows), jnp.float32),
             scratch(block_shape),
-            pltpu.SemaphoreType.DMA((ys + 2,)),
+            pltpu.SemaphoreType.DMA((ys + 1 + zs,)),
         ],
         compiler_params=limits(40),
-    )(code, count, kv, *map(pin, near_kv[1:]), pin(far_kv), qg)
+    )(code, count, z_at, kv, *map(pin, near_kv[1:]), far_kv, *map(pin, qg))
+    odq, dkv_parts = list(parts[:zs]), parts[zs:]
 
     near_back = [dkv_parts[0]] + [over_y(dkv_parts[shift], shift) for shift in range(1, ys)]
     far_back = over_groups(dkv_parts[ys])
-    odq, far_back, near_back[1], near_back[-1] = after(odq, far_back, near_back[1], near_back[-1])
-    odq_back = over_z(odq)
+    odq[1:] = [shift_z(odq[shift], shift) for shift in range(1, zs)]
+    last_rank, *odq[1:] = lax.optimization_barrier((far_rank, *odq[1:]))
     dkv = pl.pallas_call(
         functools.partial(combine_kernel, ys=ys, far=far, zs=zs, tile_dev=tile_dev),
         out_shape=block_shape,
@@ -387,8 +468,8 @@
             pltpu.SemaphoreType.DMA((ys + 1,)),
         ],
         compiler_params=limits(24),
-    )(far_rank, *map(pin, near_back), pin(far_back))
-    attended, grad_queries = unpack(odq_back)
+    )(last_rank, *map(pin, near_back), far_back)
+    attended, grad_queries = unpack_apart(odq)
     grad_keys, grad_values = unpack(over_z(dkv))
     return attended, grad_queries, grad_keys, grad_values
 

time: 224 us -> 199 us (0.89)
  waiting for transfers between devices: 124 us -> 84.9 us
  starting transfers between devices: 43.4 us -> 59 us
    ppermute x6, waiting for transfers between devices: 69.5 us -> 0.02 us  [over_y(): return lax.ppermute(source, 'seq', pairs)]
    ppermute x0 -> x14, waiting for transfers between devices: none -> 45.3 us  [shift_z(): return lax.ppermute(source, 'seq', pairs)]
    ppermute x0 -> x14, starting transfers between devices: none -> 23 us  [shift_z(): return lax.ppermute(source, 'seq', pairs)]
    all_to_all x2, waiting for transfers between devices: 10.4 us -> 0.01 us  [over_groups(): lax.all_to_all(source, 'grp', split_axis=0, concat_axis=0, tiled=True)]
    all_to_all x4 -> x2, starting transfers between devices: 23.3 us -> 14.4 us  [over_z(): lax.all_to_all(source.reshape(head_shape.shape), 'seq', split_axis=0, con...]
    pallas_call x0 -> x2, Pallas kernels: none -> 4.74 us  [the longest x1 2.41 us: unpack_apart(): pl.pallas_call(unpack_apart_kernel, out_shape=(tile_shape, tile_shape), i...]
    all_to_all x4 -> x2, waiting for transfers between devices: 43.9 us -> 39.5 us  [over_z(): lax.all_to_all(source.reshape(head_shape.shape), 'seq', split_axis=0, con...]
    pallas_call x2 -> x1, Pallas kernels: 4.61 us -> 2.33 us  [pack(): pl.pallas_call(pack_kernel, out_shape=head_shape, in_specs=hbm(2), out_sp...]
  transfers between devices with their start and end apart: 12 -> 24, of which waited for: 11 -> 14; matrix products, arithmetic and copies ran while one was open for 2% -> 1% of each run, Pallas kernels for 4% -> 2%
where the time goes in v3:
time: 199 us; the launch traced here: 198 us
  waiting for transfers between devices  84.9 us (43%)
  starting transfers between devices  59 us (30%)
  Pallas kernels  49.8 us (25%)
  local copies, waits for them, and re-layouts  2.43 us (1%)
    ppermute x14, waiting for transfers between devices, shift_z(): return lax.ppermute(source, 'seq', pairs)  45.3 us
    all_to_all x2, waiting for transfers between devices, over_z(): lax.all_to_all(source.reshape(head_shape.shape), 'seq', split_axis=0, con...  39.5 us
    pallas_call x1, Pallas kernels, per_device(): pl.pallas_call(functools.partial(attend_kernel, tiles=tiles, entries=entr...  34.5 us
    ppermute x14, starting transfers between devices, shift_z(): return lax.ppermute(source, 'seq', pairs)  23 us
    all_to_all x2, starting transfers between devices, over_z(): lax.all_to_all(source.reshape(head_shape.shape), 'seq', split_axis=0, con...  14.4 us
    all_to_all x2, starting transfers between devices, over_groups(): lax.all_to_all(source, 'grp', split_axis=0, concat_axis=0, tiled=True)  12.6 us
    ppermute x6, starting transfers between devices, over_y(): return lax.ppermute(source, 'seq', pairs)  8.95 us
    pallas_call x1, Pallas kernels, per_device(): pl.pallas_call(functools.partial(combine_kernel, ys=ys, far=far, zs=zs, t...  5.13 us
  transfers between devices with their start and end apart: 24, of which 14 were waited for; matrix products, arithmetic and copies ran while one was open for 1% of the time, Pallas kernels for 2%

profile of v3, /device:TPU:10, one launch (start us, length us, event | category | flops | bytes accessed | tf_op | source)
XLA Modules:
  0.0 197.9 jit_solution(14742611011398521532)
XLA Ops:
  0.7 2.3 %shard_map.93 = bf16[8,3,128,128]{3,2,1,0:T(8,128)(2,1)} custom-call(bf16[3,128,512]{2,1,0:T(8,128)(2,1)} %bitcast.165, bf16[3,128,512]{2,1,0:T(8,128)(2,1)} %bitcast.166), custom_call_target="tpu_custom_call" | custom-call | tf_op jit(solution)/shard_map/pallas_call | solution.py:351
  3.0 8.5 %all-to-all-start = ((bf16[8,3,128,128]{3,2,1,0:T(8,128)(2,1)}), bf16[8,3,128,128]{3,2,1,0:T(8,128)(2,1)S(1)}, u32[]{:S(2)}, u32[]{:S(2)}) async-start(bf16[8,3,128,128]{3,2,1,0:T(8,128)(2,1)} %shard_map.93), calls=%async_computation | async-start | bytes 1572864 | tf_op jit(solution)/shard_map/all_to_all | solution.py:406
  11.5 0.2 copy.57
  11.6 0.2 copy.64
  11.8 0.2 constant_dynamic-slice_fusion
  12.1 0.5 fusion.1
  12.5 0.1 broadcast_select_fusion
  12.6 0.1 select_n.93.rank_ref.refs_0_
  12.7 21.9 %all-to-all-done = bf16[8,3,128,128]{3,2,1,0:T(8,128)(2,1)S(1)} async-done(((bf16[8,3,128,128]{3,2,1,0:T(8,128)(2,1)}), bf16[8,3,128,128]{3,2,1,0:T(8,128)(2,1)S(1)}, u32[]{:S(2)}, u32[]{:S(2)}) %all-to-all-start) | async-done | bytes 786464 | tf_op jit(solution)/shard_map/all_to_all | solution.py:406
  34.6 1.9 shard_map.94
  36.5 4.8 %all-to-all-start.1 = ((bf16[64,128,128]{2,1,0:T(8,128)(2,1)}), bf16[64,128,128]{2,1,0:T(8,128)(2,1)S(1)}, u32[]{:S(2)}, u32[]{:S(2)}) async-start(bf16[64,128,128]{2,1,0:T(8,128)(2,1)} %shard_map.94), calls=%async_computation.1 | async-start | bytes 4194304 | tf_op jit(solution)/shard_map/all_to_all | solution.py:416
  41.3 1.6 collective-permute-start.2
  42.9 0.9 collective-permute-start.1
  43.8 2.4 %collective-permute-start = (bf16[24,128,128]{2,1,0:T(8,128)(2,1)S(1)}, bf16[24,128,128]{2,1,0:T(8,128)(2,1)}, u32[]{:S(2)}, u32[]{:S(2)}) collective-permute-start(bf16[24,128,128]{2,1,0:T(8,128)(2,1)S(1)} %bitcast.157), channel_id=1, source_target_pairs={{0,3},{1,0},{2,1},{3,2},{4,7},{5,4},{6,5},{7,6},{8,11},{9,8},{10,9... | collective-permute-start | bytes 2359304 | tf_op jit(solution)/shard_map/ppermute | solution.py:420
  46.3 2.3 %shard_map.95 = (bf16[3,128,128]{2,1,0:T(8,128)(2,1)}, bf16[3,128,128]{2,1,0:T(8,128)(2,1)}, bf16[3,128,128]{2,1,0:T(8,128)(2,1)}, bf16[3,128,128]{2,1,0:T(8,128...) custom-call(s32[1]{0:T(128)} %bitcast.z_ref.refs_2_, ...), custom_call_target="tpu_custom_call" | custom-call | tf_op jit(solution)/shard_map/pallas_call | solution.py:364
  48.6 0.6 collective-permute-start.3
  49.2 0.0 collective-permute-start.4
  49.2 7.5 %collective-permute-done.3.refs_9_ = bf16[3,128,128]{2,1,0:T(8,128)(2,1)S(1)} collective-permute-done((bf16[3,128,128]{2,1,0:T(8,128)(2,1)}, bf16[3,128,128]{2,1,0:T(8,128)(2,1)S(1)}, u32[]{:S(2)}, u32[]{:S(2)}) %collective-permute-start.3) | collective-permute-done | bytes 98336 | tf_op jit(solution)/shard_map/ppermute | solution.py:389
  56.7 0.0 collective-permute-start.5
  56.7 4.2 %collective-permute-done.4.refs_10_ = bf16[3,128,128]{2,1,0:T(8,128)(2,1)S(1)} collective-permute-done((bf16[3,128,128]{2,1,0:T(8,128)(2,1)}, bf16[3,128,128]{2,1,0:T(8,128)(2,1)S(1)}, u32[]{:S(2)}, u32[]{:S(2)}) %collective-permute-start.4) | collective-permute-done | bytes 98336 | tf_op jit(solution)/shard_map/ppermute | solution.py:389
  60.9 0.0 collective-permute-start.6
  60.9 6.5 %collective-permute-done.5.refs_11_ = bf16[3,128,128]{2,1,0:T(8,128)(2,1)S(1)} collective-permute-done((bf16[3,128,128]{2,1,0:T(8,128)(2,1)}, bf16[3,128,128]{2,1,0:T(8,128)(2,1)S(1)}, u32[]{:S(2)}, u32[]{:S(2)}) %collective-permute-start.5) | collective-permute-done | bytes 98336 | tf_op jit(solution)/shard_map/ppermute | solution.py:389
  67.4 1.9 collective-permute-start.7
  69.3 0.1 convert_reduce_fusion
  69.5 0.1 copy.67
  69.5 0.1 reshape.93.refs_1_
  69.6 0.5 collective-permute-done.6.refs_12_
  70.1 0.0 collective-permute-start.8
  70.1 6.8 %collective-permute-done.7.refs_13_ = bf16[3,128,128]{2,1,0:T(8,128)(2,1)} collective-permute-done((bf16[3,128,128]{2,1,0:T(8,128)(2,1)}, bf16[3,128,128]{2,1,0:T(8,128)(2,1)}, u32[]{:S(2)}, u32[]{:S(2)}) %collective-permute-start.7) | collective-permute-done | bytes 98336 | tf_op jit(solution)/shard_map/ppermute | solution.py:389
  76.9 0.0 collective-permute-start.9
  77.0 0.1 reshape.92.refs_0_
  77.1 0.5 collective-permute-done.8.refs_14_
  77.6 4.3 %collective-permute-done.9.refs_15_ = bf16[3,128,128]{2,1,0:T(8,128)(2,1)} collective-permute-done((bf16[3,128,128]{2,1,0:T(8,128)(2,1)}, bf16[3,128,128]{2,1,0:T(8,128)(2,1)}, u32[]{:S(2)}, u32[]{:S(2)}) %collective-permute-start.9) | collective-permute-done | bytes 98336 | tf_op jit(solution)/shard_map/ppermute | solution.py:389
  81.9 0.0 collective-permute-done.2.refs_6_
  81.9 0.0 collective-permute-done.1.refs_5_
  81.9 0.0 collective-permute-done.refs_4_
  81.9 0.0 all-to-all-done.1.refs_7_
  81.9 34.5 %shard_map.96 = (bf16[3,128,128]{2,1,0:T(8,128)(2,1)}, bf16[3,128,128]{2,1,0:T(8,128)(2,1)}, bf16[3,128,128]{2,1,0:T(8,128)(2,1)}, bf16[3,128,128]{2,1,0:T(8,128...) custom-call(s32[384]{0:T(512)S(1)} %reshape.92.refs_0_, ...), custom_call_target="tpu_custom_call" | custom-call | tf_op jit(solution)/shard_map/pallas_call | solution.py:437
  116.5 7.8 %all-to-all-start.2 = ((bf16[64,128,128]{2,1,0:T(8,128)(2,1)}), bf16[64,128,128]{2,1,0:T(8,128)(2,1)S(1)}, u32[]{:S(2)}, u32[]{:S(2)}) async-start(bf16[64,128,128]{2,1,0:T(8,128)(2,1)} %get-tuple-element.67), calls=%async_computation.2 | async-start | bytes 4194304 | tf_op jit(solution)/shard_map/all_to_all | solution.py:416
  124.3 0.0 collective-permute-start.17
  124.3 4.0 %collective-permute-start.18 = (bf16[24,128,128]{2,1,0:T(8,128)(2,1)}, bf16[24,128,128]{2,1,0:T(8,128)(2,1)S(1)}, u32[]{:S(2)}, u32[]{:S(2)}) collective-permute-start(bf16[24,128,128]{2,1,0:T(8,128)(2,1)} %get-tuple-element.65), channel_id=1, source_target_pairs={{0,2},{1,3},{2,0},{3,1},{4,6},{5,7},{6,4},{7,5},{8,10},{9,11},{10,... | collective-permute-start | bytes 2359304 | tf_op jit(solution)/shard_map/ppermute | solution.py:420
  128.3 0.0 collective-permute-start.19
  128.3 2.4 %collective-permute-start.10 = (bf16[3,128,128]{2,1,0:T(8,128)(2,1)S(1)}, bf16[3,128,128]{2,1,0:T(8,128)(2,1)S(1)}, u32[]{:S(2)}, u32[]{:S(2)}) collective-permute-start(bf16[3,128,128]{2,1,0:T(8,128)(2,1)S(1)} %copy-done.17), channel_id=1, source_target_pairs={{0,4},{1,5},{2,6},{3,7},{4,8},{5,9},{6,10},{7,11},{8,12},{9,13},{1... | collective-permute-start | bytes 294920 | tf_op jit(solution)/shard_map/ppermute | solution.py:389
  130.7 1.9 collective-permute-start.11
  132.6 1.5 collective-permute-done.10.refs_1_
  134.1 3.9 %collective-permute-start.12 = (bf16[3,128,128]{2,1,0:T(8,128)(2,1)S(1)}, bf16[3,128,128]{2,1,0:T(8,128)(2,1)S(1)}, u32[]{:S(2)}, u32[]{:S(2)}) collective-permute-start(bf16[3,128,128]{2,1,0:T(8,128)(2,1)S(1)} %copy-done.15), channel_id=1, source_target_pairs={{0,12},{1,13},{2,14},{3,15},{4,16},{5,17},{6,18},{7,19},{8,20},{9,... | collective-permute-start | bytes 294920 | tf_op jit(solution)/shard_map/ppermute | solution.py:389
  138.0 0.1 collective-permute-done.11.refs_2_
  138.1 3.7 %collective-permute-start.13 = (bf16[3,128,128]{2,1,0:T(8,128)(2,1)S(1)}, bf16[3,128,128]{2,1,0:T(8,128)(2,1)S(1)}, u32[]{:S(2)}, u32[]{:S(2)}) collective-permute-start(bf16[3,128,128]{2,1,0:T(8,128)(2,1)S(1)} %copy-done.14), channel_id=1, source_target_pairs={{0,16},{1,17},{2,18},{3,19},{4,20},{5,21},{6,22},{7,23},{8,24},{9,... | collective-permute-start | bytes 294920 | tf_op jit(solution)/shard_map/ppermute | solution.py:389
  141.8 6.7 %collective-permute-done.12.refs_3_ = bf16[3,128,128]{2,1,0:T(8,128)(2,1)S(1)} collective-permute-done((bf16[3,128,128]{2,1,0:T(8,128)(2,1)S(1)}, bf16[3,128,128]{2,1,0:T(8,128)(2,1)S(1)}, u32[]{:S(2)}, u32[]{:S(2)}) %collective-permute-start.12) | collective-permute-done | bytes 98336 | tf_op jit(solution)/shard_map/ppermute | solution.py:389
  148.4 2.8 %collective-permute-start.14 = (bf16[3,128,128]{2,1,0:T(8,128)(2,1)}, bf16[3,128,128]{2,1,0:T(8,128)(2,1)S(1)}, u32[]{:S(2)}, u32[]{:S(2)}) collective-permute-start(bf16[3,128,128]{2,1,0:T(8,128)(2,1)} %get-tuple-element.50), channel_id=1, source_target_pairs={{0,20},{1,21},{2,22},{3,23},{4,24},{5,25},{6,26},{7,27},{8,28},{9,... | collective-permute-start | bytes 294920 | tf_op jit(solution)/shard_map/ppermute | solution.py:389
  151.2 0.0 collective-permute-done.13.refs_4_
  151.2 2.0 collective-permute-start.15
  153.2 4.3 %collective-permute-done.14.refs_5_ = bf16[3,128,128]{2,1,0:T(8,128)(2,1)S(1)} collective-permute-done((bf16[3,128,128]{2,1,0:T(8,128)(2,1)}, bf16[3,128,128]{2,1,0:T(8,128)(2,1)S(1)}, u32[]{:S(2)}, u32[]{:S(2)}) %collective-permute-start.14) | collective-permute-done | bytes 98336 | tf_op jit(solution)/shard_map/ppermute | solution.py:389
  157.6 3.8 %collective-permute-start.16 = (bf16[3,128,128]{2,1,0:T(8,128)(2,1)}, bf16[3,128,128]{2,1,0:T(8,128)(2,1)S(1)}, u32[]{:S(2)}, u32[]{:S(2)}) collective-permute-start(bf16[3,128,128]{2,1,0:T(8,128)(2,1)} %get-tuple-element.52), channel_id=1, source_target_pairs={{0,28},{1,29},{2,30},{3,31},{4,0},{5,1},{6,2},{7,3},{8,4},{9,5},{1... | collective-permute-start | bytes 294920 | tf_op jit(solution)/shard_map/ppermute | solution.py:389
  161.3 2.5 %collective-permute-done.16.refs_7_ = bf16[3,128,128]{2,1,0:T(8,128)(2,1)S(1)} collective-permute-done((bf16[3,128,128]{2,1,0:T(8,128)(2,1)}, bf16[3,128,128]{2,1,0:T(8,128)(2,1)S(1)}, u32[]{:S(2)}, u32[]{:S(2)}) %collective-permute-start.16) | collective-permute-done | bytes 98336 | tf_op jit(solution)/shard_map/ppermute | solution.py:389
  163.9 0.0 collective-permute-done.17.refs_2_
  163.9 0.0 collective-permute-done.18.refs_3_
  163.9 0.6 copy-done.8
  164.5 0.9 copy-done.1
  165.4 5.1 %shard_map.98 = bf16[24,128,128]{2,1,0:T(8,128)(2,1)} custom-call(s32[64]{0:T(128)S(1)} %select_n.93.rank_ref.refs_0_, bf16[24,128,128]{2,1,0:T(8,128)(2,1)} %get-tuple-element.63.refs_1_, bf16[24,128,128]{2,1,0:T(8,128)(2,1)} %copy-done, bf16[24,128,128]{2,1,0:T(8,128)(2,1)} %copy-done.1, bf16[24,128,128]{2,1,0:T(8,128)(2,1)} %collective-permute-done.19.refs_4_, ...), custom_call_target="tpu_custom_call" | custom-call | tf_op jit(solution)/shard_map/pallas_call | solution.py:459
  170.5 5.9 %all-to-all-start.3 = ((bf16[8,3,128,128]{3,2,1,0:T(8,128)(2,1)}), bf16[8,3,128,128]{3,2,1,0:T(8,128)(2,1)S(1)}, u32[]{:S(2)}, u32[]{:S(2)}) async-start(bf16[8,3,128,128]{3,2,1,0:T(8,128)(2,1)} %bitcast.159), calls=%async_computation.3 | async-start | bytes 1572864 | tf_op jit(solution)/shard_map/all_to_all | solution.py:406
  176.5 2.4 %shard_map.97 = (bf16[3,128,512]{2,1,0:T(8,128)(2,1)}, bf16[3,128,512]{2,1,0:T(8,128)(2,1)}) custom-call(s32[1]{0:T(128)} %bitcast.z_ref.refs_2_, bf16[3,128,128]{2,1,0:T(8,128)(2,1)} %get-tuple-element.45.refs_0_, bf16[3,128,128]{2,1,0:T(8,128)(2,1)} %copy-done.2, bf16[3,128,128]{2,1,0:T(8,128)(2,1)} %copy-done.3, bf16[3,128,128]{2,1,0:T(8,128)(2,1)} %copy-done.4, ...), custom_call_target="tpu_custom_call" | custom-call | tf_op jit(solution)/shard_map/pallas_call | solution.py:374
  178.9 17.6 %all-to-all-done.3.in_ref = bf16[8,3,128,128]{3,2,1,0:T(8,128)(2,1)S(1)} async-done(((bf16[8,3,128,128]{3,2,1,0:T(8,128)(2,1)}), bf16[8,3,128,128]{3,2,1,0:T(8,128)(2,1)S(1)}, u32[]{:S(2)}, u32[]{:S(2)}) %all-to-all-start.3) | async-done | bytes 786464 | tf_op jit(solution)/shard_map/all_to_all | solution.py:406
  196.6 1.2 shard_map.99
  (42 shorter events, 0.1 us)
Async XLA Ops:
  0.6 10.8 %copy-start.12 = (s32[768,16]{0,1:T(8,128)S(1)}, s32[768,16]{0,1:T(8,128)}, u32[]{:S(2)}) copy-start(s32[768,16]{0,1:T(8,128)} %param.10) | copy-start | bytes 147460
  0.6 11.0 %copy-start.13 = (s32[768,16]{0,1:T(8,128)S(1)}, s32[768,16]{0,1:T(8,128)}, u32[]{:S(2)}) copy-start(s32[768,16]{0,1:T(8,128)} %param.11) | copy-start | bytes 147460
  3.0 31.6 %all-to-all-start = ((bf16[8,3,128,128]{3,2,1,0:T(8,128)(2,1)}), bf16[8,3,128,128]{3,2,1,0:T(8,128)(2,1)S(1)}, u32[]{:S(2)}, u32[]{:S(2)}) async-start(bf16[8,3,128,128]{3,2,1,0:T(8,128)(2,1)} %shard_map.93), calls=%async_computation | async-start | bytes 1572864 | tf_op jit(solution)/shard_map/all_to_all | solution.py:406
  36.5 45.4 %all-to-all-start.1 = ((bf16[64,128,128]{2,1,0:T(8,128)(2,1)}), bf16[64,128,128]{2,1,0:T(8,128)(2,1)S(1)}, u32[]{:S(2)}, u32[]{:S(2)}) async-start(bf16[64,128,128]{2,1,0:T(8,128)(2,1)} %shard_map.94), calls=%async_computation.1 | async-start | bytes 4194304 | tf_op jit(solution)/shard_map/all_to_all | solution.py:416
  41.3 40.6 %collective-permute-start.2 = (bf16[24,128,128]{2,1,0:T(8,128)(2,1)S(1)}, bf16[24,128,128]{2,1,0:T(8,128)(2,1)}, u32[]{:S(2)}, u32[]{:S(2)}) collective-permute-start(bf16[24,128,128]{2,1,0:T(8,128)(2,1)S(1)} %bitcast.155), channel_id=1, source_target_pairs={{0,1},{1,2},{2,3},{3,0},{4,5},{5,6},{6,7},{7,4},{8,9},{9,10},{10,1... | collective-permute-start | bytes 2359304 | tf_op jit(solution)/shard_map/ppermute | solution.py:420
  42.9 39.0 %collective-permute-start.1 = (bf16[24,128,128]{2,1,0:T(8,128)(2,1)S(1)}, bf16[24,128,128]{2,1,0:T(8,128)(2,1)}, u32[]{:S(2)}, u32[]{:S(2)}) collective-permute-start(bf16[24,128,128]{2,1,0:T(8,128)(2,1)S(1)} %bitcast.156), channel_id=1, source_target_pairs={{0,2},{1,3},{2,0},{3,1},{4,6},{5,7},{6,4},{7,5},{8,10},{9,11},{10,... | collective-permute-start | bytes 2359304 | tf_op jit(solution)/shard_map/ppermute | solution.py:420
  43.8 38.0 %collective-permute-start = (bf16[24,128,128]{2,1,0:T(8,128)(2,1)S(1)}, bf16[24,128,128]{2,1,0:T(8,128)(2,1)}, u32[]{:S(2)}, u32[]{:S(2)}) collective-permute-start(bf16[24,128,128]{2,1,0:T(8,128)(2,1)S(1)} %bitcast.157), channel_id=1, source_target_pairs={{0,3},{1,0},{2,1},{3,2},{4,7},{5,4},{6,5},{7,6},{8,11},{9,8},{10,9... | collective-permute-start | bytes 2359304 | tf_op jit(solution)/shard_map/ppermute | solution.py:420
  48.6 8.1 %collective-permute-start.3 = (bf16[3,128,128]{2,1,0:T(8,128)(2,1)}, bf16[3,128,128]{2,1,0:T(8,128)(2,1)S(1)}, u32[]{:S(2)}, u32[]{:S(2)}) collective-permute-start(bf16[3,128,128]{2,1,0:T(8,128)(2,1)} %get-tuple-element.38), channel_id=1, source_target_pairs={{0,4},{1,5},{2,6},{3,7},{4,8},{5,9},{6,10},{7,11},{8,12},{9,13},{1... | collective-permute-start | bytes 294920 | tf_op jit(solution)/shard_map/ppermute | solution.py:389
  49.2 11.7 %collective-permute-start.4 = (bf16[3,128,128]{2,1,0:T(8,128)(2,1)}, bf16[3,128,128]{2,1,0:T(8,128)(2,1)S(1)}, u32[]{:S(2)}, u32[]{:S(2)}) collective-permute-start(bf16[3,128,128]{2,1,0:T(8,128)(2,1)} %get-tuple-element.39), channel_id=1, source_target_pairs={{0,8},{1,9},{2,10},{3,11},{4,12},{5,13},{6,14},{7,15},{8,16},{9,17... | collective-permute-start | bytes 294920 | tf_op jit(solution)/shard_map/ppermute | solution.py:389
  56.7 12.6 %copy-start.9 = (bf16[3,128,128]{2,1,0:T(8,128)(2,1)}, bf16[3,128,128]{2,1,0:T(8,128)(2,1)S(1)}, u32[]{:S(2)}) copy-start(bf16[3,128,128]{2,1,0:T(8,128)(2,1)S(1)} %collective-permute-done.3.refs_9_) | copy-start | bytes 294916
  56.7 10.6 %collective-permute-start.5 = (bf16[3,128,128]{2,1,0:T(8,128)(2,1)}, bf16[3,128,128]{2,1,0:T(8,128)(2,1)S(1)}, u32[]{:S(2)}, u32[]{:S(2)}) collective-permute-start(bf16[3,128,128]{2,1,0:T(8,128)(2,1)} %get-tuple-element.40), channel_id=1, source_target_pairs={{0,12},{1,13},{2,14},{3,15},{4,16},{5,17},{6,18},{7,19},{8,20},{9,... | collective-permute-start | bytes 294920 | tf_op jit(solution)/shard_map/ppermute | solution.py:389
  60.9 8.4 %copy-start.10 = (bf16[3,128,128]{2,1,0:T(8,128)(2,1)}, bf16[3,128,128]{2,1,0:T(8,128)(2,1)S(1)}, u32[]{:S(2)}) copy-start(bf16[3,128,128]{2,1,0:T(8,128)(2,1)S(1)} %collective-permute-done.4.refs_10_) | copy-start | bytes 294916
  60.9 9.2 %collective-permute-start.6 = (bf16[3,128,128]{2,1,0:T(8,128)(2,1)}, bf16[3,128,128]{2,1,0:T(8,128)(2,1)}, u32[]{:S(2)}, u32[]{:S(2)}) collective-permute-start(bf16[3,128,128]{2,1,0:T(8,128)(2,1)} %get-tuple-element.41), channel_id=1, source_target_pairs={{0,16},{1,17},{2,18},{3,19},{4,20},{5,21},{6,22},{7,23},{8,24},{9,... | collective-permute-start | bytes 294920 | tf_op jit(solution)/shard_map/ppermute | solution.py:389
  67.4 1.9 copy-start.11
  67.4 9.6 %collective-permute-start.7 = (bf16[3,128,128]{2,1,0:T(8,128)(2,1)}, bf16[3,128,128]{2,1,0:T(8,128)(2,1)}, u32[]{:S(2)}, u32[]{:S(2)}) collective-permute-start(bf16[3,128,128]{2,1,0:T(8,128)(2,1)} %get-tuple-element.42), channel_id=1, source_target_pairs={{0,20},{1,21},{2,22},{3,23},{4,24},{5,25},{6,26},{7,27},{8,28},{9,... | collective-permute-start | bytes 294920 | tf_op jit(solution)/shard_map/ppermute | solution.py:389
  70.1 7.4 %collective-permute-start.8 = (bf16[3,128,128]{2,1,0:T(8,128)(2,1)}, bf16[3,128,128]{2,1,0:T(8,128)(2,1)}, u32[]{:S(2)}, u32[]{:S(2)}) collective-permute-start(bf16[3,128,128]{2,1,0:T(8,128)(2,1)} %get-tuple-element.43), channel_id=1, source_target_pairs={{0,24},{1,25},{2,26},{3,27},{4,28},{5,29},{6,30},{7,31},{8,0},{9,1... | collective-permute-start | bytes 294920 | tf_op jit(solution)/shard_map/ppermute | solution.py:389
  76.9 4.9 %collective-permute-start.9 = (bf16[3,128,128]{2,1,0:T(8,128)(2,1)}, bf16[3,128,128]{2,1,0:T(8,128)(2,1)}, u32[]{:S(2)}, u32[]{:S(2)}) collective-permute-start(bf16[3,128,128]{2,1,0:T(8,128)(2,1)} %get-tuple-element.44), channel_id=1, source_target_pairs={{0,28},{1,29},{2,30},{3,31},{4,0},{5,1},{6,2},{7,3},{8,4},{9,5},{1... | collective-permute-start | bytes 294920 | tf_op jit(solution)/shard_map/ppermute | solution.py:389
  116.4 11.9 %copy-start.17 = (bf16[3,128,128]{2,1,0:T(8,128)(2,1)S(1)}, bf16[3,128,128]{2,1,0:T(8,128)(2,1)}, u32[]{:S(2)}) copy-start(bf16[3,128,128]{2,1,0:T(8,128)(2,1)} %get-tuple-element.46) | copy-start | bytes 294916
  116.4 14.3 %copy-start.16 = (bf16[3,128,128]{2,1,0:T(8,128)(2,1)S(1)}, bf16[3,128,128]{2,1,0:T(8,128)(2,1)}, u32[]{:S(2)}) copy-start(bf16[3,128,128]{2,1,0:T(8,128)(2,1)} %get-tuple-element.47) | copy-start | bytes 294916
  116.4 17.7 %copy-start.15 = (bf16[3,128,128]{2,1,0:T(8,128)(2,1)S(1)}, bf16[3,128,128]{2,1,0:T(8,128)(2,1)}, u32[]{:S(2)}) copy-start(bf16[3,128,128]{2,1,0:T(8,128)(2,1)} %get-tuple-element.48) | copy-start | bytes 294916
  116.4 21.6 %copy-start.14 = (bf16[3,128,128]{2,1,0:T(8,128)(2,1)S(1)}, bf16[3,128,128]{2,1,0:T(8,128)(2,1)}, u32[]{:S(2)}) copy-start(bf16[3,128,128]{2,1,0:T(8,128)(2,1)} %get-tuple-element.49) | copy-start | bytes 294916
  116.5 48.9 %all-to-all-start.2 = ((bf16[64,128,128]{2,1,0:T(8,128)(2,1)}), bf16[64,128,128]{2,1,0:T(8,128)(2,1)S(1)}, u32[]{:S(2)}, u32[]{:S(2)}) async-start(bf16[64,128,128]{2,1,0:T(8,128)(2,1)} %get-tuple-element.67), calls=%async_computation.2 | async-start | bytes 4194304 | tf_op jit(solution)/shard_map/all_to_all | solution.py:416
  124.3 39.6 %collective-permute-start.17 = (bf16[24,128,128]{2,1,0:T(8,128)(2,1)}, bf16[24,128,128]{2,1,0:T(8,128)(2,1)S(1)}, u32[]{:S(2)}, u32[]{:S(2)}) collective-permute-start(bf16[24,128,128]{2,1,0:T(8,128)(2,1)} %get-tuple-element.64), channel_id=1, source_target_pairs={{0,1},{1,2},{2,3},{3,0},{4,5},{5,6},{6,7},{7,4},{8,9},{9,10},{10,1... | collective-permute-start | bytes 2359304 | tf_op jit(solution)/shard_map/ppermute | solution.py:420
  124.3 39.6 %collective-permute-start.18 = (bf16[24,128,128]{2,1,0:T(8,128)(2,1)}, bf16[24,128,128]{2,1,0:T(8,128)(2,1)S(1)}, u32[]{:S(2)}, u32[]{:S(2)}) collective-permute-start(bf16[24,128,128]{2,1,0:T(8,128)(2,1)} %get-tuple-element.65), channel_id=1, source_target_pairs={{0,2},{1,3},{2,0},{3,1},{4,6},{5,7},{6,4},{7,5},{8,10},{9,11},{10,... | collective-permute-start | bytes 2359304 | tf_op jit(solution)/shard_map/ppermute | solution.py:420
  128.3 37.1 %collective-permute-start.19 = (bf16[24,128,128]{2,1,0:T(8,128)(2,1)}, bf16[24,128,128]{2,1,0:T(8,128)(2,1)}, u32[]{:S(2)}, u32[]{:S(2)}) collective-permute-start(bf16[24,128,128]{2,1,0:T(8,128)(2,1)} %get-tuple-element.66), channel_id=1, source_target_pairs={{0,3},{1,0},{2,1},{3,2},{4,7},{5,4},{6,5},{7,6},{8,11},{9,8},{10,9... | collective-permute-start | bytes 2359304 | tf_op jit(solution)/shard_map/ppermute | solution.py:420
  128.3 5.8 %collective-permute-start.10 = (bf16[3,128,128]{2,1,0:T(8,128)(2,1)S(1)}, bf16[3,128,128]{2,1,0:T(8,128)(2,1)S(1)}, u32[]{:S(2)}, u32[]{:S(2)}) collective-permute-start(bf16[3,128,128]{2,1,0:T(8,128)(2,1)S(1)} %copy-done.17), channel_id=1, source_target_pairs={{0,4},{1,5},{2,6},{3,7},{4,8},{5,9},{6,10},{7,11},{8,12},{9,13},{1... | collective-permute-start | bytes 294920 | tf_op jit(solution)/shard_map/ppermute | solution.py:389
  130.7 7.4 %collective-permute-start.11 = (bf16[3,128,128]{2,1,0:T(8,128)(2,1)S(1)}, bf16[3,128,128]{2,1,0:T(8,128)(2,1)S(1)}, u32[]{:S(2)}, u32[]{:S(2)}) collective-permute-start(bf16[3,128,128]{2,1,0:T(8,128)(2,1)S(1)} %copy-done.16), channel_id=1, source_target_pairs={{0,8},{1,9},{2,10},{3,11},{4,12},{5,13},{6,14},{7,15},{8,16},{9,17... | collective-permute-start | bytes 294920 | tf_op jit(solution)/shard_map/ppermute | solution.py:389
  134.1 42.3 %copy-start.2 = (bf16[3,128,128]{2,1,0:T(8,128)(2,1)}, bf16[3,128,128]{2,1,0:T(8,128)(2,1)S(1)}, u32[]{:S(2)}) copy-start(bf16[3,128,128]{2,1,0:T(8,128)(2,1)S(1)} %collective-permute-done.10.refs_1_) | copy-start | bytes 294916
  134.1 14.3 %collective-permute-start.12 = (bf16[3,128,128]{2,1,0:T(8,128)(2,1)S(1)}, bf16[3,128,128]{2,1,0:T(8,128)(2,1)S(1)}, u32[]{:S(2)}, u32[]{:S(2)}) collective-permute-start(bf16[3,128,128]{2,1,0:T(8,128)(2,1)S(1)} %copy-done.15), channel_id=1, source_target_pairs={{0,12},{1,13},{2,14},{3,15},{4,16},{5,17},{6,18},{7,19},{8,20},{9,... | collective-permute-start | bytes 294920 | tf_op jit(solution)/shard_map/ppermute | solution.py:389
  138.1 38.4 %copy-start.3 = (bf16[3,128,128]{2,1,0:T(8,128)(2,1)}, bf16[3,128,128]{2,1,0:T(8,128)(2,1)S(1)}, u32[]{:S(2)}) copy-start(bf16[3,128,128]{2,1,0:T(8,128)(2,1)S(1)} %collective-permute-done.11.refs_2_) | copy-start | bytes 294916
  138.1 13.1 %collective-permute-start.13 = (bf16[3,128,128]{2,1,0:T(8,128)(2,1)S(1)}, bf16[3,128,128]{2,1,0:T(8,128)(2,1)S(1)}, u32[]{:S(2)}, u32[]{:S(2)}) collective-permute-start(bf16[3,128,128]{2,1,0:T(8,128)(2,1)S(1)} %copy-done.14), channel_id=1, source_target_pairs={{0,16},{1,17},{2,18},{3,19},{4,20},{5,21},{6,22},{7,23},{8,24},{9,... | collective-permute-start | bytes 294920 | tf_op jit(solution)/shard_map/ppermute | solution.py:389
  148.4 28.0 %copy-start.4 = (bf16[3,128,128]{2,1,0:T(8,128)(2,1)}, bf16[3,128,128]{2,1,0:T(8,128)(2,1)S(1)}, u32[]{:S(2)}) copy-start(bf16[3,128,128]{2,1,0:T(8,128)(2,1)S(1)} %collective-permute-done.12.refs_3_) | copy-start | bytes 294916
  148.4 9.1 %collective-permute-start.14 = (bf16[3,128,128]{2,1,0:T(8,128)(2,1)}, bf16[3,128,128]{2,1,0:T(8,128)(2,1)S(1)}, u32[]{:S(2)}, u32[]{:S(2)}) collective-permute-start(bf16[3,128,128]{2,1,0:T(8,128)(2,1)} %get-tuple-element.50), channel_id=1, source_target_pairs={{0,20},{1,21},{2,22},{3,23},{4,24},{5,25},{6,26},{7,27},{8,28},{9,... | collective-permute-start | bytes 294920 | tf_op jit(solution)/shard_map/ppermute | solution.py:389
  151.2 25.3 %copy-start.5 = (bf16[3,128,128]{2,1,0:T(8,128)(2,1)}, bf16[3,128,128]{2,1,0:T(8,128)(2,1)S(1)}, u32[]{:S(2)}) copy-start(bf16[3,128,128]{2,1,0:T(8,128)(2,1)S(1)} %collective-permute-done.13.refs_4_) | copy-start | bytes 294916
  151.2 10.1 %collective-permute-start.15 = (bf16[3,128,128]{2,1,0:T(8,128)(2,1)}, bf16[3,128,128]{2,1,0:T(8,128)(2,1)S(1)}, u32[]{:S(2)}, u32[]{:S(2)}) collective-permute-start(bf16[3,128,128]{2,1,0:T(8,128)(2,1)} %get-tuple-element.51), channel_id=1, source_target_pairs={{0,24},{1,25},{2,26},{3,27},{4,28},{5,29},{6,30},{7,31},{8,0},{9,1... | collective-permute-start | bytes 294920 | tf_op jit(solution)/shard_map/ppermute | solution.py:389
  157.5 18.9 %copy-start.6 = (bf16[3,128,128]{2,1,0:T(8,128)(2,1)}, bf16[3,128,128]{2,1,0:T(8,128)(2,1)S(1)}, u32[]{:S(2)}) copy-start(bf16[3,128,128]{2,1,0:T(8,128)(2,1)S(1)} %collective-permute-done.14.refs_5_) | copy-start | bytes 294916
  157.6 6.3 %collective-permute-start.16 = (bf16[3,128,128]{2,1,0:T(8,128)(2,1)}, bf16[3,128,128]{2,1,0:T(8,128)(2,1)S(1)}, u32[]{:S(2)}, u32[]{:S(2)}) collective-permute-start(bf16[3,128,128]{2,1,0:T(8,128)(2,1)} %get-tuple-element.52), channel_id=1, source_target_pairs={{0,28},{1,29},{2,30},{3,31},{4,0},{5,1},{6,2},{7,3},{8,4},{9,5},{1... | collective-permute-start | bytes 294920 | tf_op jit(solution)/shard_map/ppermute | solution.py:389
  161.3 15.2 %copy-start.7 = (bf16[3,128,128]{2,1,0:T(8,128)(2,1)}, bf16[3,128,128]{2,1,0:T(8,128)(2,1)S(1)}, u32[]{:S(2)}) copy-start(bf16[3,128,128]{2,1,0:T(8,128)(2,1)S(1)} %collective-permute-done.15.refs_6_) | copy-start | bytes 294916
  163.9 0.6 copy-start.8
  163.9 1.5 copy-start
  164.5 0.9 copy-start.1
  170.5 26.0 %all-to-all-start.3 = ((bf16[8,3,128,128]{3,2,1,0:T(8,128)(2,1)}), bf16[8,3,128,128]{3,2,1,0:T(8,128)(2,1)S(1)}, u32[]{:S(2)}, u32[]{:S(2)}) async-start(bf16[8,3,128,128]{3,2,1,0:T(8,128)(2,1)} %bitcast.159), calls=%async_computation.3 | async-start | bytes 1572864 | tf_op jit(solution)/shard_map/all_to_all | solution.py:406

commit v4 on v3

--- a/solution.py
+++ b/solution.py
@@ -144,50 +144,63 @@
     left = query_at < HEAD_DIM
     scale = HEAD_DIM ** -0.5
     group = 4
+    banks = 3
+    chain = 4
 
     def fold(block, op):
         return op(block.reshape(rows // 8, 8, rows), axis=0)
 
-    def one_tile(tile, size):
-        qg = qg_tiles[tile]
-        none = jnp.zeros_like(qg)
-        weights = jnp.concatenate([jnp.where(left, qg, none), jnp.where(left, none, qg)], axis=0)
-        codes = [code_ref[tile * entries + entry] for entry in range(size)]
-        slots = [code // 4 for code in codes]
-        top = jnp.full((8, rows), HIDDEN, jnp.float32)
-        for start in range(0, size, group):
-            kv = jnp.concatenate([table[slot] for slot in slots[start : start + group]], axis=0)
+    class Tile:
+        def __init__(self, tile, size, bank):
+            self.tile = tile
+            self.first = bank * entries
+            qg = qg_tiles[tile]
+            none = jnp.zeros_like(qg)
+            self.weights = jnp.concatenate([jnp.where(left, qg, none), jnp.where(left, none, qg)], axis=0)
+            self.codes = [code_ref[tile * entries + entry] for entry in range(size)]
+            self.slots = [code // 4 for code in self.codes]
+            self.top = jnp.full((8, rows), HIDDEN, jnp.float32)
+            self.total = jnp.zeros((8, rows), jnp.float32)
+            self.mixed = self.total
+            self.attended = jnp.zeros((HEAD_DIM, rows), jnp.float32)
+            self.grad_query = self.attended
+
+        def score(self, start):
+            kv = jnp.concatenate([table[slot] for slot in self.slots[start : start + group]], axis=0)
             both = lax.dot_general(
-                kv, weights, (((1,), (1,)), ((), ())), preferred_element_type=jnp.float32
+                kv, self.weights, (((1,), (1,)), ((), ())), preferred_element_type=jnp.float32
             )
             for at in range(group):
                 entry = start + at
                 part = both[at * rows : (at + 1) * rows]
-                masked = part[:, :rows] + masks[codes[entry] % 4]
-                scores[entry] = masked
-                dprobs[entry] = part[:, rows:]
-                top = jnp.maximum(top, fold(masked, jnp.max))
-        row_top = jnp.max(top, axis=0, keepdims=True)
-        total = jnp.zeros((8, rows), jnp.float32)
-        mixed = total
-        for entry in range(size):
-            prob = jnp.exp2((scores[entry] - row_top) * (scale * LOG2E))
-            scores[entry] = prob
-            total = total + fold(prob, jnp.sum)
-            mixed = mixed + fold(prob * dprobs[entry], jnp.sum)
-        inverse = 1.0 / jnp.sum(total, axis=0, keepdims=True)
-        delta = jnp.sum(mixed, axis=0, keepdims=True) * inverse
-        attended = jnp.zeros((HEAD_DIM, rows), jnp.float32)
-        grad_query = attended
-        for start in range(0, size, group):
+                masked = part[:, :rows] + masks[self.codes[entry] % 4]
+                scores[self.first + entry] = masked
+                dprobs[self.first + entry] = part[:, rows:]
+                self.top = jnp.maximum(self.top, fold(masked, jnp.max))
+
+        def score_end(self):
+            self.row_top = jnp.max(self.top, axis=0, keepdims=True)
+
+        def exp(self, start):
+            for entry in range(self.first + start, self.first + start + group):
+                prob = jnp.exp2((scores[entry] - self.row_top) * (scale * LOG2E))
+                scores[entry] = prob
+                self.total = self.total + fold(prob, jnp.sum)
+                self.mixed = self.mixed + fold(prob * dprobs[entry], jnp.sum)
+
+        def exp_end(self):
+            self.inverse = 1.0 / jnp.sum(self.total, axis=0, keepdims=True)
+            self.delta = jnp.sum(self.mixed, axis=0, keepdims=True) * self.inverse
+
+        def grad(self, start):
             parts = []
-            for entry in range(start, start + group):
-                prob = scores[entry] * inverse
-                dscore = prob * (dprobs[entry] - delta)
+            for entry in range(self.first + start, self.first + start + group):
+                prob = scores[entry] * self.inverse
+                dscore = prob * (dprobs[entry] - self.delta)
                 parts.append(jnp.concatenate([dscore, prob], axis=1).astype(jnp.bfloat16))
             both = jnp.concatenate(parts, axis=0)
-            chosen = slots[start : start + group]
-            added = jnp.dot(both, weights, preferred_element_type=jnp.float32)
+            chosen = self.slots[start : start + group]
+            added = jnp.dot(both, self.weights, preferred_element_type=jnp.float32)
             before = [totals[slot] for slot in chosen]
             for at in range(group):
                 totals[chosen[at]] = before[at] + added[at * rows : (at + 1) * rows]
@@ -195,22 +208,48 @@
             back = lax.dot_general(
                 kv, both, (((0,), (0,)), ((), ())), preferred_element_type=jnp.float32
             )
-            attended = attended + back[HEAD_DIM:, rows:]
-            grad_query = grad_query + back[:HEAD_DIM, :rows]
-        joined = jnp.concatenate([attended, grad_query * scale], axis=0)
-        qg_tiles[tile] = joined.T.astype(qg_tiles.dtype)
-
-    def tile_step(tile, carry):
-        count = count_ref[tile]
+            self.attended = self.attended + back[HEAD_DIM:, rows:]
+            self.grad_query = self.grad_query + back[:HEAD_DIM, :rows]
+
+        def grad_end(self):
+            joined = jnp.concatenate([self.attended, self.grad_query * scale], axis=0)
+            qg_tiles[self.tile] = joined.T.astype(qg_tiles.dtype)
+
+    def run_chain(ids, size):
+        live = []
+        for at in range(len(ids) + 2):
+            if at < len(ids):
+                live.append(Tile(ids[at], size, at % banks))
+            ready = [live[at - back] if 0 <= at - back < len(ids) else None for back in range(3)]
+            for start in range(0, size, group):
+                if ready[2]:
+                    ready[2].grad(start)
+                if ready[1]:
+                    ready[1].exp(start)
+                if ready[0]:
+                    ready[0].score(start)
+            if ready[2]:
+                ready[2].grad_end()
+            if ready[1]:
+                ready[1].exp_end()
+            if ready[0]:
+                ready[0].score_end()
+
+    def chain_step(step, carry):
+        first = (step // tile_dev) * chain * tile_dev + step % tile_dev
+        ids = [first + at * tile_dev for at in range(chain)]
+        count = count_ref[ids[0]]
+        for tile in ids[1:]:
+            count = jnp.maximum(count, count_ref[tile])
         for size in range(group, entries + 1, group):
 
             @pl.when((count > size - group) & (count <= size))
             def _():
-                one_tile(tile, size)
+                run_chain(ids, size)
 
         return carry
 
-    lax.fori_loop(0, tiles, tile_step, 0)
+    lax.fori_loop(0, tiles // chain, chain_step, 0)
     copies = [
         pltpu.make_async_copy(z_part(at), ref, sems.at[ys + 1 + at])
         for at, ref in enumerate(odq_refs)
@@ -232,49 +271,60 @@
         copy.wait()
 
 
-def combine_kernel(*refs, ys, far, zs, tile_dev):
+def combine_kernel(*refs, ys, groups, zs, tile_dev):
     rank_ref = refs[0]
     near_refs = refs[1 : 1 + ys]
     far_ref, out_ref, near, far_tiles, sums, sems = refs[1 + ys :]
-    tiles = zs * tile_dev
-    copies = [
-        pltpu.make_async_copy(ref, near.at[at], sems.at[at]) for at, ref in enumerate(near_refs)
-    ]
-    copies.append(pltpu.make_async_copy(far_ref, far_tiles, sems.at[ys]))
-    for copy in copies:
-        copy.start()
-    for copy in copies:
-        copy.wait()
-
-    def add_near(at, carry):
-        total = near[0, at].astype(jnp.float32)
-        for y in range(1, ys):
-            total = total + near[y, at].astype(jnp.float32)
-        sums[at] = total
+    halves = 2
+    span = zs // halves
+    copies = []
+    for half in range(halves):
+        part = pl.ds(half * span * tile_dev, span * tile_dev)
+        copies.append(
+            [
+                pltpu.make_async_copy(ref.at[part], near.at[at, part], sems.at[half, at])
+                for at, ref in enumerate(near_refs)
+            ]
+            + [
+                pltpu.make_async_copy(
+                    far_ref.at[:, pl.ds(half * span, span)],
+                    far_tiles.at[:, pl.ds(half * span, span)],
+                    sems.at[half, ys],
+                )
+            ]
+        )
+    for batch in copies:
+        for copy in batch:
+            copy.start()
+
+    def z_step(z, carry):
+        first = z * tile_dev
+        for rank in range(tile_dev):
+            total = near[0, first + rank].astype(jnp.float32)
+            for y in range(1, ys):
+                total = total + near[y, first + rank].astype(jnp.float32)
+            sums[first + rank] = total
+        for group in range(groups):
+            rank = rank_ref[group * zs + z]
+
+            @pl.when(rank >= 0)
+            def _():
+                sums[first + rank] = sums[first + rank] + far_tiles[group, z].astype(jnp.float32)
+
+        for rank in range(tile_dev):
+            near[0, first + rank] = sums[first + rank].astype(near.dtype)
         return carry
 
-    lax.fori_loop(0, tiles, add_near, 0, unroll=2)
-
-    def add_far(at, carry):
-        rank = rank_ref[at]
-
-        @pl.when(rank >= 0)
-        def _():
-            slot = (at % zs) * tile_dev + rank
-            sums[slot] = sums[slot] + far_tiles[at].astype(jnp.float32)
-
-        return carry
-
-    lax.fori_loop(0, far, add_far, 0)
-
-    def write(at, carry):
-        near[0, at] = sums[at].astype(near.dtype)
-        return carry
-
-    lax.fori_loop(0, tiles, write, 0, unroll=4)
-    copy = pltpu.make_async_copy(near.at[0], out_ref, sems.at[0])
-    copy.start()
-    copy.wait()
+    outs = []
+    for half in range(halves):
+        for copy in copies[half]:
+            copy.wait()
+        lax.fori_loop(half * span, (half + 1) * span, z_step, 0)
+        part = pl.ds(half * span * tile_dev, span * tile_dev)
+        outs.append(pltpu.make_async_copy(near.at[0, part], out_ref.at[part], sems.at[half, ys + 1]))
+        outs[-1].start()
+    for copy in outs:
+        copy.wait()
 
 
 def pin(source):
@@ -442,13 +492,13 @@
         scratch_shapes=[
             pltpu.VMEM((slots, rows, 128), bf16),
             pltpu.VMEM((slots, rows, 128), jnp.float32),
-            pltpu.VMEM((entries, rows, rows), jnp.float32),
-            pltpu.VMEM((entries, rows, rows), jnp.float32),
+            pltpu.VMEM((3 * entries, rows, rows), jnp.float32),
+            pltpu.VMEM((3 * entries, rows, rows), jnp.float32),
             pltpu.VMEM((3, rows, rows), jnp.float32),
             scratch(block_shape),
             pltpu.SemaphoreType.DMA((ys + 1 + zs,)),
         ],
-        compiler_params=limits(40),
+        compiler_params=limits(48),
     )(code, count, z_at, kv, *map(pin, near_kv[1:]), far_kv, *map(pin, qg))
     odq, dkv_parts = list(parts[:zs]), parts[zs:]
 
@@ -457,18 +507,18 @@
     odq[1:] = [shift_z(odq[shift], shift) for shift in range(1, zs)]
     last_rank, *odq[1:] = lax.optimization_barrier((far_rank, *odq[1:]))
     dkv = pl.pallas_call(
-        functools.partial(combine_kernel, ys=ys, far=far, zs=zs, tile_dev=tile_dev),
+        functools.partial(combine_kernel, ys=ys, groups=groups, zs=zs, tile_dev=tile_dev),
         out_shape=block_shape,
         in_specs=smem(1) + hbm(ys + 1),
         out_specs=hbm(1)[0],
         scratch_shapes=[
             pltpu.VMEM((ys, tiles, rows, 128), bf16),
-            scratch(far_shape),
+            pltpu.VMEM((groups, zs, rows, 128), bf16),
             scratch(block_shape, jnp.float32),
-            pltpu.SemaphoreType.DMA((ys + 1,)),
+            pltpu.SemaphoreType.DMA((2, ys + 2)),
         ],
         compiler_params=limits(24),
-    )(last_rank, *map(pin, near_back), far_back)
+    )(last_rank, *map(pin, near_back), far_back.reshape(groups, zs, rows, 128))
     attended, grad_queries = unpack_apart(odq)
     grad_keys, grad_values = unpack(over_z(dkv))
     return attended, grad_queries, grad_keys, grad_values

time: 199 us -> 189 us (0.950)
  Pallas kernels: 49.8 us -> 41.5 us
    pallas_call x1, Pallas kernels: 34.5 us -> 27.4 us  [per_device(): pl.pallas_call(functools.partial(attend_kernel, tiles=tiles, entries=entr...]
    ppermute x14, starting transfers between devices: 23 us -> 26.6 us  [shift_z(): return lax.ppermute(source, 'seq', pairs)]
    ppermute x14, waiting for transfers between devices: 45.3 us -> 42.8 us  [shift_z(): return lax.ppermute(source, 'seq', pairs)]
  transfers between devices with their start and end apart: 24 -> 24, of which waited for: 14 -> 13; matrix products, arithmetic and copies ran while one was open for 1% -> 1% of each run, Pallas kernels for 2% -> 3%
where the time goes in v4:
time: 189 us
  waiting for transfers between devices  83.9 us (44%)
  starting transfers between devices  59.2 us (31%)
  Pallas kernels  41.5 us (22%)
  local copies, waits for them, and re-layouts  2.43 us (1%)
    ppermute x14, waiting for transfers between devices, shift_z(): return lax.ppermute(source, 'seq', pairs)  42.8 us
    all_to_all x2, waiting for transfers between devices, over_z(): lax.all_to_all(source.reshape(head_shape.shape), 'seq', split_axis=0, con...  41.1 us
    pallas_call x1, Pallas kernels, per_device(): pl.pallas_call(functools.partial(attend_kernel, tiles=tiles, entries=entr...  27.4 us
    ppermute x14, starting transfers between devices, shift_z(): return lax.ppermute(source, 'seq', pairs)  26.6 us
    all_to_all x2, starting transfers between devices, over_z(): lax.all_to_all(source.reshape(head_shape.shape), 'seq', split_axis=0, con...  13.3 us
    all_to_all x2, starting transfers between devices, over_groups(): lax.all_to_all(source, 'grp', split_axis=0, concat_axis=0, tiled=True)  12 us
    ppermute x6, starting transfers between devices, over_y(): return lax.ppermute(source, 'seq', pairs)  7.35 us
    pallas_call x1, Pallas kernels, per_device(): pl.pallas_call(functools.partial(combine_kernel, ys=ys, groups=groups, zs...  3.94 us
  transfers between devices with their start and end apart: 24, of which 13 were waited for; matrix products, arithmetic and copies ran while one was open for 1% of the time, Pallas kernels for 3%

profile of v4, /device:TPU:10, one launch (start us, length us, event | category | flops | bytes accessed | tf_op | source)
XLA Modules:
  0.0 188.9 jit_solution(17822163398710469977)
XLA Ops:
  0.7 2.3 %shard_map.93 = bf16[8,3,128,128]{3,2,1,0:T(8,128)(2,1)} custom-call(bf16[3,128,512]{2,1,0:T(8,128)(2,1)} %bitcast.167, bf16[3,128,512]{2,1,0:T(8,128)(2,1)} %bitcast.168), custom_call_target="tpu_custom_call" | custom-call | tf_op jit(solution)/shard_map/pallas_call | solution.py:401
  3.0 8.5 %all-to-all-start = ((bf16[8,3,128,128]{3,2,1,0:T(8,128)(2,1)}), bf16[8,3,128,128]{3,2,1,0:T(8,128)(2,1)S(1)}, u32[]{:S(2)}, u32[]{:S(2)}) async-start(bf16[8,3,128,128]{3,2,1,0:T(8,128)(2,1)} %shard_map.93), calls=%async_computation | async-start | bytes 1572864 | tf_op jit(solution)/shard_map/all_to_all | solution.py:456
  11.5 0.2 copy.57
  11.6 0.2 copy.64
  11.8 0.2 constant_dynamic-slice_fusion
  12.1 0.5 fusion.1
  12.5 0.1 broadcast_select_fusion
  12.6 0.1 select_n.93.rank_ref.refs_0_
  12.7 21.9 %all-to-all-done = bf16[8,3,128,128]{3,2,1,0:T(8,128)(2,1)S(1)} async-done(((bf16[8,3,128,128]{3,2,1,0:T(8,128)(2,1)}), bf16[8,3,128,128]{3,2,1,0:T(8,128)(2,1)S(1)}, u32[]{:S(2)}, u32[]{:S(2)}) %all-to-all-start) | async-done | bytes 786464 | tf_op jit(solution)/shard_map/all_to_all | solution.py:456
  34.6 1.9 %shard_map.94 = bf16[64,128,128]{2,1,0:T(8,128)(2,1)} custom-call(s32[64]{0:T(128)S(1)} %select_n.93.rank_ref.refs_0_, bf16[24,128,128]{2,1,0:T(8,128)(2,1)S(1)} %bitcast.156), custom_call_target="tpu_custom_call" | custom-call | tf_op jit(solution)/shard_map/pallas_call | solution.py:475
  36.5 4.8 %all-to-all-start.1 = ((bf16[64,128,128]{2,1,0:T(8,128)(2,1)}), bf16[64,128,128]{2,1,0:T(8,128)(2,1)S(1)}, u32[]{:S(2)}, u32[]{:S(2)}) async-start(bf16[64,128,128]{2,1,0:T(8,128)(2,1)} %shard_map.94), calls=%async_computation.1 | async-start | bytes 4194304 | tf_op jit(solution)/shard_map/all_to_all | solution.py:466
  41.3 1.6 collective-permute-start.2
  42.9 0.9 collective-permute-start.1
  43.8 2.4 %collective-permute-start = (bf16[24,128,128]{2,1,0:T(8,128)(2,1)S(1)}, bf16[24,128,128]{2,1,0:T(8,128)(2,1)}, u32[]{:S(2)}, u32[]{:S(2)}) collective-permute-start(bf16[24,128,128]{2,1,0:T(8,128)(2,1)S(1)} %bitcast.159), channel_id=1, source_target_pairs={{0,3},{1,0},{2,1},{3,2},{4,7},{5,4},{6,5},{7,6},{8,11},{9,8},{10,9... | collective-permute-start | bytes 2359304 | tf_op jit(solution)/shard_map/ppermute | solution.py:470
  46.3 2.3 %shard_map.95 = (bf16[3,128,128]{2,1,0:T(8,128)(2,1)}, bf16[3,128,128]{2,1,0:T(8,128)(2,1)}, bf16[3,128,128]{2,1,0:T(8,128)(2,1)}, bf16[3,128,128]{2,1,0:T(8,128...) custom-call(s32[1]{0:T(128)} %bitcast.z_ref.refs_2_, ...), custom_call_target="tpu_custom_call" | custom-call | tf_op jit(solution)/shard_map/pallas_call | solution.py:414
  48.6 0.6 collective-permute-start.3
  49.2 0.0 collective-permute-start.4
  49.2 7.5 %collective-permute-done.3.refs_9_ = bf16[3,128,128]{2,1,0:T(8,128)(2,1)S(1)} collective-permute-done((bf16[3,128,128]{2,1,0:T(8,128)(2,1)}, bf16[3,128,128]{2,1,0:T(8,128)(2,1)S(1)}, u32[]{:S(2)}, u32[]{:S(2)}) %collective-permute-start.3) | collective-permute-done | bytes 98336 | tf_op jit(solution)/shard_map/ppermute | solution.py:439
  56.7 0.0 collective-permute-start.5
  56.7 4.2 %collective-permute-done.4.refs_10_ = bf16[3,128,128]{2,1,0:T(8,128)(2,1)S(1)} collective-permute-done((bf16[3,128,128]{2,1,0:T(8,128)(2,1)}, bf16[3,128,128]{2,1,0:T(8,128)(2,1)S(1)}, u32[]{:S(2)}, u32[]{:S(2)}) %collective-permute-start.4) | collective-permute-done | bytes 98336 | tf_op jit(solution)/shard_map/ppermute | solution.py:439
  60.9 0.0 collective-permute-start.6
  60.9 6.5 %collective-permute-done.5.refs_11_ = bf16[3,128,128]{2,1,0:T(8,128)(2,1)S(1)} collective-permute-done((bf16[3,128,128]{2,1,0:T(8,128)(2,1)}, bf16[3,128,128]{2,1,0:T(8,128)(2,1)S(1)}, u32[]{:S(2)}, u32[]{:S(2)}) %collective-permute-start.5) | collective-permute-done | bytes 98336 | tf_op jit(solution)/shard_map/ppermute | solution.py:439
  67.4 1.9 %collective-permute-start.7 = (bf16[3,128,128]{2,1,0:T(8,128)(2,1)}, bf16[3,128,128]{2,1,0:T(8,128)(2,1)}, u32[]{:S(2)}, u32[]{:S(2)}) collective-permute-start(bf16[3,128,128]{2,1,0:T(8,128)(2,1)} %get-tuple-element.42), channel_id=1, source_target_pairs={{0,20},{1,21},{2,22},{3,23},{4,24},{5,25},{6,26},{7,27},{8,28},{9,... | collective-permute-start | bytes 294920 | tf_op jit(solution)/shard_map/ppermute | solution.py:439
  69.3 0.1 convert_reduce_fusion
  69.5 0.1 copy.67
  69.5 0.1 reshape.96.refs_1_
  69.6 0.5 collective-permute-done.6.refs_12_
  70.1 0.0 collective-permute-start.8
  70.1 6.8 %collective-permute-done.7.refs_13_ = bf16[3,128,128]{2,1,0:T(8,128)(2,1)} collective-permute-done((bf16[3,128,128]{2,1,0:T(8,128)(2,1)}, bf16[3,128,128]{2,1,0:T(8,128)(2,1)}, u32[]{:S(2)}, u32[]{:S(2)}) %collective-permute-start.7) | collective-permute-done | bytes 98336 | tf_op jit(solution)/shard_map/ppermute | solution.py:439
  76.9 0.0 collective-permute-start.9
  77.0 0.1 reshape.95.refs_0_
  77.1 0.5 collective-permute-done.8.refs_14_
  77.6 4.3 %collective-permute-done.9.refs_15_ = bf16[3,128,128]{2,1,0:T(8,128)(2,1)} collective-permute-done((bf16[3,128,128]{2,1,0:T(8,128)(2,1)}, bf16[3,128,128]{2,1,0:T(8,128)(2,1)}, u32[]{:S(2)}, u32[]{:S(2)}) %collective-permute-start.9) | collective-permute-done | bytes 98336 | tf_op jit(solution)/shard_map/ppermute | solution.py:439
  81.9 0.0 collective-permute-done.2.refs_6_
  81.9 0.0 collective-permute-done.refs_4_
  81.9 0.0 all-to-all-done.1.refs_7_
  81.9 27.4 %shard_map.96 = (bf16[3,128,128]{2,1,0:T(8,128)(2,1)}, bf16[3,128,128]{2,1,0:T(8,128)(2,1)}, bf16[3,128,128]{2,1,0:T(8,128)(2,1)}, bf16[3,128,128]{2,1,0:T(8,128...) custom-call(s32[384]{0:T(512)S(1)} %reshape.95.refs_0_, ...), custom_call_target="tpu_custom_call" | custom-call | tf_op jit(solution)/shard_map/pallas_call | solution.py:487
  109.4 7.2 %all-to-all-start.2 = ((bf16[64,128,128]{2,1,0:T(8,128)(2,1)}), bf16[64,128,128]{2,1,0:T(8,128)(2,1)S(1)}, u32[]{:S(2)}, u32[]{:S(2)}) async-start(bf16[64,128,128]{2,1,0:T(8,128)(2,1)} %get-tuple-element.67), calls=%async_computation.2 | async-start | bytes 4194304 | tf_op jit(solution)/shard_map/all_to_all | solution.py:466
  116.6 0.0 collective-permute-start.17
  116.6 2.4 %collective-permute-start.18 = (bf16[24,128,128]{2,1,0:T(8,128)(2,1)}, bf16[24,128,128]{2,1,0:T(8,128)(2,1)S(1)}, u32[]{:S(2)}, u32[]{:S(2)}) collective-permute-start(bf16[24,128,128]{2,1,0:T(8,128)(2,1)} %get-tuple-element.65), channel_id=1, source_target_pairs={{0,2},{1,3},{2,0},{3,1},{4,6},{5,7},{6,4},{7,5},{8,10},{9,11},{10,... | collective-permute-start | bytes 2359304 | tf_op jit(solution)/shard_map/ppermute | solution.py:470
  119.0 0.0 collective-permute-start.19
  119.0 2.5 %collective-permute-start.10 = (bf16[3,128,128]{2,1,0:T(8,128)(2,1)S(1)}, bf16[3,128,128]{2,1,0:T(8,128)(2,1)S(1)}, u32[]{:S(2)}, u32[]{:S(2)}) collective-permute-start(bf16[3,128,128]{2,1,0:T(8,128)(2,1)S(1)} %copy-done.17), channel_id=1, source_target_pairs={{0,4},{1,5},{2,6},{3,7},{4,8},{5,9},{6,10},{7,11},{8,12},{9,13},{1... | collective-permute-start | bytes 294920 | tf_op jit(solution)/shard_map/ppermute | solution.py:439
  121.5 2.1 %collective-permute-start.11 = (bf16[3,128,128]{2,1,0:T(8,128)(2,1)S(1)}, bf16[3,128,128]{2,1,0:T(8,128)(2,1)S(1)}, u32[]{:S(2)}, u32[]{:S(2)}) collective-permute-start(bf16[3,128,128]{2,1,0:T(8,128)(2,1)S(1)} %copy-done.16), channel_id=1, source_target_pairs={{0,8},{1,9},{2,10},{3,11},{4,12},{5,13},{6,14},{7,15},{8,16},{9,17... | collective-permute-start | bytes 294920 | tf_op jit(solution)/shard_map/ppermute | solution.py:439
  123.5 1.3 collective-permute-done.10.refs_1_
  124.8 4.1 %collective-permute-start.12 = (bf16[3,128,128]{2,1,0:T(8,128)(2,1)S(1)}, bf16[3,128,128]{2,1,0:T(8,128)(2,1)S(1)}, u32[]{:S(2)}, u32[]{:S(2)}) collective-permute-start(bf16[3,128,128]{2,1,0:T(8,128)(2,1)S(1)} %copy-done.15), channel_id=1, source_target_pairs={{0,12},{1,13},{2,14},{3,15},{4,16},{5,17},{6,18},{7,19},{8,20},{9,... | collective-permute-start | bytes 294920 | tf_op jit(solution)/shard_map/ppermute | solution.py:439
  128.9 0.0 collective-permute-done.11.refs_2_
  128.9 5.3 %collective-permute-start.13 = (bf16[3,128,128]{2,1,0:T(8,128)(2,1)S(1)}, bf16[3,128,128]{2,1,0:T(8,128)(2,1)S(1)}, u32[]{:S(2)}, u32[]{:S(2)}) collective-permute-start(bf16[3,128,128]{2,1,0:T(8,128)(2,1)S(1)} %copy-done.14), channel_id=1, source_target_pairs={{0,16},{1,17},{2,18},{3,19},{4,20},{5,21},{6,22},{7,23},{8,24},{9,... | collective-permute-start | bytes 294920 | tf_op jit(solution)/shard_map/ppermute | solution.py:439
  134.3 4.6 %collective-permute-done.12.refs_3_ = bf16[3,128,128]{2,1,0:T(8,128)(2,1)S(1)} collective-permute-done((bf16[3,128,128]{2,1,0:T(8,128)(2,1)S(1)}, bf16[3,128,128]{2,1,0:T(8,128)(2,1)S(1)}, u32[]{:S(2)}, u32[]{:S(2)}) %collective-permute-start.12) | collective-permute-done | bytes 98336 | tf_op jit(solution)/shard_map/ppermute | solution.py:439
  138.9 3.2 %collective-permute-start.14 = (bf16[3,128,128]{2,1,0:T(8,128)(2,1)}, bf16[3,128,128]{2,1,0:T(8,128)(2,1)S(1)}, u32[]{:S(2)}, u32[]{:S(2)}) collective-permute-start(bf16[3,128,128]{2,1,0:T(8,128)(2,1)} %get-tuple-element.50), channel_id=1, source_target_pairs={{0,20},{1,21},{2,22},{3,23},{4,24},{5,25},{6,26},{7,27},{8,28},{9,... | collective-permute-start | bytes 294920 | tf_op jit(solution)/shard_map/ppermute | solution.py:439
  142.1 0.0 collective-permute-done.13.refs_4_
  142.1 2.0 %collective-permute-start.15 = (bf16[3,128,128]{2,1,0:T(8,128)(2,1)}, bf16[3,128,128]{2,1,0:T(8,128)(2,1)S(1)}, u32[]{:S(2)}, u32[]{:S(2)}) collective-permute-start(bf16[3,128,128]{2,1,0:T(8,128)(2,1)} %get-tuple-element.51), channel_id=1, source_target_pairs={{0,24},{1,25},{2,26},{3,27},{4,28},{5,29},{6,30},{7,31},{8,0},{9,1... | collective-permute-start | bytes 294920 | tf_op jit(solution)/shard_map/ppermute | solution.py:439
  144.1 4.1 %collective-permute-done.14.refs_5_ = bf16[3,128,128]{2,1,0:T(8,128)(2,1)S(1)} collective-permute-done((bf16[3,128,128]{2,1,0:T(8,128)(2,1)}, bf16[3,128,128]{2,1,0:T(8,128)(2,1)S(1)}, u32[]{:S(2)}, u32[]{:S(2)}) %collective-permute-start.14) | collective-permute-done | bytes 98336 | tf_op jit(solution)/shard_map/ppermute | solution.py:439
  148.2 4.9 %collective-permute-start.16 = (bf16[3,128,128]{2,1,0:T(8,128)(2,1)}, bf16[3,128,128]{2,1,0:T(8,128)(2,1)S(1)}, u32[]{:S(2)}, u32[]{:S(2)}) collective-permute-start(bf16[3,128,128]{2,1,0:T(8,128)(2,1)} %get-tuple-element.52), channel_id=1, source_target_pairs={{0,28},{1,29},{2,30},{3,31},{4,0},{5,1},{6,2},{7,3},{8,4},{9,5},{1... | collective-permute-start | bytes 294920 | tf_op jit(solution)/shard_map/ppermute | solution.py:439
  153.1 0.0 collective-permute-done.15.refs_6_
  153.1 2.5 %collective-permute-done.16.refs_7_ = bf16[3,128,128]{2,1,0:T(8,128)(2,1)S(1)} collective-permute-done((bf16[3,128,128]{2,1,0:T(8,128)(2,1)}, bf16[3,128,128]{2,1,0:T(8,128)(2,1)S(1)}, u32[]{:S(2)}, u32[]{:S(2)}) %collective-permute-start.16) | collective-permute-done | bytes 98336 | tf_op jit(solution)/shard_map/ppermute | solution.py:439
  155.6 0.6 copy-done.8
  156.2 0.9 copy-done.1
  157.1 0.0 collective-permute-done.19.refs_4_
  157.1 0.0 all-to-all-done.2
  157.1 3.9 %shard_map.98 = bf16[24,128,128]{2,1,0:T(8,128)(2,1)} custom-call(s32[64]{0:T(128)S(1)} %select_n.93.rank_ref.refs_0_, bf16[24,128,128]{2,1,0:T(8,128)(2,1)} %get-tuple-element.63.refs_1_, bf16[24,128,128]{2,1,0:T(8,128)(2,1)} %copy-done, bf16[24,128,128]{2,1,0:T(8,128)(2,1)} %copy-done.1, bf16[24,128,128]{2,1,0:T(8,128)(2,1)} %collective-permute-done.19.refs_4_, ...), custom_call_target="tpu_custom_call" | custom-call | tf_op jit(solution)/shard_map/pallas_call | solution.py:509
  161.1 4.8 %all-to-all-start.3 = ((bf16[8,3,128,128]{3,2,1,0:T(8,128)(2,1)}), bf16[8,3,128,128]{3,2,1,0:T(8,128)(2,1)S(1)}, u32[]{:S(2)}, u32[]{:S(2)}) async-start(bf16[8,3,128,128]{3,2,1,0:T(8,128)(2,1)} %bitcast.161), calls=%async_computation.3 | async-start | bytes 1572864 | tf_op jit(solution)/shard_map/all_to_all | solution.py:456
  165.9 2.4 %shard_map.97 = (bf16[3,128,512]{2,1,0:T(8,128)(2,1)}, bf16[3,128,512]{2,1,0:T(8,128)(2,1)}) custom-call(s32[1]{0:T(128)} %bitcast.z_ref.refs_2_, bf16[3,128,128]{2,1,0:T(8,128)(2,1)} %get-tuple-element.45.refs_0_, bf16[3,128,128]{2,1,0:T(8,128)(2,1)} %copy-done.2, bf16[3,128,128]{2,1,0:T(8,128)(2,1)} %copy-done.3, bf16[3,128,128]{2,1,0:T(8,128)(2,1)} %copy-done.4, ...), custom_call_target="tpu_custom_call" | custom-call | tf_op jit(solution)/shard_map/pallas_call | solution.py:424
  168.3 19.2 %all-to-all-done.3.in_ref = bf16[8,3,128,128]{3,2,1,0:T(8,128)(2,1)S(1)} async-done(((bf16[8,3,128,128]{3,2,1,0:T(8,128)(2,1)}), bf16[8,3,128,128]{3,2,1,0:T(8,128)(2,1)S(1)}, u32[]{:S(2)}, u32[]{:S(2)}) %all-to-all-start.3) | async-done | bytes 786464 | tf_op jit(solution)/shard_map/all_to_all | solution.py:456
  187.5 1.2 shard_map.99
  (42 shorter events, 0.1 us)
Async XLA Ops:
  0.6 10.8 %copy-start.12 = (s32[768,16]{0,1:T(8,128)S(1)}, s32[768,16]{0,1:T(8,128)}, u32[]{:S(2)}) copy-start(s32[768,16]{0,1:T(8,128)} %param.10) | copy-start | bytes 147460
  0.6 11.0 %copy-start.13 = (s32[768,16]{0,1:T(8,128)S(1)}, s32[768,16]{0,1:T(8,128)}, u32[]{:S(2)}) copy-start(s32[768,16]{0,1:T(8,128)} %param.11) | copy-start | bytes 147460
  3.0 31.6 %all-to-all-start = ((bf16[8,3,128,128]{3,2,1,0:T(8,128)(2,1)}), bf16[8,3,128,128]{3,2,1,0:T(8,128)(2,1)S(1)}, u32[]{:S(2)}, u32[]{:S(2)}) async-start(bf16[8,3,128,128]{3,2,1,0:T(8,128)(2,1)} %shard_map.93), calls=%async_computation | async-start | bytes 1572864 | tf_op jit(solution)/shard_map/all_to_all | solution.py:456
  36.5 45.4 %all-to-all-start.1 = ((bf16[64,128,128]{2,1,0:T(8,128)(2,1)}), bf16[64,128,128]{2,1,0:T(8,128)(2,1)S(1)}, u32[]{:S(2)}, u32[]{:S(2)}) async-start(bf16[64,128,128]{2,1,0:T(8,128)(2,1)} %shard_map.94), calls=%async_computation.1 | async-start | bytes 4194304 | tf_op jit(solution)/shard_map/all_to_all | solution.py:466
  41.3 40.6 %collective-permute-start.2 = (bf16[24,128,128]{2,1,0:T(8,128)(2,1)S(1)}, bf16[24,128,128]{2,1,0:T(8,128)(2,1)}, u32[]{:S(2)}, u32[]{:S(2)}) collective-permute-start(bf16[24,128,128]{2,1,0:T(8,128)(2,1)S(1)} %bitcast.157), channel_id=1, source_target_pairs={{0,1},{1,2},{2,3},{3,0},{4,5},{5,6},{6,7},{7,4},{8,9},{9,10},{10,1... | collective-permute-start | bytes 2359304 | tf_op jit(solution)/shard_map/ppermute | solution.py:470
  42.9 39.0 %collective-permute-start.1 = (bf16[24,128,128]{2,1,0:T(8,128)(2,1)S(1)}, bf16[24,128,128]{2,1,0:T(8,128)(2,1)}, u32[]{:S(2)}, u32[]{:S(2)}) collective-permute-start(bf16[24,128,128]{2,1,0:T(8,128)(2,1)S(1)} %bitcast.158), channel_id=1, source_target_pairs={{0,2},{1,3},{2,0},{3,1},{4,6},{5,7},{6,4},{7,5},{8,10},{9,11},{10,... | collective-permute-start | bytes 2359304 | tf_op jit(solution)/shard_map/ppermute | solution.py:470
  43.8 38.0 %collective-permute-start = (bf16[24,128,128]{2,1,0:T(8,128)(2,1)S(1)}, bf16[24,128,128]{2,1,0:T(8,128)(2,1)}, u32[]{:S(2)}, u32[]{:S(2)}) collective-permute-start(bf16[24,128,128]{2,1,0:T(8,128)(2,1)S(1)} %bitcast.159), channel_id=1, source_target_pairs={{0,3},{1,0},{2,1},{3,2},{4,7},{5,4},{6,5},{7,6},{8,11},{9,8},{10,9... | collective-permute-start | bytes 2359304 | tf_op jit(solution)/shard_map/ppermute | solution.py:470
  48.6 8.1 %collective-permute-start.3 = (bf16[3,128,128]{2,1,0:T(8,128)(2,1)}, bf16[3,128,128]{2,1,0:T(8,128)(2,1)S(1)}, u32[]{:S(2)}, u32[]{:S(2)}) collective-permute-start(bf16[3,128,128]{2,1,0:T(8,128)(2,1)} %get-tuple-element.38), channel_id=1, source_target_pairs={{0,4},{1,5},{2,6},{3,7},{4,8},{5,9},{6,10},{7,11},{8,12},{9,13},{1... | collective-permute-start | bytes 294920 | tf_op jit(solution)/shard_map/ppermute | solution.py:439
  49.2 11.7 %collective-permute-start.4 = (bf16[3,128,128]{2,1,0:T(8,128)(2,1)}, bf16[3,128,128]{2,1,0:T(8,128)(2,1)S(1)}, u32[]{:S(2)}, u32[]{:S(2)}) collective-permute-start(bf16[3,128,128]{2,1,0:T(8,128)(2,1)} %get-tuple-element.39), channel_id=1, source_target_pairs={{0,8},{1,9},{2,10},{3,11},{4,12},{5,13},{6,14},{7,15},{8,16},{9,17... | collective-permute-start | bytes 294920 | tf_op jit(solution)/shard_map/ppermute | solution.py:439
  56.7 12.6 %copy-start.9 = (bf16[3,128,128]{2,1,0:T(8,128)(2,1)}, bf16[3,128,128]{2,1,0:T(8,128)(2,1)S(1)}, u32[]{:S(2)}) copy-start(bf16[3,128,128]{2,1,0:T(8,128)(2,1)S(1)} %collective-permute-done.3.refs_9_) | copy-start | bytes 294916
  56.7 10.6 %collective-permute-start.5 = (bf16[3,128,128]{2,1,0:T(8,128)(2,1)}, bf16[3,128,128]{2,1,0:T(8,128)(2,1)S(1)}, u32[]{:S(2)}, u32[]{:S(2)}) collective-permute-start(bf16[3,128,128]{2,1,0:T(8,128)(2,1)} %get-tuple-element.40), channel_id=1, source_target_pairs={{0,12},{1,13},{2,14},{3,15},{4,16},{5,17},{6,18},{7,19},{8,20},{9,... | collective-permute-start | bytes 294920 | tf_op jit(solution)/shard_map/ppermute | solution.py:439
  60.9 8.4 %copy-start.10 = (bf16[3,128,128]{2,1,0:T(8,128)(2,1)}, bf16[3,128,128]{2,1,0:T(8,128)(2,1)S(1)}, u32[]{:S(2)}) copy-start(bf16[3,128,128]{2,1,0:T(8,128)(2,1)S(1)} %collective-permute-done.4.refs_10_) | copy-start | bytes 294916
  60.9 9.2 %collective-permute-start.6 = (bf16[3,128,128]{2,1,0:T(8,128)(2,1)}, bf16[3,128,128]{2,1,0:T(8,128)(2,1)}, u32[]{:S(2)}, u32[]{:S(2)}) collective-permute-start(bf16[3,128,128]{2,1,0:T(8,128)(2,1)} %get-tuple-element.41), channel_id=1, source_target_pairs={{0,16},{1,17},{2,18},{3,19},{4,20},{5,21},{6,22},{7,23},{8,24},{9,... | collective-permute-start | bytes 294920 | tf_op jit(solution)/shard_map/ppermute | solution.py:439
  67.4 1.9 %copy-start.11 = (bf16[3,128,128]{2,1,0:T(8,128)(2,1)}, bf16[3,128,128]{2,1,0:T(8,128)(2,1)S(1)}, u32[]{:S(2)}) copy-start(bf16[3,128,128]{2,1,0:T(8,128)(2,1)S(1)} %collective-permute-done.5.refs_11_) | copy-start | bytes 294916
  67.4 9.6 %collective-permute-start.7 = (bf16[3,128,128]{2,1,0:T(8,128)(2,1)}, bf16[3,128,128]{2,1,0:T(8,128)(2,1)}, u32[]{:S(2)}, u32[]{:S(2)}) collective-permute-start(bf16[3,128,128]{2,1,0:T(8,128)(2,1)} %get-tuple-element.42), channel_id=1, source_target_pairs={{0,20},{1,21},{2,22},{3,23},{4,24},{5,25},{6,26},{7,27},{8,28},{9,... | collective-permute-start | bytes 294920 | tf_op jit(solution)/shard_map/ppermute | solution.py:439
  70.1 7.4 %collective-permute-start.8 = (bf16[3,128,128]{2,1,0:T(8,128)(2,1)}, bf16[3,128,128]{2,1,0:T(8,128)(2,1)}, u32[]{:S(2)}, u32[]{:S(2)}) collective-permute-start(bf16[3,128,128]{2,1,0:T(8,128)(2,1)} %get-tuple-element.43), channel_id=1, source_target_pairs={{0,24},{1,25},{2,26},{3,27},{4,28},{5,29},{6,30},{7,31},{8,0},{9,1... | collective-permute-start | bytes 294920 | tf_op jit(solution)/shard_map/ppermute | solution.py:439
  76.9 4.9 %collective-permute-start.9 = (bf16[3,128,128]{2,1,0:T(8,128)(2,1)}, bf16[3,128,128]{2,1,0:T(8,128)(2,1)}, u32[]{:S(2)}, u32[]{:S(2)}) collective-permute-start(bf16[3,128,128]{2,1,0:T(8,128)(2,1)} %get-tuple-element.44), channel_id=1, source_target_pairs={{0,28},{1,29},{2,30},{3,31},{4,0},{5,1},{6,2},{7,3},{8,4},{9,5},{1... | collective-permute-start | bytes 294920 | tf_op jit(solution)/shard_map/ppermute | solution.py:439
  109.3 9.7 %copy-start.17 = (bf16[3,128,128]{2,1,0:T(8,128)(2,1)S(1)}, bf16[3,128,128]{2,1,0:T(8,128)(2,1)}, u32[]{:S(2)}) copy-start(bf16[3,128,128]{2,1,0:T(8,128)(2,1)} %get-tuple-element.46) | copy-start | bytes 294916
  109.3 12.1 %copy-start.16 = (bf16[3,128,128]{2,1,0:T(8,128)(2,1)S(1)}, bf16[3,128,128]{2,1,0:T(8,128)(2,1)}, u32[]{:S(2)}) copy-start(bf16[3,128,128]{2,1,0:T(8,128)(2,1)} %get-tuple-element.47) | copy-start | bytes 294916
  109.3 15.5 %copy-start.15 = (bf16[3,128,128]{2,1,0:T(8,128)(2,1)S(1)}, bf16[3,128,128]{2,1,0:T(8,128)(2,1)}, u32[]{:S(2)}) copy-start(bf16[3,128,128]{2,1,0:T(8,128)(2,1)} %get-tuple-element.48) | copy-start | bytes 294916
  109.4 19.6 %copy-start.14 = (bf16[3,128,128]{2,1,0:T(8,128)(2,1)S(1)}, bf16[3,128,128]{2,1,0:T(8,128)(2,1)}, u32[]{:S(2)}) copy-start(bf16[3,128,128]{2,1,0:T(8,128)(2,1)} %get-tuple-element.49) | copy-start | bytes 294916
  109.4 47.7 %all-to-all-start.2 = ((bf16[64,128,128]{2,1,0:T(8,128)(2,1)}), bf16[64,128,128]{2,1,0:T(8,128)(2,1)S(1)}, u32[]{:S(2)}, u32[]{:S(2)}) async-start(bf16[64,128,128]{2,1,0:T(8,128)(2,1)} %get-tuple-element.67), calls=%async_computation.2 | async-start | bytes 4194304 | tf_op jit(solution)/shard_map/all_to_all | solution.py:466
  116.6 39.0 %collective-permute-start.17 = (bf16[24,128,128]{2,1,0:T(8,128)(2,1)}, bf16[24,128,128]{2,1,0:T(8,128)(2,1)S(1)}, u32[]{:S(2)}, u32[]{:S(2)}) collective-permute-start(bf16[24,128,128]{2,1,0:T(8,128)(2,1)} %get-tuple-element.64), channel_id=1, source_target_pairs={{0,1},{1,2},{2,3},{3,0},{4,5},{5,6},{6,7},{7,4},{8,9},{9,10},{10,1... | collective-permute-start | bytes 2359304 | tf_op jit(solution)/shard_map/ppermute | solution.py:470
  116.6 39.0 %collective-permute-start.18 = (bf16[24,128,128]{2,1,0:T(8,128)(2,1)}, bf16[24,128,128]{2,1,0:T(8,128)(2,1)S(1)}, u32[]{:S(2)}, u32[]{:S(2)}) collective-permute-start(bf16[24,128,128]{2,1,0:T(8,128)(2,1)} %get-tuple-element.65), channel_id=1, source_target_pairs={{0,2},{1,3},{2,0},{3,1},{4,6},{5,7},{6,4},{7,5},{8,10},{9,11},{10,... | collective-permute-start | bytes 2359304 | tf_op jit(solution)/shard_map/ppermute | solution.py:470
  119.0 38.1 %collective-permute-start.19 = (bf16[24,128,128]{2,1,0:T(8,128)(2,1)}, bf16[24,128,128]{2,1,0:T(8,128)(2,1)}, u32[]{:S(2)}, u32[]{:S(2)}) collective-permute-start(bf16[24,128,128]{2,1,0:T(8,128)(2,1)} %get-tuple-element.66), channel_id=1, source_target_pairs={{0,3},{1,0},{2,1},{3,2},{4,7},{5,4},{6,5},{7,6},{8,11},{9,8},{10,9... | collective-permute-start | bytes 2359304 | tf_op jit(solution)/shard_map/ppermute | solution.py:470
  119.0 5.8 %collective-permute-start.10 = (bf16[3,128,128]{2,1,0:T(8,128)(2,1)S(1)}, bf16[3,128,128]{2,1,0:T(8,128)(2,1)S(1)}, u32[]{:S(2)}, u32[]{:S(2)}) collective-permute-start(bf16[3,128,128]{2,1,0:T(8,128)(2,1)S(1)} %copy-done.17), channel_id=1, source_target_pairs={{0,4},{1,5},{2,6},{3,7},{4,8},{5,9},{6,10},{7,11},{8,12},{9,13},{1... | collective-permute-start | bytes 294920 | tf_op jit(solution)/shard_map/ppermute | solution.py:439
  121.5 7.5 %collective-permute-start.11 = (bf16[3,128,128]{2,1,0:T(8,128)(2,1)S(1)}, bf16[3,128,128]{2,1,0:T(8,128)(2,1)S(1)}, u32[]{:S(2)}, u32[]{:S(2)}) collective-permute-start(bf16[3,128,128]{2,1,0:T(8,128)(2,1)S(1)} %copy-done.16), channel_id=1, source_target_pairs={{0,8},{1,9},{2,10},{3,11},{4,12},{5,13},{6,14},{7,15},{8,16},{9,17... | collective-permute-start | bytes 294920 | tf_op jit(solution)/shard_map/ppermute | solution.py:439
  124.8 41.0 %copy-start.2 = (bf16[3,128,128]{2,1,0:T(8,128)(2,1)}, bf16[3,128,128]{2,1,0:T(8,128)(2,1)S(1)}, u32[]{:S(2)}) copy-start(bf16[3,128,128]{2,1,0:T(8,128)(2,1)S(1)} %collective-permute-done.10.refs_1_) | copy-start | bytes 294916
  124.8 14.1 %collective-permute-start.12 = (bf16[3,128,128]{2,1,0:T(8,128)(2,1)S(1)}, bf16[3,128,128]{2,1,0:T(8,128)(2,1)S(1)}, u32[]{:S(2)}, u32[]{:S(2)}) collective-permute-start(bf16[3,128,128]{2,1,0:T(8,128)(2,1)S(1)} %copy-done.15), channel_id=1, source_target_pairs={{0,12},{1,13},{2,14},{3,15},{4,16},{5,17},{6,18},{7,19},{8,20},{9,... | collective-permute-start | bytes 294920 | tf_op jit(solution)/shard_map/ppermute | solution.py:439
  128.9 36.9 %copy-start.3 = (bf16[3,128,128]{2,1,0:T(8,128)(2,1)}, bf16[3,128,128]{2,1,0:T(8,128)(2,1)S(1)}, u32[]{:S(2)}) copy-start(bf16[3,128,128]{2,1,0:T(8,128)(2,1)S(1)} %collective-permute-done.11.refs_2_) | copy-start | bytes 294916
  128.9 13.2 %collective-permute-start.13 = (bf16[3,128,128]{2,1,0:T(8,128)(2,1)S(1)}, bf16[3,128,128]{2,1,0:T(8,128)(2,1)S(1)}, u32[]{:S(2)}, u32[]{:S(2)}) collective-permute-start(bf16[3,128,128]{2,1,0:T(8,128)(2,1)S(1)} %copy-done.14), channel_id=1, source_target_pairs={{0,16},{1,17},{2,18},{3,19},{4,20},{5,21},{6,22},{7,23},{8,24},{9,... | collective-permute-start | bytes 294920 | tf_op jit(solution)/shard_map/ppermute | solution.py:439
  138.9 26.9 %copy-start.4 = (bf16[3,128,128]{2,1,0:T(8,128)(2,1)}, bf16[3,128,128]{2,1,0:T(8,128)(2,1)S(1)}, u32[]{:S(2)}) copy-start(bf16[3,128,128]{2,1,0:T(8,128)(2,1)S(1)} %collective-permute-done.12.refs_3_) | copy-start | bytes 294916
  138.9 9.3 %collective-permute-start.14 = (bf16[3,128,128]{2,1,0:T(8,128)(2,1)}, bf16[3,128,128]{2,1,0:T(8,128)(2,1)S(1)}, u32[]{:S(2)}, u32[]{:S(2)}) collective-permute-start(bf16[3,128,128]{2,1,0:T(8,128)(2,1)} %get-tuple-element.50), channel_id=1, source_target_pairs={{0,20},{1,21},{2,22},{3,23},{4,24},{5,25},{6,26},{7,27},{8,28},{9,... | collective-permute-start | bytes 294920 | tf_op jit(solution)/shard_map/ppermute | solution.py:439
  142.1 23.8 %copy-start.5 = (bf16[3,128,128]{2,1,0:T(8,128)(2,1)}, bf16[3,128,128]{2,1,0:T(8,128)(2,1)S(1)}, u32[]{:S(2)}) copy-start(bf16[3,128,128]{2,1,0:T(8,128)(2,1)S(1)} %collective-permute-done.13.refs_4_) | copy-start | bytes 294916
  142.1 11.0 %collective-permute-start.15 = (bf16[3,128,128]{2,1,0:T(8,128)(2,1)}, bf16[3,128,128]{2,1,0:T(8,128)(2,1)S(1)}, u32[]{:S(2)}, u32[]{:S(2)}) collective-permute-start(bf16[3,128,128]{2,1,0:T(8,128)(2,1)} %get-tuple-element.51), channel_id=1, source_target_pairs={{0,24},{1,25},{2,26},{3,27},{4,28},{5,29},{6,30},{7,31},{8,0},{9,1... | collective-permute-start | bytes 294920 | tf_op jit(solution)/shard_map/ppermute | solution.py:439
  148.2 17.7 %copy-start.6 = (bf16[3,128,128]{2,1,0:T(8,128)(2,1)}, bf16[3,128,128]{2,1,0:T(8,128)(2,1)S(1)}, u32[]{:S(2)}) copy-start(bf16[3,128,128]{2,1,0:T(8,128)(2,1)S(1)} %collective-permute-done.14.refs_5_) | copy-start | bytes 294916
  148.2 7.4 %collective-permute-start.16 = (bf16[3,128,128]{2,1,0:T(8,128)(2,1)}, bf16[3,128,128]{2,1,0:T(8,128)(2,1)S(1)}, u32[]{:S(2)}, u32[]{:S(2)}) collective-permute-start(bf16[3,128,128]{2,1,0:T(8,128)(2,1)} %get-tuple-element.52), channel_id=1, source_target_pairs={{0,28},{1,29},{2,30},{3,31},{4,0},{5,1},{6,2},{7,3},{8,4},{9,5},{1... | collective-permute-start | bytes 294920 | tf_op jit(solution)/shard_map/ppermute | solution.py:439
  153.1 12.8 %copy-start.7 = (bf16[3,128,128]{2,1,0:T(8,128)(2,1)}, bf16[3,128,128]{2,1,0:T(8,128)(2,1)S(1)}, u32[]{:S(2)}) copy-start(bf16[3,128,128]{2,1,0:T(8,128)(2,1)S(1)} %collective-permute-done.15.refs_6_) | copy-start | bytes 294916
  155.6 0.6 copy-start.8
  155.6 1.5 copy-start
  156.2 0.9 copy-start.1
  161.1 26.5 %all-to-all-start.3 = ((bf16[8,3,128,128]{3,2,1,0:T(8,128)(2,1)}), bf16[8,3,128,128]{3,2,1,0:T(8,128)(2,1)S(1)}, u32[]{:S(2)}, u32[]{:S(2)}) async-start(bf16[8,3,128,128]{3,2,1,0:T(8,128)(2,1)} %bitcast.161), calls=%async_computation.3 | async-start | bytes 1572864 | tf_op jit(solution)/shard_map/all_to_all | solution.py:456

commit v5 on v4

--- a/solution.py
+++ b/solution.py
@@ -471,6 +471,7 @@
 
     kv = over_z(pack(key_input, value_input))
     qg = list(pack_apart(queries, grad_output))
+    first_rank, *qg = lax.optimization_barrier((far_rank, *qg))
     near_kv = [kv] + [over_y(kv, -shift) for shift in range(1, ys)]
     far_send = pl.pallas_call(
         functools.partial(far_kernel, far=far, zs=zs, tile_dev=tile_dev),
@@ -479,7 +480,7 @@
         out_specs=hbm(1)[0],
         scratch_shapes=[pltpu.SemaphoreType.DMA],
         compiler_params=limits(8),
-    )(far_rank, kv)
+    )(first_rank, kv)
     far_kv = over_groups(far_send)
     qg[1:] = [shift_z(qg[shift], shift) for shift in range(1, zs)]
 

time: 189 us -> 187 us (0.989)
  starting transfers between devices: 59.2 us -> 53.9 us
  waiting for transfers between devices: 83.9 us -> 87.6 us
    ppermute x14, starting transfers between devices: 26.6 us -> 17.1 us  [shift_z(): return lax.ppermute(source, 'seq', pairs)]
    ppermute x14, waiting for transfers between devices: 42.8 us -> 49.7 us  [shift_z(): return lax.ppermute(source, 'seq', pairs)]
    all_to_all x2, waiting for transfers between devices: 41.1 us -> 37.4 us  [over_z(): lax.all_to_all(source.reshape(head_shape.shape), 'seq', split_axis=0, con...]
    ppermute x6, starting transfers between devices: 7.35 us -> 9.8 us  [over_y(): return lax.ppermute(source, 'seq', pairs)]
  transfers between devices with their start and end apart: 24 -> 24, of which waited for: 13 -> 15; matrix products, arithmetic and copies ran while one was open for 1% -> 1% of each run, Pallas kernels for 3% -> 3%
where the time goes in v5:
time: 187 us; the launch traced here: 186 us
  waiting for transfers between devices  87.6 us (47%)
  starting transfers between devices  53.9 us (29%)
  Pallas kernels  40.7 us (22%)
  local copies, waits for them, and re-layouts  2.45 us (1%)
    ppermute x14, waiting for transfers between devices, shift_z(): return lax.ppermute(source, 'seq', pairs)  49.7 us
    all_to_all x2, waiting for transfers between devices, over_z(): lax.all_to_all(source.reshape(head_shape.shape), 'seq', split_axis=0, con...  37.4 us
    pallas_call x1, Pallas kernels, per_device(): pl.pallas_call(functools.partial(attend_kernel, tiles=tiles, entries=entr...  26.6 us
    ppermute x14, starting transfers between devices, shift_z(): return lax.ppermute(source, 'seq', pairs)  17.1 us
    all_to_all x2, starting transfers between devices, over_z(): lax.all_to_all(source.reshape(head_shape.shape), 'seq', split_axis=0, con...  14.5 us
    all_to_all x2, starting transfers between devices, over_groups(): lax.all_to_all(source, 'grp', split_axis=0, concat_axis=0, tiled=True)  12.6 us
    ppermute x6, starting transfers between devices, over_y(): return lax.ppermute(source, 'seq', pairs)  9.8 us
    pallas_call x1, Pallas kernels, per_device(): pl.pallas_call(functools.partial(combine_kernel, ys=ys, groups=groups, zs...  3.96 us
  transfers between devices with their start and end apart: 24, of which 15 were waited for; matrix products, arithmetic and copies ran while one was open for 1% of the time, Pallas kernels for 3%

profile of v5, /device:TPU:10, one launch (start us, length us, event | category | flops | bytes accessed | tf_op | source)
XLA Modules:
  0.0 186.5 jit_solution(5605325814040162268)
XLA Ops:
  0.7 2.3 %shard_map.93 = bf16[8,3,128,128]{3,2,1,0:T(8,128)(2,1)} custom-call(bf16[3,128,512]{2,1,0:T(8,128)(2,1)} %bitcast.167, bf16[3,128,512]{2,1,0:T(8,128)(2,1)} %bitcast.168), custom_call_target="tpu_custom_call" | custom-call | tf_op jit(solution)/shard_map/pallas_call | solution.py:401
  3.0 8.5 %all-to-all-start = ((bf16[8,3,128,128]{3,2,1,0:T(8,128)(2,1)}), bf16[8,3,128,128]{3,2,1,0:T(8,128)(2,1)S(1)}, u32[]{:S(2)}, u32[]{:S(2)}) async-start(bf16[8,3,128,128]{3,2,1,0:T(8,128)(2,1)} %shard_map.93), calls=%async_computation | async-start | bytes 1572864 | tf_op jit(solution)/shard_map/all_to_all | solution.py:456
  11.5 0.2 copy.57
  11.6 0.2 copy.64
  11.8 0.2 constant_dynamic-slice_fusion
  12.1 0.5 fusion.1
  12.5 0.1 broadcast_select_fusion
  12.6 0.1 select_n.93.rank_ref.refs_0_
  12.7 2.3 %shard_map.94 = (bf16[3,128,128]{2,1,0:T(8,128)(2,1)}, bf16[3,128,128]{2,1,0:T(8,128)(2,1)}, bf16[3,128,128]{2,1,0:T(8,128)(2,1)}, bf16[3,128,128]{2,1,0:T(8,128...) custom-call(s32[1]{0:T(128)} %bitcast.z_ref.refs_2_, ...), custom_call_target="tpu_custom_call" | custom-call | tf_op jit(solution)/shard_map/pallas_call | solution.py:414
  15.0 19.6 %all-to-all-done = bf16[8,3,128,128]{3,2,1,0:T(8,128)(2,1)S(1)} async-done(((bf16[8,3,128,128]{3,2,1,0:T(8,128)(2,1)}), bf16[8,3,128,128]{3,2,1,0:T(8,128)(2,1)S(1)}, u32[]{:S(2)}, u32[]{:S(2)}) %all-to-all-start) | async-done | bytes 786464 | tf_op jit(solution)/shard_map/all_to_all | solution.py:456
  34.6 1.9 %shard_map.95 = bf16[64,128,128]{2,1,0:T(8,128)(2,1)} custom-call(s32[64]{0:T(128)S(1)} %select_n.93.rank_ref.refs_0_, bf16[24,128,128]{2,1,0:T(8,128)(2,1)S(1)} %bitcast.156), custom_call_target="tpu_custom_call" | custom-call | tf_op jit(solution)/shard_map/pallas_call | solution.py:476
  36.5 4.8 %all-to-all-start.1 = ((bf16[64,128,128]{2,1,0:T(8,128)(2,1)}), bf16[64,128,128]{2,1,0:T(8,128)(2,1)S(1)}, u32[]{:S(2)}, u32[]{:S(2)}) async-start(bf16[64,128,128]{2,1,0:T(8,128)(2,1)} %shard_map.95), calls=%async_computation.1 | async-start | bytes 4194304 | tf_op jit(solution)/shard_map/all_to_all | solution.py:466
  41.3 1.6 collective-permute-start.2
  42.9 0.9 collective-permute-start.1
  43.8 2.4 %collective-permute-start = (bf16[24,128,128]{2,1,0:T(8,128)(2,1)S(1)}, bf16[24,128,128]{2,1,0:T(8,128)(2,1)}, u32[]{:S(2)}, u32[]{:S(2)}) collective-permute-start(bf16[24,128,128]{2,1,0:T(8,128)(2,1)S(1)} %bitcast.159), channel_id=1, source_target_pairs={{0,3},{1,0},{2,1},{3,2},{4,7},{5,4},{6,5},{7,6},{8,11},{9,8},{10,9... | collective-permute-start | bytes 2359304 | tf_op jit(solution)/shard_map/ppermute | solution.py:470
  46.3 0.6 collective-permute-start.3
  46.8 0.0 collective-permute-start.4
  46.8 7.5 %collective-permute-done.3.refs_9_ = bf16[3,128,128]{2,1,0:T(8,128)(2,1)S(1)} collective-permute-done((bf16[3,128,128]{2,1,0:T(8,128)(2,1)}, bf16[3,128,128]{2,1,0:T(8,128)(2,1)S(1)}, u32[]{:S(2)}, u32[]{:S(2)}) %collective-permute-start.3) | collective-permute-done | bytes 98336 | tf_op jit(solution)/shard_map/ppermute | solution.py:439
  54.3 0.0 collective-permute-start.5
  54.3 4.2 %collective-permute-done.4.refs_10_ = bf16[3,128,128]{2,1,0:T(8,128)(2,1)S(1)} collective-permute-done((bf16[3,128,128]{2,1,0:T(8,128)(2,1)}, bf16[3,128,128]{2,1,0:T(8,128)(2,1)S(1)}, u32[]{:S(2)}, u32[]{:S(2)}) %collective-permute-start.4) | collective-permute-done | bytes 98336 | tf_op jit(solution)/shard_map/ppermute | solution.py:439
  58.5 0.0 collective-permute-start.6
  58.5 6.5 %collective-permute-done.5.refs_11_ = bf16[3,128,128]{2,1,0:T(8,128)(2,1)S(1)} collective-permute-done((bf16[3,128,128]{2,1,0:T(8,128)(2,1)}, bf16[3,128,128]{2,1,0:T(8,128)(2,1)S(1)}, u32[]{:S(2)}, u32[]{:S(2)}) %collective-permute-start.5) | collective-permute-done | bytes 98336 | tf_op jit(solution)/shard_map/ppermute | solution.py:439
  65.0 1.9 %collective-permute-start.7 = (bf16[3,128,128]{2,1,0:T(8,128)(2,1)}, bf16[3,128,128]{2,1,0:T(8,128)(2,1)}, u32[]{:S(2)}, u32[]{:S(2)}) collective-permute-start(bf16[3,128,128]{2,1,0:T(8,128)(2,1)} %get-tuple-element.60), channel_id=1, source_target_pairs={{0,20},{1,21},{2,22},{3,23},{4,24},{5,25},{6,26},{7,27},{8,28},{9,... | collective-permute-start | bytes 294920 | tf_op jit(solution)/shard_map/ppermute | solution.py:439
  66.9 0.1 convert_reduce_fusion
  67.1 0.1 copy.67
  67.1 0.1 reshape.96.refs_1_
  67.2 0.5 collective-permute-done.6.refs_12_
  67.7 0.0 collective-permute-start.8
  67.7 6.8 %collective-permute-done.7.refs_13_ = bf16[3,128,128]{2,1,0:T(8,128)(2,1)} collective-permute-done((bf16[3,128,128]{2,1,0:T(8,128)(2,1)}, bf16[3,128,128]{2,1,0:T(8,128)(2,1)}, u32[]{:S(2)}, u32[]{:S(2)}) %collective-permute-start.7) | collective-permute-done | bytes 98336 | tf_op jit(solution)/shard_map/ppermute | solution.py:439
  74.5 0.1 collective-permute-start.9
  74.6 0.1 reshape.95.refs_0_
  74.7 0.5 collective-permute-done.8.refs_14_
  75.2 4.3 %collective-permute-done.9.refs_15_ = bf16[3,128,128]{2,1,0:T(8,128)(2,1)} collective-permute-done((bf16[3,128,128]{2,1,0:T(8,128)(2,1)}, bf16[3,128,128]{2,1,0:T(8,128)(2,1)}, u32[]{:S(2)}, u32[]{:S(2)}) %collective-permute-start.9) | collective-permute-done | bytes 98336 | tf_op jit(solution)/shard_map/ppermute | solution.py:439
  79.5 0.0 collective-permute-done.2.refs_6_
  79.5 0.0 collective-permute-done.1.refs_5_
  79.5 0.4 collective-permute-done.refs_4_
  79.9 0.0 all-to-all-done.1.refs_7_
  79.9 26.6 %shard_map.96 = (bf16[3,128,128]{2,1,0:T(8,128)(2,1)}, bf16[3,128,128]{2,1,0:T(8,128)(2,1)}, bf16[3,128,128]{2,1,0:T(8,128)(2,1)}, bf16[3,128,128]{2,1,0:T(8,128...) custom-call(s32[384]{0:T(512)S(1)} %reshape.95.refs_0_, ...), custom_call_target="tpu_custom_call" | custom-call | tf_op jit(solution)/shard_map/pallas_call | solution.py:488
  106.6 7.7 %all-to-all-start.2 = ((bf16[64,128,128]{2,1,0:T(8,128)(2,1)}), bf16[64,128,128]{2,1,0:T(8,128)(2,1)S(1)}, u32[]{:S(2)}, u32[]{:S(2)}) async-start(bf16[64,128,128]{2,1,0:T(8,128)(2,1)} %get-tuple-element.85), calls=%async_computation.2 | async-start | bytes 4194304 | tf_op jit(solution)/shard_map/all_to_all | solution.py:466
  114.3 1.4 collective-permute-start.17
  115.7 1.3 collective-permute-start.18
  117.0 2.2 %collective-permute-start.19 = (bf16[24,128,128]{2,1,0:T(8,128)(2,1)}, bf16[24,128,128]{2,1,0:T(8,128)(2,1)}, u32[]{:S(2)}, u32[]{:S(2)}) collective-permute-start(bf16[24,128,128]{2,1,0:T(8,128)(2,1)} %get-tuple-element.84), channel_id=1, source_target_pairs={{0,3},{1,0},{2,1},{3,2},{4,7},{5,4},{6,5},{7,6},{8,11},{9,8},{10,9... | collective-permute-start | bytes 2359304 | tf_op jit(solution)/shard_map/ppermute | solution.py:470
  119.2 0.8 collective-permute-start.10
  120.0 2.0 %collective-permute-start.11 = (bf16[3,128,128]{2,1,0:T(8,128)(2,1)S(1)}, bf16[3,128,128]{2,1,0:T(8,128)(2,1)S(1)}, u32[]{:S(2)}, u32[]{:S(2)}) collective-permute-start(bf16[3,128,128]{2,1,0:T(8,128)(2,1)S(1)} %copy-done.16), channel_id=1, source_target_pairs={{0,8},{1,9},{2,10},{3,11},{4,12},{5,13},{6,14},{7,15},{8,16},{9,17... | collective-permute-start | bytes 294920 | tf_op jit(solution)/shard_map/ppermute | solution.py:439
  122.0 5.9 %collective-permute-done.10.refs_1_ = bf16[3,128,128]{2,1,0:T(8,128)(2,1)S(1)} collective-permute-done((bf16[3,128,128]{2,1,0:T(8,128)(2,1)S(1)}, bf16[3,128,128]{2,1,0:T(8,128)(2,1)S(1)}, u32[]{:S(2)}, u32[]{:S(2)}) %collective-permute-start.10) | collective-permute-done | bytes 98336 | tf_op jit(solution)/shard_map/ppermute | solution.py:439
  127.9 0.0 collective-permute-start.12
  127.9 1.0 collective-permute-done.11.refs_2_
  129.0 4.5 %collective-permute-start.13 = (bf16[3,128,128]{2,1,0:T(8,128)(2,1)S(1)}, bf16[3,128,128]{2,1,0:T(8,128)(2,1)S(1)}, u32[]{:S(2)}, u32[]{:S(2)}) collective-permute-start(bf16[3,128,128]{2,1,0:T(8,128)(2,1)S(1)} %copy-done.14), channel_id=1, source_target_pairs={{0,16},{1,17},{2,18},{3,19},{4,20},{5,21},{6,22},{7,23},{8,24},{9,... | collective-permute-start | bytes 294920 | tf_op jit(solution)/shard_map/ppermute | solution.py:439
  133.5 4.8 %collective-permute-done.12.refs_3_ = bf16[3,128,128]{2,1,0:T(8,128)(2,1)S(1)} collective-permute-done((bf16[3,128,128]{2,1,0:T(8,128)(2,1)S(1)}, bf16[3,128,128]{2,1,0:T(8,128)(2,1)S(1)}, u32[]{:S(2)}, u32[]{:S(2)}) %collective-permute-start.12) | collective-permute-done | bytes 98336 | tf_op jit(solution)/shard_map/ppermute | solution.py:439
  138.3 1.9 %collective-permute-start.14 = (bf16[3,128,128]{2,1,0:T(8,128)(2,1)}, bf16[3,128,128]{2,1,0:T(8,128)(2,1)S(1)}, u32[]{:S(2)}, u32[]{:S(2)}) collective-permute-start(bf16[3,128,128]{2,1,0:T(8,128)(2,1)} %get-tuple-element.68), channel_id=1, source_target_pairs={{0,20},{1,21},{2,22},{3,23},{4,24},{5,25},{6,26},{7,27},{8,28},{9,... | collective-permute-start | bytes 294920 | tf_op jit(solution)/shard_map/ppermute | solution.py:439
  140.2 0.0 collective-permute-done.13.refs_4_
  140.2 1.9 %collective-permute-start.15 = (bf16[3,128,128]{2,1,0:T(8,128)(2,1)}, bf16[3,128,128]{2,1,0:T(8,128)(2,1)S(1)}, u32[]{:S(2)}, u32[]{:S(2)}) collective-permute-start(bf16[3,128,128]{2,1,0:T(8,128)(2,1)} %get-tuple-element.69), channel_id=1, source_target_pairs={{0,24},{1,25},{2,26},{3,27},{4,28},{5,29},{6,30},{7,31},{8,0},{9,1... | collective-permute-start | bytes 294920 | tf_op jit(solution)/shard_map/ppermute | solution.py:439
  142.1 4.8 %collective-permute-done.14.refs_5_ = bf16[3,128,128]{2,1,0:T(8,128)(2,1)S(1)} collective-permute-done((bf16[3,128,128]{2,1,0:T(8,128)(2,1)}, bf16[3,128,128]{2,1,0:T(8,128)(2,1)S(1)}, u32[]{:S(2)}, u32[]{:S(2)}) %collective-permute-start.14) | collective-permute-done | bytes 98336 | tf_op jit(solution)/shard_map/ppermute | solution.py:439
  147.0 3.4 %collective-permute-start.16 = (bf16[3,128,128]{2,1,0:T(8,128)(2,1)}, bf16[3,128,128]{2,1,0:T(8,128)(2,1)S(1)}, u32[]{:S(2)}, u32[]{:S(2)}) collective-permute-start(bf16[3,128,128]{2,1,0:T(8,128)(2,1)} %get-tuple-element.70), channel_id=1, source_target_pairs={{0,28},{1,29},{2,30},{3,31},{4,0},{5,1},{6,2},{7,3},{8,4},{9,5},{1... | collective-permute-start | bytes 294920 | tf_op jit(solution)/shard_map/ppermute | solution.py:439
  150.4 0.0 collective-permute-done.15.refs_6_
  150.4 2.9 %collective-permute-done.16.refs_7_ = bf16[3,128,128]{2,1,0:T(8,128)(2,1)S(1)} collective-permute-done((bf16[3,128,128]{2,1,0:T(8,128)(2,1)}, bf16[3,128,128]{2,1,0:T(8,128)(2,1)S(1)}, u32[]{:S(2)}, u32[]{:S(2)}) %collective-permute-start.16) | collective-permute-done | bytes 98336 | tf_op jit(solution)/shard_map/ppermute | solution.py:439
  153.3 0.0 collective-permute-done.17.refs_2_
  153.3 0.6 copy-done.8
  153.9 0.9 copy-done.1
  154.8 4.0 %shard_map.98 = bf16[24,128,128]{2,1,0:T(8,128)(2,1)} custom-call(s32[64]{0:T(128)S(1)} %select_n.93.rank_ref.refs_0_, bf16[24,128,128]{2,1,0:T(8,128)(2,1)} %get-tuple-element.81.refs_1_, bf16[24,128,128]{2,1,0:T(8,128)(2,1)} %copy-done, bf16[24,128,128]{2,1,0:T(8,128)(2,1)} %copy-done.1, bf16[24,128,128]{2,1,0:T(8,128)(2,1)} %collective-permute-done.19.refs_4_, ...), custom_call_target="tpu_custom_call" | custom-call | tf_op jit(solution)/shard_map/pallas_call | solution.py:510
  158.8 6.0 %all-to-all-start.3 = ((bf16[8,3,128,128]{3,2,1,0:T(8,128)(2,1)}), bf16[8,3,128,128]{3,2,1,0:T(8,128)(2,1)S(1)}, u32[]{:S(2)}, u32[]{:S(2)}) async-start(bf16[8,3,128,128]{3,2,1,0:T(8,128)(2,1)} %bitcast.161), calls=%async_computation.3 | async-start | bytes 1572864 | tf_op jit(solution)/shard_map/all_to_all | solution.py:456
  164.9 2.4 %shard_map.97 = (bf16[3,128,512]{2,1,0:T(8,128)(2,1)}, bf16[3,128,512]{2,1,0:T(8,128)(2,1)}) custom-call(s32[1]{0:T(128)} %bitcast.z_ref.refs_2_, bf16[3,128,128]{2,1,0:T(8,128)(2,1)} %get-tuple-element.63.refs_0_, bf16[3,128,128]{2,1,0:T(8,128)(2,1)} %copy-done.2, bf16[3,128,128]{2,1,0:T(8,128)(2,1)} %copy-done.3, bf16[3,128,128]{2,1,0:T(8,128)(2,1)} %copy-done.4, ...), custom_call_target="tpu_custom_call" | custom-call | tf_op jit(solution)/shard_map/pallas_call | solution.py:424
  167.3 17.8 %all-to-all-done.3.in_ref = bf16[8,3,128,128]{3,2,1,0:T(8,128)(2,1)S(1)} async-done(((bf16[8,3,128,128]{3,2,1,0:T(8,128)(2,1)}), bf16[8,3,128,128]{3,2,1,0:T(8,128)(2,1)S(1)}, u32[]{:S(2)}, u32[]{:S(2)}) %all-to-all-start.3) | async-done | bytes 786464 | tf_op jit(solution)/shard_map/all_to_all | solution.py:456
  185.1 1.2 shard_map.99
  (42 shorter events, 0.1 us)
Async XLA Ops:
  0.6 10.8 %copy-start.12 = (s32[768,16]{0,1:T(8,128)S(1)}, s32[768,16]{0,1:T(8,128)}, u32[]{:S(2)}) copy-start(s32[768,16]{0,1:T(8,128)} %param.10) | copy-start | bytes 147460
  0.6 11.0 %copy-start.13 = (s32[768,16]{0,1:T(8,128)S(1)}, s32[768,16]{0,1:T(8,128)}, u32[]{:S(2)}) copy-start(s32[768,16]{0,1:T(8,128)} %param.11) | copy-start | bytes 147460
  3.0 31.6 %all-to-all-start = ((bf16[8,3,128,128]{3,2,1,0:T(8,128)(2,1)}), bf16[8,3,128,128]{3,2,1,0:T(8,128)(2,1)S(1)}, u32[]{:S(2)}, u32[]{:S(2)}) async-start(bf16[8,3,128,128]{3,2,1,0:T(8,128)(2,1)} %shard_map.93), calls=%async_computation | async-start | bytes 1572864 | tf_op jit(solution)/shard_map/all_to_all | solution.py:456
  36.5 43.4 %all-to-all-start.1 = ((bf16[64,128,128]{2,1,0:T(8,128)(2,1)}), bf16[64,128,128]{2,1,0:T(8,128)(2,1)S(1)}, u32[]{:S(2)}, u32[]{:S(2)}) async-start(bf16[64,128,128]{2,1,0:T(8,128)(2,1)} %shard_map.95), calls=%async_computation.1 | async-start | bytes 4194304 | tf_op jit(solution)/shard_map/all_to_all | solution.py:466
  41.3 38.1 %collective-permute-start.2 = (bf16[24,128,128]{2,1,0:T(8,128)(2,1)S(1)}, bf16[24,128,128]{2,1,0:T(8,128)(2,1)}, u32[]{:S(2)}, u32[]{:S(2)}) collective-permute-start(bf16[24,128,128]{2,1,0:T(8,128)(2,1)S(1)} %bitcast.157), channel_id=1, source_target_pairs={{0,1},{1,2},{2,3},{3,0},{4,5},{5,6},{6,7},{7,4},{8,9},{9,10},{10,1... | collective-permute-start | bytes 2359304 | tf_op jit(solution)/shard_map/ppermute | solution.py:470
  42.9 36.6 %collective-permute-start.1 = (bf16[24,128,128]{2,1,0:T(8,128)(2,1)S(1)}, bf16[24,128,128]{2,1,0:T(8,128)(2,1)}, u32[]{:S(2)}, u32[]{:S(2)}) collective-permute-start(bf16[24,128,128]{2,1,0:T(8,128)(2,1)S(1)} %bitcast.158), channel_id=1, source_target_pairs={{0,2},{1,3},{2,0},{3,1},{4,6},{5,7},{6,4},{7,5},{8,10},{9,11},{10,... | collective-permute-start | bytes 2359304 | tf_op jit(solution)/shard_map/ppermute | solution.py:470
  43.8 36.1 %collective-permute-start = (bf16[24,128,128]{2,1,0:T(8,128)(2,1)S(1)}, bf16[24,128,128]{2,1,0:T(8,128)(2,1)}, u32[]{:S(2)}, u32[]{:S(2)}) collective-permute-start(bf16[24,128,128]{2,1,0:T(8,128)(2,1)S(1)} %bitcast.159), channel_id=1, source_target_pairs={{0,3},{1,0},{2,1},{3,2},{4,7},{5,4},{6,5},{7,6},{8,11},{9,8},{10,9... | collective-permute-start | bytes 2359304 | tf_op jit(solution)/shard_map/ppermute | solution.py:470
  46.3 8.1 %collective-permute-start.3 = (bf16[3,128,128]{2,1,0:T(8,128)(2,1)}, bf16[3,128,128]{2,1,0:T(8,128)(2,1)S(1)}, u32[]{:S(2)}, u32[]{:S(2)}) collective-permute-start(bf16[3,128,128]{2,1,0:T(8,128)(2,1)} %get-tuple-element.56), channel_id=1, source_target_pairs={{0,4},{1,5},{2,6},{3,7},{4,8},{5,9},{6,10},{7,11},{8,12},{9,13},{1... | collective-permute-start | bytes 294920 | tf_op jit(solution)/shard_map/ppermute | solution.py:439
  46.8 11.7 %collective-permute-start.4 = (bf16[3,128,128]{2,1,0:T(8,128)(2,1)}, bf16[3,128,128]{2,1,0:T(8,128)(2,1)S(1)}, u32[]{:S(2)}, u32[]{:S(2)}) collective-permute-start(bf16[3,128,128]{2,1,0:T(8,128)(2,1)} %get-tuple-element.57), channel_id=1, source_target_pairs={{0,8},{1,9},{2,10},{3,11},{4,12},{5,13},{6,14},{7,15},{8,16},{9,17... | collective-permute-start | bytes 294920 | tf_op jit(solution)/shard_map/ppermute | solution.py:439
  54.3 12.6 %copy-start.9 = (bf16[3,128,128]{2,1,0:T(8,128)(2,1)}, bf16[3,128,128]{2,1,0:T(8,128)(2,1)S(1)}, u32[]{:S(2)}) copy-start(bf16[3,128,128]{2,1,0:T(8,128)(2,1)S(1)} %collective-permute-done.3.refs_9_) | copy-start | bytes 294916
  54.3 10.6 %collective-permute-start.5 = (bf16[3,128,128]{2,1,0:T(8,128)(2,1)}, bf16[3,128,128]{2,1,0:T(8,128)(2,1)S(1)}, u32[]{:S(2)}, u32[]{:S(2)}) collective-permute-start(bf16[3,128,128]{2,1,0:T(8,128)(2,1)} %get-tuple-element.58), channel_id=1, source_target_pairs={{0,12},{1,13},{2,14},{3,15},{4,16},{5,17},{6,18},{7,19},{8,20},{9,... | collective-permute-start | bytes 294920 | tf_op jit(solution)/shard_map/ppermute | solution.py:439
  58.5 8.4 %copy-start.10 = (bf16[3,128,128]{2,1,0:T(8,128)(2,1)}, bf16[3,128,128]{2,1,0:T(8,128)(2,1)S(1)}, u32[]{:S(2)}) copy-start(bf16[3,128,128]{2,1,0:T(8,128)(2,1)S(1)} %collective-permute-done.4.refs_10_) | copy-start | bytes 294916
  58.5 9.2 %collective-permute-start.6 = (bf16[3,128,128]{2,1,0:T(8,128)(2,1)}, bf16[3,128,128]{2,1,0:T(8,128)(2,1)}, u32[]{:S(2)}, u32[]{:S(2)}) collective-permute-start(bf16[3,128,128]{2,1,0:T(8,128)(2,1)} %get-tuple-element.59), channel_id=1, source_target_pairs={{0,16},{1,17},{2,18},{3,19},{4,20},{5,21},{6,22},{7,23},{8,24},{9,... | collective-permute-start | bytes 294920 | tf_op jit(solution)/shard_map/ppermute | solution.py:439
  65.0 1.9 %copy-start.11 = (bf16[3,128,128]{2,1,0:T(8,128)(2,1)}, bf16[3,128,128]{2,1,0:T(8,128)(2,1)S(1)}, u32[]{:S(2)}) copy-start(bf16[3,128,128]{2,1,0:T(8,128)(2,1)S(1)} %collective-permute-done.5.refs_11_) | copy-start | bytes 294916
  65.0 9.6 %collective-permute-start.7 = (bf16[3,128,128]{2,1,0:T(8,128)(2,1)}, bf16[3,128,128]{2,1,0:T(8,128)(2,1)}, u32[]{:S(2)}, u32[]{:S(2)}) collective-permute-start(bf16[3,128,128]{2,1,0:T(8,128)(2,1)} %get-tuple-element.60), channel_id=1, source_target_pairs={{0,20},{1,21},{2,22},{3,23},{4,24},{5,25},{6,26},{7,27},{8,28},{9,... | collective-permute-start | bytes 294920 | tf_op jit(solution)/shard_map/ppermute | solution.py:439
  67.7 7.4 %collective-permute-start.8 = (bf16[3,128,128]{2,1,0:T(8,128)(2,1)}, bf16[3,128,128]{2,1,0:T(8,128)(2,1)}, u32[]{:S(2)}, u32[]{:S(2)}) collective-permute-start(bf16[3,128,128]{2,1,0:T(8,128)(2,1)} %get-tuple-element.61), channel_id=1, source_target_pairs={{0,24},{1,25},{2,26},{3,27},{4,28},{5,29},{6,30},{7,31},{8,0},{9,1... | collective-permute-start | bytes 294920 | tf_op jit(solution)/shard_map/ppermute | solution.py:439
  74.5 4.9 %collective-permute-start.9 = (bf16[3,128,128]{2,1,0:T(8,128)(2,1)}, bf16[3,128,128]{2,1,0:T(8,128)(2,1)}, u32[]{:S(2)}, u32[]{:S(2)}) collective-permute-start(bf16[3,128,128]{2,1,0:T(8,128)(2,1)} %get-tuple-element.62), channel_id=1, source_target_pairs={{0,28},{1,29},{2,30},{3,31},{4,0},{5,1},{6,2},{7,3},{8,4},{9,5},{1... | collective-permute-start | bytes 294920 | tf_op jit(solution)/shard_map/ppermute | solution.py:439
  106.5 12.6 %copy-start.17 = (bf16[3,128,128]{2,1,0:T(8,128)(2,1)S(1)}, bf16[3,128,128]{2,1,0:T(8,128)(2,1)}, u32[]{:S(2)}) copy-start(bf16[3,128,128]{2,1,0:T(8,128)(2,1)} %get-tuple-element.64) | copy-start | bytes 294916
  106.5 13.5 %copy-start.16 = (bf16[3,128,128]{2,1,0:T(8,128)(2,1)S(1)}, bf16[3,128,128]{2,1,0:T(8,128)(2,1)}, u32[]{:S(2)}) copy-start(bf16[3,128,128]{2,1,0:T(8,128)(2,1)} %get-tuple-element.65) | copy-start | bytes 294916
  106.5 21.4 %copy-start.15 = (bf16[3,128,128]{2,1,0:T(8,128)(2,1)S(1)}, bf16[3,128,128]{2,1,0:T(8,128)(2,1)}, u32[]{:S(2)}) copy-start(bf16[3,128,128]{2,1,0:T(8,128)(2,1)} %get-tuple-element.66) | copy-start | bytes 294916
  106.6 22.4 %copy-start.14 = (bf16[3,128,128]{2,1,0:T(8,128)(2,1)S(1)}, bf16[3,128,128]{2,1,0:T(8,128)(2,1)}, u32[]{:S(2)}) copy-start(bf16[3,128,128]{2,1,0:T(8,128)(2,1)} %get-tuple-element.67) | copy-start | bytes 294916
  106.6 48.3 %all-to-all-start.2 = ((bf16[64,128,128]{2,1,0:T(8,128)(2,1)}), bf16[64,128,128]{2,1,0:T(8,128)(2,1)S(1)}, u32[]{:S(2)}, u32[]{:S(2)}) async-start(bf16[64,128,128]{2,1,0:T(8,128)(2,1)} %get-tuple-element.85), calls=%async_computation.2 | async-start | bytes 4194304 | tf_op jit(solution)/shard_map/all_to_all | solution.py:466
  114.3 39.0 %collective-permute-start.17 = (bf16[24,128,128]{2,1,0:T(8,128)(2,1)}, bf16[24,128,128]{2,1,0:T(8,128)(2,1)S(1)}, u32[]{:S(2)}, u32[]{:S(2)}) collective-permute-start(bf16[24,128,128]{2,1,0:T(8,128)(2,1)} %get-tuple-element.82), channel_id=1, source_target_pairs={{0,1},{1,2},{2,3},{3,0},{4,5},{5,6},{6,7},{7,4},{8,9},{9,10},{10,1... | collective-permute-start | bytes 2359304 | tf_op jit(solution)/shard_map/ppermute | solution.py:470
  115.7 37.6 %collective-permute-start.18 = (bf16[24,128,128]{2,1,0:T(8,128)(2,1)}, bf16[24,128,128]{2,1,0:T(8,128)(2,1)S(1)}, u32[]{:S(2)}, u32[]{:S(2)}) collective-permute-start(bf16[24,128,128]{2,1,0:T(8,128)(2,1)} %get-tuple-element.83), channel_id=1, source_target_pairs={{0,2},{1,3},{2,0},{3,1},{4,6},{5,7},{6,4},{7,5},{8,10},{9,11},{10,... | collective-permute-start | bytes 2359304 | tf_op jit(solution)/shard_map/ppermute | solution.py:470
  117.0 37.8 %collective-permute-start.19 = (bf16[24,128,128]{2,1,0:T(8,128)(2,1)}, bf16[24,128,128]{2,1,0:T(8,128)(2,1)}, u32[]{:S(2)}, u32[]{:S(2)}) collective-permute-start(bf16[24,128,128]{2,1,0:T(8,128)(2,1)} %get-tuple-element.84), channel_id=1, source_target_pairs={{0,3},{1,0},{2,1},{3,2},{4,7},{5,4},{6,5},{7,6},{8,11},{9,8},{10,9... | collective-permute-start | bytes 2359304 | tf_op jit(solution)/shard_map/ppermute | solution.py:470
  119.2 8.8 %collective-permute-start.10 = (bf16[3,128,128]{2,1,0:T(8,128)(2,1)S(1)}, bf16[3,128,128]{2,1,0:T(8,128)(2,1)S(1)}, u32[]{:S(2)}, u32[]{:S(2)}) collective-permute-start(bf16[3,128,128]{2,1,0:T(8,128)(2,1)S(1)} %copy-done.17), channel_id=1, source_target_pairs={{0,4},{1,5},{2,6},{3,7},{4,8},{5,9},{6,10},{7,11},{8,12},{9,13},{1... | collective-permute-start | bytes 294920 | tf_op jit(solution)/shard_map/ppermute | solution.py:439
  120.0 8.9 %collective-permute-start.11 = (bf16[3,128,128]{2,1,0:T(8,128)(2,1)S(1)}, bf16[3,128,128]{2,1,0:T(8,128)(2,1)S(1)}, u32[]{:S(2)}, u32[]{:S(2)}) collective-permute-start(bf16[3,128,128]{2,1,0:T(8,128)(2,1)S(1)} %copy-done.16), channel_id=1, source_target_pairs={{0,8},{1,9},{2,10},{3,11},{4,12},{5,13},{6,14},{7,15},{8,16},{9,17... | collective-permute-start | bytes 294920 | tf_op jit(solution)/shard_map/ppermute | solution.py:439
  127.9 36.9 %copy-start.2 = (bf16[3,128,128]{2,1,0:T(8,128)(2,1)}, bf16[3,128,128]{2,1,0:T(8,128)(2,1)S(1)}, u32[]{:S(2)}) copy-start(bf16[3,128,128]{2,1,0:T(8,128)(2,1)S(1)} %collective-permute-done.10.refs_1_) | copy-start | bytes 294916
  127.9 10.4 %collective-permute-start.12 = (bf16[3,128,128]{2,1,0:T(8,128)(2,1)S(1)}, bf16[3,128,128]{2,1,0:T(8,128)(2,1)S(1)}, u32[]{:S(2)}, u32[]{:S(2)}) collective-permute-start(bf16[3,128,128]{2,1,0:T(8,128)(2,1)S(1)} %copy-done.15), channel_id=1, source_target_pairs={{0,12},{1,13},{2,14},{3,15},{4,16},{5,17},{6,18},{7,19},{8,20},{9,... | collective-permute-start | bytes 294920 | tf_op jit(solution)/shard_map/ppermute | solution.py:439
  129.0 35.8 %copy-start.3 = (bf16[3,128,128]{2,1,0:T(8,128)(2,1)}, bf16[3,128,128]{2,1,0:T(8,128)(2,1)S(1)}, u32[]{:S(2)}) copy-start(bf16[3,128,128]{2,1,0:T(8,128)(2,1)S(1)} %collective-permute-done.11.refs_2_) | copy-start | bytes 294916
  129.0 11.2 %collective-permute-start.13 = (bf16[3,128,128]{2,1,0:T(8,128)(2,1)S(1)}, bf16[3,128,128]{2,1,0:T(8,128)(2,1)S(1)}, u32[]{:S(2)}, u32[]{:S(2)}) collective-permute-start(bf16[3,128,128]{2,1,0:T(8,128)(2,1)S(1)} %copy-done.14), channel_id=1, source_target_pairs={{0,16},{1,17},{2,18},{3,19},{4,20},{5,21},{6,22},{7,23},{8,24},{9,... | collective-permute-start | bytes 294920 | tf_op jit(solution)/shard_map/ppermute | solution.py:439
  138.3 26.5 %copy-start.4 = (bf16[3,128,128]{2,1,0:T(8,128)(2,1)}, bf16[3,128,128]{2,1,0:T(8,128)(2,1)S(1)}, u32[]{:S(2)}) copy-start(bf16[3,128,128]{2,1,0:T(8,128)(2,1)S(1)} %collective-permute-done.12.refs_3_) | copy-start | bytes 294916
  138.3 8.6 %collective-permute-start.14 = (bf16[3,128,128]{2,1,0:T(8,128)(2,1)}, bf16[3,128,128]{2,1,0:T(8,128)(2,1)S(1)}, u32[]{:S(2)}, u32[]{:S(2)}) collective-permute-start(bf16[3,128,128]{2,1,0:T(8,128)(2,1)} %get-tuple-element.68), channel_id=1, source_target_pairs={{0,20},{1,21},{2,22},{3,23},{4,24},{5,25},{6,26},{7,27},{8,28},{9,... | collective-permute-start | bytes 294920 | tf_op jit(solution)/shard_map/ppermute | solution.py:439
  140.2 24.6 %copy-start.5 = (bf16[3,128,128]{2,1,0:T(8,128)(2,1)}, bf16[3,128,128]{2,1,0:T(8,128)(2,1)S(1)}, u32[]{:S(2)}) copy-start(bf16[3,128,128]{2,1,0:T(8,128)(2,1)S(1)} %collective-permute-done.13.refs_4_) | copy-start | bytes 294916
  140.2 10.2 %collective-permute-start.15 = (bf16[3,128,128]{2,1,0:T(8,128)(2,1)}, bf16[3,128,128]{2,1,0:T(8,128)(2,1)S(1)}, u32[]{:S(2)}, u32[]{:S(2)}) collective-permute-start(bf16[3,128,128]{2,1,0:T(8,128)(2,1)} %get-tuple-element.69), channel_id=1, source_target_pairs={{0,24},{1,25},{2,26},{3,27},{4,28},{5,29},{6,30},{7,31},{8,0},{9,1... | collective-permute-start | bytes 294920 | tf_op jit(solution)/shard_map/ppermute | solution.py:439
  147.0 17.9 %copy-start.6 = (bf16[3,128,128]{2,1,0:T(8,128)(2,1)}, bf16[3,128,128]{2,1,0:T(8,128)(2,1)S(1)}, u32[]{:S(2)}) copy-start(bf16[3,128,128]{2,1,0:T(8,128)(2,1)S(1)} %collective-permute-done.14.refs_5_) | copy-start | bytes 294916
  147.0 6.3 %collective-permute-start.16 = (bf16[3,128,128]{2,1,0:T(8,128)(2,1)}, bf16[3,128,128]{2,1,0:T(8,128)(2,1)S(1)}, u32[]{:S(2)}, u32[]{:S(2)}) collective-permute-start(bf16[3,128,128]{2,1,0:T(8,128)(2,1)} %get-tuple-element.70), channel_id=1, source_target_pairs={{0,28},{1,29},{2,30},{3,31},{4,0},{5,1},{6,2},{7,3},{8,4},{9,5},{1... | collective-permute-start | bytes 294920 | tf_op jit(solution)/shard_map/ppermute | solution.py:439
  150.4 14.5 %copy-start.7 = (bf16[3,128,128]{2,1,0:T(8,128)(2,1)}, bf16[3,128,128]{2,1,0:T(8,128)(2,1)S(1)}, u32[]{:S(2)}) copy-start(bf16[3,128,128]{2,1,0:T(8,128)(2,1)S(1)} %collective-permute-done.15.refs_6_) | copy-start | bytes 294916
  153.3 0.6 copy-start.8
  153.3 1.5 copy-start
  153.9 0.9 copy-start.1
  158.8 26.3 %all-to-all-start.3 = ((bf16[8,3,128,128]{3,2,1,0:T(8,128)(2,1)}), bf16[8,3,128,128]{3,2,1,0:T(8,128)(2,1)S(1)}, u32[]{:S(2)}, u32[]{:S(2)}) async-start(bf16[8,3,128,128]{3,2,1,0:T(8,128)(2,1)} %bitcast.161), calls=%async_computation.3 | async-start | bytes 1572864 | tf_op jit(solution)/shard_map/all_to_all | solution.py:456

commit v6 on v5

--- a/solution.py
+++ b/solution.py
@@ -143,7 +143,7 @@
         copy.wait()
     left = query_at < HEAD_DIM
     scale = HEAD_DIM ** -0.5
-    group = 4
+    group = 2
     banks = 3
     chain = 4
 
@@ -241,9 +241,10 @@
         count = count_ref[ids[0]]
         for tile in ids[1:]:
             count = jnp.maximum(count, count_ref[tile])
-        for size in range(group, entries + 1, group):
-
-            @pl.when((count > size - group) & (count <= size))
+        sizes = [size for size in range(group, entries + 1, group) if size >= entries // 2]
+        for below, size in zip([0, *sizes], sizes):
+
+            @pl.when((count > below) & (count <= size))
             def _():
                 run_chain(ids, size)
 

time: 187 us -> 187 us (level)
  transfers between devices with their start and end apart: 24 -> 24, of which waited for: 15 -> 14; matrix products, arithmetic and copies ran while one was open for 1% -> 1% of each run, Pallas kernels for 3% -> 3%
where the time goes in v6:
time: 187 us; the launch traced here: 186 us
  waiting for transfers between devices  87.1 us (47%)
  starting transfers between devices  53.2 us (28%)
  Pallas kernels  41.9 us (22%)
  local copies, waits for them, and re-layouts  2.45 us (1%)
    ppermute x14, waiting for transfers between devices, shift_z(): return lax.ppermute(source, 'seq', pairs)  48.4 us
    all_to_all x2, waiting for transfers between devices, over_z(): lax.all_to_all(source.reshape(head_shape.shape), 'seq', split_axis=0, con...  38.3 us
    pallas_call x1, Pallas kernels, per_device(): pl.pallas_call(functools.partial(attend_kernel, tiles=tiles, entries=entr...  27.8 us
    ppermute x14, starting transfers between devices, shift_z(): return lax.ppermute(source, 'seq', pairs)  18.2 us
    all_to_all x2, starting transfers between devices, over_z(): lax.all_to_all(source.reshape(head_shape.shape), 'seq', split_axis=0, con...  13.6 us
    all_to_all x2, starting transfers between devices, over_groups(): lax.all_to_all(source, 'grp', split_axis=0, concat_axis=0, tiled=True)  11.4 us
    ppermute x6, starting transfers between devices, over_y(): return lax.ppermute(source, 'seq', pairs)  10 us
    pallas_call x1, Pallas kernels, per_device(): pl.pallas_call(functools.partial(combine_kernel, ys=ys, groups=groups, zs...  3.96 us
  transfers between devices with their start and end apart: 24, of which 14 were waited for; matrix products, arithmetic and copies ran while one was open for 1% of the time, Pallas kernels for 3%

profile of v6, /device:TPU:10, one launch (start us, length us, event | category | flops | bytes accessed | tf_op | source)
XLA Modules:
  0.0 186.5 jit_solution(7502120071570485773)
XLA Ops:
  0.7 2.3 %shard_map.93 = bf16[8,3,128,128]{3,2,1,0:T(8,128)(2,1)} custom-call(bf16[3,128,512]{2,1,0:T(8,128)(2,1)} %bitcast.167, bf16[3,128,512]{2,1,0:T(8,128)(2,1)} %bitcast.168), custom_call_target="tpu_custom_call" | custom-call | tf_op jit(solution)/shard_map/pallas_call | solution.py:402
  3.0 8.5 %all-to-all-start = ((bf16[8,3,128,128]{3,2,1,0:T(8,128)(2,1)}), bf16[8,3,128,128]{3,2,1,0:T(8,128)(2,1)S(1)}, u32[]{:S(2)}, u32[]{:S(2)}) async-start(bf16[8,3,128,128]{3,2,1,0:T(8,128)(2,1)} %shard_map.93), calls=%async_computation | async-start | bytes 1572864 | tf_op jit(solution)/shard_map/all_to_all | solution.py:457
  11.5 0.2 copy.57
  11.6 0.2 copy.64
  11.8 0.2 constant_dynamic-slice_fusion
  12.1 0.5 fusion.1
  12.5 0.1 broadcast_select_fusion
  12.6 0.1 select_n.93.rank_ref.refs_0_
  12.7 2.3 %shard_map.94 = (bf16[3,128,128]{2,1,0:T(8,128)(2,1)}, bf16[3,128,128]{2,1,0:T(8,128)(2,1)}, bf16[3,128,128]{2,1,0:T(8,128)(2,1)}, bf16[3,128,128]{2,1,0:T(8,128...) custom-call(s32[1]{0:T(128)} %bitcast.z_ref.refs_2_, ...), custom_call_target="tpu_custom_call" | custom-call | tf_op jit(solution)/shard_map/pallas_call | solution.py:415
  15.0 19.6 %all-to-all-done = bf16[8,3,128,128]{3,2,1,0:T(8,128)(2,1)S(1)} async-done(((bf16[8,3,128,128]{3,2,1,0:T(8,128)(2,1)}), bf16[8,3,128,128]{3,2,1,0:T(8,128)(2,1)S(1)}, u32[]{:S(2)}, u32[]{:S(2)}) %all-to-all-start) | async-done | bytes 786464 | tf_op jit(solution)/shard_map/all_to_all | solution.py:457
  34.6 1.9 %shard_map.95 = bf16[64,128,128]{2,1,0:T(8,128)(2,1)} custom-call(s32[64]{0:T(128)S(1)} %select_n.93.rank_ref.refs_0_, bf16[24,128,128]{2,1,0:T(8,128)(2,1)S(1)} %bitcast.156), custom_call_target="tpu_custom_call" | custom-call | tf_op jit(solution)/shard_map/pallas_call | solution.py:477
  36.5 4.8 %all-to-all-start.1 = ((bf16[64,128,128]{2,1,0:T(8,128)(2,1)}), bf16[64,128,128]{2,1,0:T(8,128)(2,1)S(1)}, u32[]{:S(2)}, u32[]{:S(2)}) async-start(bf16[64,128,128]{2,1,0:T(8,128)(2,1)} %shard_map.95), calls=%async_computation.1 | async-start | bytes 4194304 | tf_op jit(solution)/shard_map/all_to_all | solution.py:467
  41.3 1.6 collective-permute-start.2
  42.9 0.9 collective-permute-start.1
  43.8 2.4 %collective-permute-start = (bf16[24,128,128]{2,1,0:T(8,128)(2,1)S(1)}, bf16[24,128,128]{2,1,0:T(8,128)(2,1)}, u32[]{:S(2)}, u32[]{:S(2)}) collective-permute-start(bf16[24,128,128]{2,1,0:T(8,128)(2,1)S(1)} %bitcast.159), channel_id=1, source_target_pairs={{0,3},{1,0},{2,1},{3,2},{4,7},{5,4},{6,5},{7,6},{8,11},{9,8},{10,9... | collective-permute-start | bytes 2359304 | tf_op jit(solution)/shard_map/ppermute | solution.py:471
  46.3 0.6 collective-permute-start.3
  46.8 0.0 collective-permute-start.4
  46.8 7.5 %collective-permute-done.3.refs_9_ = bf16[3,128,128]{2,1,0:T(8,128)(2,1)S(1)} collective-permute-done((bf16[3,128,128]{2,1,0:T(8,128)(2,1)}, bf16[3,128,128]{2,1,0:T(8,128)(2,1)S(1)}, u32[]{:S(2)}, u32[]{:S(2)}) %collective-permute-start.3) | collective-permute-done | bytes 98336 | tf_op jit(solution)/shard_map/ppermute | solution.py:440
  54.3 0.0 collective-permute-start.5
  54.3 4.2 %collective-permute-done.4.refs_10_ = bf16[3,128,128]{2,1,0:T(8,128)(2,1)S(1)} collective-permute-done((bf16[3,128,128]{2,1,0:T(8,128)(2,1)}, bf16[3,128,128]{2,1,0:T(8,128)(2,1)S(1)}, u32[]{:S(2)}, u32[]{:S(2)}) %collective-permute-start.4) | collective-permute-done | bytes 98336 | tf_op jit(solution)/shard_map/ppermute | solution.py:440
  58.5 0.0 collective-permute-start.6
  58.5 6.5 %collective-permute-done.5.refs_11_ = bf16[3,128,128]{2,1,0:T(8,128)(2,1)S(1)} collective-permute-done((bf16[3,128,128]{2,1,0:T(8,128)(2,1)}, bf16[3,128,128]{2,1,0:T(8,128)(2,1)S(1)}, u32[]{:S(2)}, u32[]{:S(2)}) %collective-permute-start.5) | collective-permute-done | bytes 98336 | tf_op jit(solution)/shard_map/ppermute | solution.py:440
  65.0 1.9 %collective-permute-start.7 = (bf16[3,128,128]{2,1,0:T(8,128)(2,1)}, bf16[3,128,128]{2,1,0:T(8,128)(2,1)}, u32[]{:S(2)}, u32[]{:S(2)}) collective-permute-start(bf16[3,128,128]{2,1,0:T(8,128)(2,1)} %get-tuple-element.60), channel_id=1, source_target_pairs={{0,20},{1,21},{2,22},{3,23},{4,24},{5,25},{6,26},{7,27},{8,28},{9,... | collective-permute-start | bytes 294920 | tf_op jit(solution)/shard_map/ppermute | solution.py:440
  66.9 0.1 convert_reduce_fusion
  67.1 0.1 copy.67
  67.1 0.1 reshape.96.refs_1_
  67.2 0.5 collective-permute-done.6.refs_12_
  67.7 0.0 collective-permute-start.8
  67.7 6.8 %collective-permute-done.7.refs_13_ = bf16[3,128,128]{2,1,0:T(8,128)(2,1)} collective-permute-done((bf16[3,128,128]{2,1,0:T(8,128)(2,1)}, bf16[3,128,128]{2,1,0:T(8,128)(2,1)}, u32[]{:S(2)}, u32[]{:S(2)}) %collective-permute-start.7) | collective-permute-done | bytes 98336 | tf_op jit(solution)/shard_map/ppermute | solution.py:440
  74.5 0.1 collective-permute-start.9
  74.6 0.1 reshape.95.refs_0_
  74.7 0.5 collective-permute-done.8.refs_14_
  75.2 4.3 %collective-permute-done.9.refs_15_ = bf16[3,128,128]{2,1,0:T(8,128)(2,1)} collective-permute-done((bf16[3,128,128]{2,1,0:T(8,128)(2,1)}, bf16[3,128,128]{2,1,0:T(8,128)(2,1)}, u32[]{:S(2)}, u32[]{:S(2)}) %collective-permute-start.9) | collective-permute-done | bytes 98336 | tf_op jit(solution)/shard_map/ppermute | solution.py:440
  79.5 0.0 collective-permute-done.2.refs_6_
  79.5 0.4 collective-permute-done.refs_4_
  79.9 0.0 all-to-all-done.1.refs_7_
  79.9 27.8 %shard_map.96 = (bf16[3,128,128]{2,1,0:T(8,128)(2,1)}, bf16[3,128,128]{2,1,0:T(8,128)(2,1)}, bf16[3,128,128]{2,1,0:T(8,128)(2,1)}, bf16[3,128,128]{2,1,0:T(8,128...) custom-call(s32[384]{0:T(512)S(1)} %reshape.95.refs_0_, ...), custom_call_target="tpu_custom_call" | custom-call | tf_op jit(solution)/shard_map/pallas_call | solution.py:489
  107.7 6.6 %all-to-all-start.2 = ((bf16[64,128,128]{2,1,0:T(8,128)(2,1)}), bf16[64,128,128]{2,1,0:T(8,128)(2,1)S(1)}, u32[]{:S(2)}, u32[]{:S(2)}) async-start(bf16[64,128,128]{2,1,0:T(8,128)(2,1)} %get-tuple-element.85), calls=%async_computation.2 | async-start | bytes 4194304 | tf_op jit(solution)/shard_map/all_to_all | solution.py:467
  114.3 1.5 collective-permute-start.17
  115.8 1.5 collective-permute-start.18
  117.3 2.1 %collective-permute-start.19 = (bf16[24,128,128]{2,1,0:T(8,128)(2,1)}, bf16[24,128,128]{2,1,0:T(8,128)(2,1)}, u32[]{:S(2)}, u32[]{:S(2)}) collective-permute-start(bf16[24,128,128]{2,1,0:T(8,128)(2,1)} %get-tuple-element.84), channel_id=1, source_target_pairs={{0,3},{1,0},{2,1},{3,2},{4,7},{5,4},{6,5},{7,6},{8,11},{9,8},{10,9... | collective-permute-start | bytes 2359304 | tf_op jit(solution)/shard_map/ppermute | solution.py:471
  119.4 1.3 collective-permute-start.10
  120.7 2.0 %collective-permute-start.11 = (bf16[3,128,128]{2,1,0:T(8,128)(2,1)S(1)}, bf16[3,128,128]{2,1,0:T(8,128)(2,1)S(1)}, u32[]{:S(2)}, u32[]{:S(2)}) collective-permute-start(bf16[3,128,128]{2,1,0:T(8,128)(2,1)S(1)} %copy-done.16), channel_id=1, source_target_pairs={{0,8},{1,9},{2,10},{3,11},{4,12},{5,13},{6,14},{7,15},{8,16},{9,17... | collective-permute-start | bytes 294920 | tf_op jit(solution)/shard_map/ppermute | solution.py:440
  122.6 5.4 %collective-permute-done.10.refs_1_ = bf16[3,128,128]{2,1,0:T(8,128)(2,1)S(1)} collective-permute-done((bf16[3,128,128]{2,1,0:T(8,128)(2,1)S(1)}, bf16[3,128,128]{2,1,0:T(8,128)(2,1)S(1)}, u32[]{:S(2)}, u32[]{:S(2)}) %collective-permute-start.10) | collective-permute-done | bytes 98336 | tf_op jit(solution)/shard_map/ppermute | solution.py:440
  128.0 0.0 collective-permute-done.11.refs_2_
  128.0 0.0 copy-start.3
  128.1 6.4 %collective-permute-start.13 = (bf16[3,128,128]{2,1,0:T(8,128)(2,1)S(1)}, bf16[3,128,128]{2,1,0:T(8,128)(2,1)S(1)}, u32[]{:S(2)}, u32[]{:S(2)}) collective-permute-start(bf16[3,128,128]{2,1,0:T(8,128)(2,1)S(1)} %copy-done.14), channel_id=1, source_target_pairs={{0,16},{1,17},{2,18},{3,19},{4,20},{5,21},{6,22},{7,23},{8,24},{9,... | collective-permute-start | bytes 294920 | tf_op jit(solution)/shard_map/ppermute | solution.py:440
  134.5 4.6 %collective-permute-done.12.refs_3_ = bf16[3,128,128]{2,1,0:T(8,128)(2,1)S(1)} collective-permute-done((bf16[3,128,128]{2,1,0:T(8,128)(2,1)S(1)}, bf16[3,128,128]{2,1,0:T(8,128)(2,1)S(1)}, u32[]{:S(2)}, u32[]{:S(2)}) %collective-permute-start.12) | collective-permute-done | bytes 98336 | tf_op jit(solution)/shard_map/ppermute | solution.py:440
  139.1 1.5 collective-permute-start.14
  140.7 0.0 collective-permute-done.13.refs_4_
  140.7 1.4 collective-permute-start.15
  142.1 5.7 %collective-permute-done.14.refs_5_ = bf16[3,128,128]{2,1,0:T(8,128)(2,1)S(1)} collective-permute-done((bf16[3,128,128]{2,1,0:T(8,128)(2,1)}, bf16[3,128,128]{2,1,0:T(8,128)(2,1)S(1)}, u32[]{:S(2)}, u32[]{:S(2)}) %collective-permute-start.14) | collective-permute-done | bytes 98336 | tf_op jit(solution)/shard_map/ppermute | solution.py:440
  147.7 3.0 %collective-permute-start.16 = (bf16[3,128,128]{2,1,0:T(8,128)(2,1)}, bf16[3,128,128]{2,1,0:T(8,128)(2,1)S(1)}, u32[]{:S(2)}, u32[]{:S(2)}) collective-permute-start(bf16[3,128,128]{2,1,0:T(8,128)(2,1)} %get-tuple-element.70), channel_id=1, source_target_pairs={{0,28},{1,29},{2,30},{3,31},{4,0},{5,1},{6,2},{7,3},{8,4},{9,5},{1... | collective-permute-start | bytes 294920 | tf_op jit(solution)/shard_map/ppermute | solution.py:440
  150.7 0.0 collective-permute-done.15.refs_6_
  150.7 2.5 %collective-permute-done.16.refs_7_ = bf16[3,128,128]{2,1,0:T(8,128)(2,1)S(1)} collective-permute-done((bf16[3,128,128]{2,1,0:T(8,128)(2,1)}, bf16[3,128,128]{2,1,0:T(8,128)(2,1)S(1)}, u32[]{:S(2)}, u32[]{:S(2)}) %collective-permute-start.16) | collective-permute-done | bytes 98336 | tf_op jit(solution)/shard_map/ppermute | solution.py:440
  153.3 0.6 copy-done.8
  153.9 0.9 copy-done.1
  154.8 0.0 collective-permute-done.19.refs_4_
  154.8 0.0 all-to-all-done.2
  154.8 4.0 %shard_map.98 = bf16[24,128,128]{2,1,0:T(8,128)(2,1)} custom-call(s32[64]{0:T(128)S(1)} %select_n.93.rank_ref.refs_0_, bf16[24,128,128]{2,1,0:T(8,128)(2,1)} %get-tuple-element.81.refs_1_, bf16[24,128,128]{2,1,0:T(8,128)(2,1)} %copy-done, bf16[24,128,128]{2,1,0:T(8,128)(2,1)} %copy-done.1, bf16[24,128,128]{2,1,0:T(8,128)(2,1)} %collective-permute-done.19.refs_4_, ...), custom_call_target="tpu_custom_call" | custom-call | tf_op jit(solution)/shard_map/pallas_call | solution.py:511
  158.8 5.1 %all-to-all-start.3 = ((bf16[8,3,128,128]{3,2,1,0:T(8,128)(2,1)}), bf16[8,3,128,128]{3,2,1,0:T(8,128)(2,1)S(1)}, u32[]{:S(2)}, u32[]{:S(2)}) async-start(bf16[8,3,128,128]{3,2,1,0:T(8,128)(2,1)} %bitcast.161), calls=%async_computation.3 | async-start | bytes 1572864 | tf_op jit(solution)/shard_map/all_to_all | solution.py:457
  164.0 2.4 %shard_map.97 = (bf16[3,128,512]{2,1,0:T(8,128)(2,1)}, bf16[3,128,512]{2,1,0:T(8,128)(2,1)}) custom-call(s32[1]{0:T(128)} %bitcast.z_ref.refs_2_, bf16[3,128,128]{2,1,0:T(8,128)(2,1)} %get-tuple-element.63.refs_0_, bf16[3,128,128]{2,1,0:T(8,128)(2,1)} %copy-done.2, bf16[3,128,128]{2,1,0:T(8,128)(2,1)} %copy-done.3, bf16[3,128,128]{2,1,0:T(8,128)(2,1)} %copy-done.4, ...), custom_call_target="tpu_custom_call" | custom-call | tf_op jit(solution)/shard_map/pallas_call | solution.py:425
  166.4 18.7 %all-to-all-done.3.in_ref = bf16[8,3,128,128]{3,2,1,0:T(8,128)(2,1)S(1)} async-done(((bf16[8,3,128,128]{3,2,1,0:T(8,128)(2,1)}), bf16[8,3,128,128]{3,2,1,0:T(8,128)(2,1)S(1)}, u32[]{:S(2)}, u32[]{:S(2)}) %all-to-all-start.3) | async-done | bytes 786464 | tf_op jit(solution)/shard_map/all_to_all | solution.py:457
  185.1 1.2 shard_map.99
  (42 shorter events, 0.1 us)
Async XLA Ops:
  0.6 10.8 %copy-start.12 = (s32[768,16]{0,1:T(8,128)S(1)}, s32[768,16]{0,1:T(8,128)}, u32[]{:S(2)}) copy-start(s32[768,16]{0,1:T(8,128)} %param.10) | copy-start | bytes 147460
  0.6 11.0 %copy-start.13 = (s32[768,16]{0,1:T(8,128)S(1)}, s32[768,16]{0,1:T(8,128)}, u32[]{:S(2)}) copy-start(s32[768,16]{0,1:T(8,128)} %param.11) | copy-start | bytes 147460
  3.0 31.6 %all-to-all-start = ((bf16[8,3,128,128]{3,2,1,0:T(8,128)(2,1)}), bf16[8,3,128,128]{3,2,1,0:T(8,128)(2,1)S(1)}, u32[]{:S(2)}, u32[]{:S(2)}) async-start(bf16[8,3,128,128]{3,2,1,0:T(8,128)(2,1)} %shard_map.93), calls=%async_computation | async-start | bytes 1572864 | tf_op jit(solution)/shard_map/all_to_all | solution.py:457
  36.5 43.4 %all-to-all-start.1 = ((bf16[64,128,128]{2,1,0:T(8,128)(2,1)}), bf16[64,128,128]{2,1,0:T(8,128)(2,1)S(1)}, u32[]{:S(2)}, u32[]{:S(2)}) async-start(bf16[64,128,128]{2,1,0:T(8,128)(2,1)} %shard_map.95), calls=%async_computation.1 | async-start | bytes 4194304 | tf_op jit(solution)/shard_map/all_to_all | solution.py:467
  41.3 38.1 %collective-permute-start.2 = (bf16[24,128,128]{2,1,0:T(8,128)(2,1)S(1)}, bf16[24,128,128]{2,1,0:T(8,128)(2,1)}, u32[]{:S(2)}, u32[]{:S(2)}) collective-permute-start(bf16[24,128,128]{2,1,0:T(8,128)(2,1)S(1)} %bitcast.157), channel_id=1, source_target_pairs={{0,1},{1,2},{2,3},{3,0},{4,5},{5,6},{6,7},{7,4},{8,9},{9,10},{10,1... | collective-permute-start | bytes 2359304 | tf_op jit(solution)/shard_map/ppermute | solution.py:471
  42.9 36.6 %collective-permute-start.1 = (bf16[24,128,128]{2,1,0:T(8,128)(2,1)S(1)}, bf16[24,128,128]{2,1,0:T(8,128)(2,1)}, u32[]{:S(2)}, u32[]{:S(2)}) collective-permute-start(bf16[24,128,128]{2,1,0:T(8,128)(2,1)S(1)} %bitcast.158), channel_id=1, source_target_pairs={{0,2},{1,3},{2,0},{3,1},{4,6},{5,7},{6,4},{7,5},{8,10},{9,11},{10,... | collective-permute-start | bytes 2359304 | tf_op jit(solution)/shard_map/ppermute | solution.py:471
  43.8 36.1 %collective-permute-start = (bf16[24,128,128]{2,1,0:T(8,128)(2,1)S(1)}, bf16[24,128,128]{2,1,0:T(8,128)(2,1)}, u32[]{:S(2)}, u32[]{:S(2)}) collective-permute-start(bf16[24,128,128]{2,1,0:T(8,128)(2,1)S(1)} %bitcast.159), channel_id=1, source_target_pairs={{0,3},{1,0},{2,1},{3,2},{4,7},{5,4},{6,5},{7,6},{8,11},{9,8},{10,9... | collective-permute-start | bytes 2359304 | tf_op jit(solution)/shard_map/ppermute | solution.py:471
  46.3 8.1 %collective-permute-start.3 = (bf16[3,128,128]{2,1,0:T(8,128)(2,1)}, bf16[3,128,128]{2,1,0:T(8,128)(2,1)S(1)}, u32[]{:S(2)}, u32[]{:S(2)}) collective-permute-start(bf16[3,128,128]{2,1,0:T(8,128)(2,1)} %get-tuple-element.56), channel_id=1, source_target_pairs={{0,4},{1,5},{2,6},{3,7},{4,8},{5,9},{6,10},{7,11},{8,12},{9,13},{1... | collective-permute-start | bytes 294920 | tf_op jit(solution)/shard_map/ppermute | solution.py:440
  46.8 11.7 %collective-permute-start.4 = (bf16[3,128,128]{2,1,0:T(8,128)(2,1)}, bf16[3,128,128]{2,1,0:T(8,128)(2,1)S(1)}, u32[]{:S(2)}, u32[]{:S(2)}) collective-permute-start(bf16[3,128,128]{2,1,0:T(8,128)(2,1)} %get-tuple-element.57), channel_id=1, source_target_pairs={{0,8},{1,9},{2,10},{3,11},{4,12},{5,13},{6,14},{7,15},{8,16},{9,17... | collective-permute-start | bytes 294920 | tf_op jit(solution)/shard_map/ppermute | solution.py:440
  54.3 12.6 %copy-start.9 = (bf16[3,128,128]{2,1,0:T(8,128)(2,1)}, bf16[3,128,128]{2,1,0:T(8,128)(2,1)S(1)}, u32[]{:S(2)}) copy-start(bf16[3,128,128]{2,1,0:T(8,128)(2,1)S(1)} %collective-permute-done.3.refs_9_) | copy-start | bytes 294916
  54.3 10.6 %collective-permute-start.5 = (bf16[3,128,128]{2,1,0:T(8,128)(2,1)}, bf16[3,128,128]{2,1,0:T(8,128)(2,1)S(1)}, u32[]{:S(2)}, u32[]{:S(2)}) collective-permute-start(bf16[3,128,128]{2,1,0:T(8,128)(2,1)} %get-tuple-element.58), channel_id=1, source_target_pairs={{0,12},{1,13},{2,14},{3,15},{4,16},{5,17},{6,18},{7,19},{8,20},{9,... | collective-permute-start | bytes 294920 | tf_op jit(solution)/shard_map/ppermute | solution.py:440
  58.5 8.4 %copy-start.10 = (bf16[3,128,128]{2,1,0:T(8,128)(2,1)}, bf16[3,128,128]{2,1,0:T(8,128)(2,1)S(1)}, u32[]{:S(2)}) copy-start(bf16[3,128,128]{2,1,0:T(8,128)(2,1)S(1)} %collective-permute-done.4.refs_10_) | copy-start | bytes 294916
  58.5 9.2 %collective-permute-start.6 = (bf16[3,128,128]{2,1,0:T(8,128)(2,1)}, bf16[3,128,128]{2,1,0:T(8,128)(2,1)}, u32[]{:S(2)}, u32[]{:S(2)}) collective-permute-start(bf16[3,128,128]{2,1,0:T(8,128)(2,1)} %get-tuple-element.59), channel_id=1, source_target_pairs={{0,16},{1,17},{2,18},{3,19},{4,20},{5,21},{6,22},{7,23},{8,24},{9,... | collective-permute-start | bytes 294920 | tf_op jit(solution)/shard_map/ppermute | solution.py:440
  65.0 1.9 %copy-start.11 = (bf16[3,128,128]{2,1,0:T(8,128)(2,1)}, bf16[3,128,128]{2,1,0:T(8,128)(2,1)S(1)}, u32[]{:S(2)}) copy-start(bf16[3,128,128]{2,1,0:T(8,128)(2,1)S(1)} %collective-permute-done.5.refs_11_) | copy-start | bytes 294916
  65.0 9.6 %collective-permute-start.7 = (bf16[3,128,128]{2,1,0:T(8,128)(2,1)}, bf16[3,128,128]{2,1,0:T(8,128)(2,1)}, u32[]{:S(2)}, u32[]{:S(2)}) collective-permute-start(bf16[3,128,128]{2,1,0:T(8,128)(2,1)} %get-tuple-element.60), channel_id=1, source_target_pairs={{0,20},{1,21},{2,22},{3,23},{4,24},{5,25},{6,26},{7,27},{8,28},{9,... | collective-permute-start | bytes 294920 | tf_op jit(solution)/shard_map/ppermute | solution.py:440
  67.7 7.4 %collective-permute-start.8 = (bf16[3,128,128]{2,1,0:T(8,128)(2,1)}, bf16[3,128,128]{2,1,0:T(8,128)(2,1)}, u32[]{:S(2)}, u32[]{:S(2)}) collective-permute-start(bf16[3,128,128]{2,1,0:T(8,128)(2,1)} %get-tuple-element.61), channel_id=1, source_target_pairs={{0,24},{1,25},{2,26},{3,27},{4,28},{5,29},{6,30},{7,31},{8,0},{9,1... | collective-permute-start | bytes 294920 | tf_op jit(solution)/shard_map/ppermute | solution.py:440
  74.5 4.9 %collective-permute-start.9 = (bf16[3,128,128]{2,1,0:T(8,128)(2,1)}, bf16[3,128,128]{2,1,0:T(8,128)(2,1)}, u32[]{:S(2)}, u32[]{:S(2)}) collective-permute-start(bf16[3,128,128]{2,1,0:T(8,128)(2,1)} %get-tuple-element.62), channel_id=1, source_target_pairs={{0,28},{1,29},{2,30},{3,31},{4,0},{5,1},{6,2},{7,3},{8,4},{9,5},{1... | collective-permute-start | bytes 294920 | tf_op jit(solution)/shard_map/ppermute | solution.py:440
  107.7 11.7 %copy-start.17 = (bf16[3,128,128]{2,1,0:T(8,128)(2,1)S(1)}, bf16[3,128,128]{2,1,0:T(8,128)(2,1)}, u32[]{:S(2)}) copy-start(bf16[3,128,128]{2,1,0:T(8,128)(2,1)} %get-tuple-element.64) | copy-start | bytes 294916
  107.7 13.0 %copy-start.16 = (bf16[3,128,128]{2,1,0:T(8,128)(2,1)S(1)}, bf16[3,128,128]{2,1,0:T(8,128)(2,1)}, u32[]{:S(2)}) copy-start(bf16[3,128,128]{2,1,0:T(8,128)(2,1)} %get-tuple-element.65) | copy-start | bytes 294916
  107.7 20.3 %copy-start.15 = (bf16[3,128,128]{2,1,0:T(8,128)(2,1)S(1)}, bf16[3,128,128]{2,1,0:T(8,128)(2,1)}, u32[]{:S(2)}) copy-start(bf16[3,128,128]{2,1,0:T(8,128)(2,1)} %get-tuple-element.66) | copy-start | bytes 294916
  107.7 20.3 %copy-start.14 = (bf16[3,128,128]{2,1,0:T(8,128)(2,1)S(1)}, bf16[3,128,128]{2,1,0:T(8,128)(2,1)}, u32[]{:S(2)}) copy-start(bf16[3,128,128]{2,1,0:T(8,128)(2,1)} %get-tuple-element.67) | copy-start | bytes 294916
  107.7 47.1 %all-to-all-start.2 = ((bf16[64,128,128]{2,1,0:T(8,128)(2,1)}), bf16[64,128,128]{2,1,0:T(8,128)(2,1)S(1)}, u32[]{:S(2)}, u32[]{:S(2)}) async-start(bf16[64,128,128]{2,1,0:T(8,128)(2,1)} %get-tuple-element.85), calls=%async_computation.2 | async-start | bytes 4194304 | tf_op jit(solution)/shard_map/all_to_all | solution.py:467
  114.3 39.0 %collective-permute-start.17 = (bf16[24,128,128]{2,1,0:T(8,128)(2,1)}, bf16[24,128,128]{2,1,0:T(8,128)(2,1)S(1)}, u32[]{:S(2)}, u32[]{:S(2)}) collective-permute-start(bf16[24,128,128]{2,1,0:T(8,128)(2,1)} %get-tuple-element.82), channel_id=1, source_target_pairs={{0,1},{1,2},{2,3},{3,0},{4,5},{5,6},{6,7},{7,4},{8,9},{9,10},{10,1... | collective-permute-start | bytes 2359304 | tf_op jit(solution)/shard_map/ppermute | solution.py:471
  115.8 37.5 %collective-permute-start.18 = (bf16[24,128,128]{2,1,0:T(8,128)(2,1)}, bf16[24,128,128]{2,1,0:T(8,128)(2,1)S(1)}, u32[]{:S(2)}, u32[]{:S(2)}) collective-permute-start(bf16[24,128,128]{2,1,0:T(8,128)(2,1)} %get-tuple-element.83), channel_id=1, source_target_pairs={{0,2},{1,3},{2,0},{3,1},{4,6},{5,7},{6,4},{7,5},{8,10},{9,11},{10,... | collective-permute-start | bytes 2359304 | tf_op jit(solution)/shard_map/ppermute | solution.py:471
  117.3 37.5 %collective-permute-start.19 = (bf16[24,128,128]{2,1,0:T(8,128)(2,1)}, bf16[24,128,128]{2,1,0:T(8,128)(2,1)}, u32[]{:S(2)}, u32[]{:S(2)}) collective-permute-start(bf16[24,128,128]{2,1,0:T(8,128)(2,1)} %get-tuple-element.84), channel_id=1, source_target_pairs={{0,3},{1,0},{2,1},{3,2},{4,7},{5,4},{6,5},{7,6},{8,11},{9,8},{10,9... | collective-permute-start | bytes 2359304 | tf_op jit(solution)/shard_map/ppermute | solution.py:471
  119.4 8.6 %collective-permute-start.10 = (bf16[3,128,128]{2,1,0:T(8,128)(2,1)S(1)}, bf16[3,128,128]{2,1,0:T(8,128)(2,1)S(1)}, u32[]{:S(2)}, u32[]{:S(2)}) collective-permute-start(bf16[3,128,128]{2,1,0:T(8,128)(2,1)S(1)} %copy-done.17), channel_id=1, source_target_pairs={{0,4},{1,5},{2,6},{3,7},{4,8},{5,9},{6,10},{7,11},{8,12},{9,13},{1... | collective-permute-start | bytes 294920 | tf_op jit(solution)/shard_map/ppermute | solution.py:440
  120.7 7.4 %collective-permute-start.11 = (bf16[3,128,128]{2,1,0:T(8,128)(2,1)S(1)}, bf16[3,128,128]{2,1,0:T(8,128)(2,1)S(1)}, u32[]{:S(2)}, u32[]{:S(2)}) collective-permute-start(bf16[3,128,128]{2,1,0:T(8,128)(2,1)S(1)} %copy-done.16), channel_id=1, source_target_pairs={{0,8},{1,9},{2,10},{3,11},{4,12},{5,13},{6,14},{7,15},{8,16},{9,17... | collective-permute-start | bytes 294920 | tf_op jit(solution)/shard_map/ppermute | solution.py:440
  128.0 35.9 %copy-start.2 = (bf16[3,128,128]{2,1,0:T(8,128)(2,1)}, bf16[3,128,128]{2,1,0:T(8,128)(2,1)S(1)}, u32[]{:S(2)}) copy-start(bf16[3,128,128]{2,1,0:T(8,128)(2,1)S(1)} %collective-permute-done.10.refs_1_) | copy-start | bytes 294916
  128.0 11.1 %collective-permute-start.12 = (bf16[3,128,128]{2,1,0:T(8,128)(2,1)S(1)}, bf16[3,128,128]{2,1,0:T(8,128)(2,1)S(1)}, u32[]{:S(2)}, u32[]{:S(2)}) collective-permute-start(bf16[3,128,128]{2,1,0:T(8,128)(2,1)S(1)} %copy-done.15), channel_id=1, source_target_pairs={{0,12},{1,13},{2,14},{3,15},{4,16},{5,17},{6,18},{7,19},{8,20},{9,... | collective-permute-start | bytes 294920 | tf_op jit(solution)/shard_map/ppermute | solution.py:440
  128.0 35.9 %copy-start.3 = (bf16[3,128,128]{2,1,0:T(8,128)(2,1)}, bf16[3,128,128]{2,1,0:T(8,128)(2,1)S(1)}, u32[]{:S(2)}) copy-start(bf16[3,128,128]{2,1,0:T(8,128)(2,1)S(1)} %collective-permute-done.11.refs_2_) | copy-start | bytes 294916
  128.1 12.6 %collective-permute-start.13 = (bf16[3,128,128]{2,1,0:T(8,128)(2,1)S(1)}, bf16[3,128,128]{2,1,0:T(8,128)(2,1)S(1)}, u32[]{:S(2)}, u32[]{:S(2)}) collective-permute-start(bf16[3,128,128]{2,1,0:T(8,128)(2,1)S(1)} %copy-done.14), channel_id=1, source_target_pairs={{0,16},{1,17},{2,18},{3,19},{4,20},{5,21},{6,22},{7,23},{8,24},{9,... | collective-permute-start | bytes 294920 | tf_op jit(solution)/shard_map/ppermute | solution.py:440
  139.1 24.8 %copy-start.4 = (bf16[3,128,128]{2,1,0:T(8,128)(2,1)}, bf16[3,128,128]{2,1,0:T(8,128)(2,1)S(1)}, u32[]{:S(2)}) copy-start(bf16[3,128,128]{2,1,0:T(8,128)(2,1)S(1)} %collective-permute-done.12.refs_3_) | copy-start | bytes 294916
  139.1 8.6 %collective-permute-start.14 = (bf16[3,128,128]{2,1,0:T(8,128)(2,1)}, bf16[3,128,128]{2,1,0:T(8,128)(2,1)S(1)}, u32[]{:S(2)}, u32[]{:S(2)}) collective-permute-start(bf16[3,128,128]{2,1,0:T(8,128)(2,1)} %get-tuple-element.68), channel_id=1, source_target_pairs={{0,20},{1,21},{2,22},{3,23},{4,24},{5,25},{6,26},{7,27},{8,28},{9,... | collective-permute-start | bytes 294920 | tf_op jit(solution)/shard_map/ppermute | solution.py:440
  140.7 23.3 %copy-start.5 = (bf16[3,128,128]{2,1,0:T(8,128)(2,1)}, bf16[3,128,128]{2,1,0:T(8,128)(2,1)S(1)}, u32[]{:S(2)}) copy-start(bf16[3,128,128]{2,1,0:T(8,128)(2,1)S(1)} %collective-permute-done.13.refs_4_) | copy-start | bytes 294916
  140.7 10.1 %collective-permute-start.15 = (bf16[3,128,128]{2,1,0:T(8,128)(2,1)}, bf16[3,128,128]{2,1,0:T(8,128)(2,1)S(1)}, u32[]{:S(2)}, u32[]{:S(2)}) collective-permute-start(bf16[3,128,128]{2,1,0:T(8,128)(2,1)} %get-tuple-element.69), channel_id=1, source_target_pairs={{0,24},{1,25},{2,26},{3,27},{4,28},{5,29},{6,30},{7,31},{8,0},{9,1... | collective-permute-start | bytes 294920 | tf_op jit(solution)/shard_map/ppermute | solution.py:440
  147.7 16.2 %copy-start.6 = (bf16[3,128,128]{2,1,0:T(8,128)(2,1)}, bf16[3,128,128]{2,1,0:T(8,128)(2,1)S(1)}, u32[]{:S(2)}) copy-start(bf16[3,128,128]{2,1,0:T(8,128)(2,1)S(1)} %collective-permute-done.14.refs_5_) | copy-start | bytes 294916
  147.7 5.5 %collective-permute-start.16 = (bf16[3,128,128]{2,1,0:T(8,128)(2,1)}, bf16[3,128,128]{2,1,0:T(8,128)(2,1)S(1)}, u32[]{:S(2)}, u32[]{:S(2)}) collective-permute-start(bf16[3,128,128]{2,1,0:T(8,128)(2,1)} %get-tuple-element.70), channel_id=1, source_target_pairs={{0,28},{1,29},{2,30},{3,31},{4,0},{5,1},{6,2},{7,3},{8,4},{9,5},{1... | collective-permute-start | bytes 294920 | tf_op jit(solution)/shard_map/ppermute | solution.py:440
  150.7 13.2 %copy-start.7 = (bf16[3,128,128]{2,1,0:T(8,128)(2,1)}, bf16[3,128,128]{2,1,0:T(8,128)(2,1)S(1)}, u32[]{:S(2)}) copy-start(bf16[3,128,128]{2,1,0:T(8,128)(2,1)S(1)} %collective-permute-done.15.refs_6_) | copy-start | bytes 294916
  153.3 0.6 copy-start.8
  153.3 1.5 copy-start
  153.9 0.9 copy-start.1
  158.8 26.3 %all-to-all-start.3 = ((bf16[8,3,128,128]{3,2,1,0:T(8,128)(2,1)}), bf16[8,3,128,128]{3,2,1,0:T(8,128)(2,1)S(1)}, u32[]{:S(2)}, u32[]{:S(2)}) async-start(bf16[8,3,128,128]{3,2,1,0:T(8,128)(2,1)} %bitcast.161), calls=%async_computation.3 | async-start | bytes 1572864 | tf_op jit(solution)/shard_map/all_to_all | solution.py:457
